TPU v7x, 256 devices: a whole 4x4x8 slice. The times are simulated.
256 devices in a mesh: depth: 8 (over z_hi, x), space: 32 (over z_lo, y, core).
Axes of the slice: x: 4, y: 4, z: 8 (z_hi: 2, z_lo: 4; z = z_hi * 4 + z_lo), core: 2. Of those that a mesh axis runs over, the one named last changes fastest.
Arguments:
- c_points: float32 [8, 64, 128, 256], P('depth', None, 'space'), may hold values from -6 to 6
- adjoint_points: float32 [8, 64, 128, 256], P('depth', None, 'space'), may hold values from -6 to 6
- conv1_weight: bfloat16 [32, 64, 576], P('depth'), may hold values from -0.25 to 0.25
- conv2_weight: bfloat16 [32, 64, 576], P('depth'), may hold values from -0.25 to 0.25
- bias1: float32 [32, 64], P('depth'), may hold values from -3 to 3
Outputs:
- new_points: float32 [8, 64, 128, 256], P('depth', None, 'space')
- new_adjoints: float32 [8, 64, 128, 256], P('depth', None, 'space')
- grad_one: float32 [32, 64, 576], P('depth')
- grad_two: float32 [32, 64, 576], P('depth')
- grad_bias: float32 [32, 64], P('depth')
All inputs are finite; a program needn't handle non-finite values.
Results may differ from a plain program's by a relative error of at most 0.006.
Values may be sent and summed in bfloat16 or wider, within the bound.
No kernel may reach another device: no remote copies, remote signals or barrier semaphores. Data moves between devices by JAX's collectives and lax.ppermute only.
A program may use at most 64 MiB of HBM per device.

v0:
```python
import math

import jax
import jax.numpy as jnp
from jax import lax
from jax.sharding import PartitionSpec as P

STEP = 0.25


def extended(block, sides, width):
    for axis, dim in sides:
        count = lax.axis_size(axis)
        forward = [(i, i + 1) for i in range(count - 1)]
        backward = [(target, source) for source, target in forward]
        low = lax.ppermute(
            lax.slice_in_dim(block, block.shape[dim] - width, None, axis=dim), axis, forward
        )
        high = lax.ppermute(lax.slice_in_dim(block, 0, width, axis=dim), axis, backward)
        block = jnp.concatenate([low, block, high], axis=dim)
    return block


def shifted(block, axis, distance):
    devices = range(lax.axis_size(axis))
    route = [(i - distance, i) for i in devices if i - distance in devices]
    return lax.ppermute(block, axis, route)


def pad_columns(field):
    return jnp.pad(field, ((0, 0), (0, 0), (1, 1)))


def tap_columns(padded, height, breadth):
    pieces = [
        padded[:, row_off : row_off + height, col_off : col_off + breadth]
        for row_off in range(3)
        for col_off in range(3)
    ]
    return jnp.stack(pieces, 0).reshape(-1, height * breadth)


def flip_taps(padded, height, breadth):
    pieces = [
        padded[:, 2 - row_off : 2 - row_off + height, 2 - col_off : 2 - col_off + breadth]
        for row_off in range(3)
        for col_off in range(3)
    ]
    return jnp.stack(pieces, 0).reshape(-1, height * breadth)


def transpose_weight(weight):
    chans = weight.shape[0]
    return weight.reshape(chans, 9, chans).transpose(2, 1, 0).reshape(chans, 9 * chans)


def outer_sum(left, right):
    return lax.dot_general(
        left, right, (((1,), (1,)), ((), ())), preferred_element_type=jnp.float32
    )


def input_rows(field):
    return pad_columns(extended(field, (("space", 1),), 1))


def hidden_rows(field):
    return pad_columns(extended(field, (("space", 1),), 1))


def state_rows(field):
    return pad_columns(extended(field, (("space", 1),), 1))


def pre_rows(field):
    return pad_columns(extended(field, (("space", 1),), 1))


def body(c_points, adjoint_points, conv1_weight, conv2_weight, bias1):
    chans = c_points.shape[1]
    height = c_points.shape[2]
    breadth = c_points.shape[3]
    layer_count = conv1_weight.shape[0]
    tiles = lax.axis_size("space")
    scale = 1.0 / math.sqrt(height * tiles * breadth)
    current = c_points[0]
    saved = []
    for depth_pos in range(layer_count):
        inputs = current.astype(jnp.bfloat16)
        padded_in = input_rows(inputs)
        pre = (
            jnp.dot(
                conv1_weight[depth_pos],
                tap_columns(padded_in, height, breadth),
                preferred_element_type=jnp.float32,
            )
            + bias1[depth_pos][:, None]
        )
        hidden = jax.nn.softplus(pre).astype(jnp.bfloat16).reshape(chans, height, breadth)
        padded_hid = hidden_rows(hidden)
        branch = jnp.dot(
            conv2_weight[depth_pos],
            tap_columns(padded_hid, height, breadth),
            preferred_element_type=jnp.float32,
        )
        current = current + STEP * branch.reshape(chans, height, breadth)
        saved.append((padded_in, padded_hid))
    arrived = shifted(current, "depth", 1)
    new_points = jnp.where(lax.axis_index("depth") == 0, c_points[0], arrived)[None]
    adjoint = adjoint_points[0]
    grads_one = []
    grads_two = []
    grads_bias = []
    for depth_pos in reversed(range(layer_count)):
        padded_in, padded_hid = saved[depth_pos]
        slope_wide = 1.0 - jnp.exp(-padded_hid[:, :, 1:-1].astype(jnp.float32))
        scaled = (STEP * adjoint).astype(jnp.bfloat16)
        hidden_adj = jnp.dot(
            transpose_weight(conv2_weight[depth_pos]),
            flip_taps(state_rows(scaled), height, breadth),
            preferred_element_type=jnp.float32,
        )
        pre_adj = (hidden_adj * slope_wide[:, 1:-1].reshape(chans, -1)).astype(jnp.bfloat16)
        back = jnp.dot(
            transpose_weight(conv1_weight[depth_pos]),
            flip_taps(pre_rows(pre_adj.reshape(chans, height, breadth)), height, breadth),
            preferred_element_type=jnp.float32,
        )
        adjoint = adjoint + back.reshape(chans, height, breadth)
        part_two = outer_sum(scaled.reshape(chans, -1), tap_columns(padded_hid, height, breadth))
        part_one = outer_sum(pre_adj, tap_columns(padded_in, height, breadth))
        part_bias = jnp.sum(pre_adj.astype(jnp.float32), axis=1)
        grads_one.append(part_one)
        grads_two.append(part_two)
        grads_bias.append(part_bias)
    stack_one = jnp.stack(grads_one[::-1], 0)
    stack_two = jnp.stack(grads_two[::-1], 0)
    stack_bias = jnp.stack(grads_bias[::-1], 0)
    stack_one, stack_two, stack_bias = lax.psum((stack_one, stack_two, stack_bias), "space")
    returned = shifted(adjoint, "depth", -1)
    new_adjoints = jnp.where(
        lax.axis_index("depth") == lax.axis_size("depth") - 1, adjoint_points[0], returned
    )[None]
    return (new_points, new_adjoints, stack_one * scale, stack_two * scale, stack_bias * scale)


def solution(mesh):
    in_specs = (
        P("depth", None, "space", None),
        P("depth", None, "space", None),
        P("depth", None, None),
        P("depth", None, None),
        P("depth", None),
    )
    out_specs = (
        P("depth", None, "space", None),
        P("depth", None, "space", None),
        P("depth", None, None),
        P("depth", None, None),
        P("depth", None),
    )
    return jax.shard_map(body, mesh=mesh, in_specs=in_specs, out_specs=out_specs, check_vma=False)
```

profile of v0, /device:TPU:1, one launch (start us, length us, event | category | flops | bytes accessed | tf_op | source)
XLA Modules:
  0.0 575.9 jit_solution(7735669884023417061)
XLA Ops:
  8.4 4.6 collective-permute-start.17
  16.1 3.6 collective-permute-start
  37.0 3.6 collective-permute-start.2
  51.7 2.9 collective-permute-start.5
  64.3 3.0 collective-permute-start.7
  88.1 6.1 %collective-permute-done.9 = bf16[64,1,256]{2,1,0:T(2,128)(2,1)S(1)} collective-permute-done((bf16[64,1,256]{2,1,0:T(2,128)(2,1)}, bf16[64,1,256]{2,1,0:T(2,128)(2,1)S(1)}, u32[]{:S(2)}, u32[]{:S(2)}) %collective-permute-start.9) | collective-permute-done | bytes 32800 | tf_op jit(solution)/shard_map/ppermute | solution.py:19
  100.9 2.9 collective-permute-start.10
  107.9 2.9 collective-permute-done.11
  123.7 3.0 collective-permute-start.13
  145.7 4.0 collective-permute-done.15
  155.9 2.9 collective-permute-start.20
  167.5 4.0 collective-permute-start.16
  178.2 6.0 %collective-permute-start.21 = (bf16[64,1,256]{2,1,0:T(2,128)(2,1)}, bf16[64,1,256]{2,1,0:T(2,128)(2,1)}, u32[]{:S(2)}, u32[]{:S(2)}) collective-permute-start(bf16[64,1,256]{2,1,0:T(2,128)(2,1)} %get-tuple-element.39), channel_id=1, source_target_pairs={{0,1},{1,2},{2,3},{3,4},{4,5},{5,6},{6,7},{7,8},{8,9},{9,10},{10,1... | collective-permute-start | bytes 98312 | tf_op jit(solution)/shard_map/ppermute | solution.py:16
  197.6 2.9 collective-permute-start.23
  203.8 3.7 collective-permute-done.24
  218.2 3.0 collective-permute-start.26
  223.2 3.2 collective-permute-done.26
  237.5 2.9 collective-permute-start.28
  244.2 3.4 collective-permute-done.28
  254.7 3.4 collective-permute-start.29
  261.1 3.9 collective-permute-done.30
  274.6 66.4 %psum.23 = f32[4,64]{1,0:T(4,128)S(1)} all-reduce(f32[4,64]{1,0:T(4,128)S(1)} %pad_maximum_fusion.38), channel_id=1, replica_groups=mesh['depth'=8,'space'=32] {'space'}, use_global_device_ids=true, to_apply=%region_6.7 | all-reduce | flops 256 | bytes 2048 | tf_op jit(solution)/shard_map/psum | solution.py:139
  347.0 5.4 collective-permute-done.33
  353.2 212.9 %all-reduce.19.cloned.1.call-done = (f32[4,64,576]{2,1,0:T(8,128)}, f32[4,64,576]{2,1,0:T(8,128)}) async-done(((f32[4,64,576]{2,1,0:T(8,128)}, f32[4,64,576]{2,1,0:T(8,128)}), (f32[4,64,576]{2,1,0:T(8,128)}, f32[4,64,576]{2,1,0:T(8,128)})) %all-reduce.19.cloned.1.call-update) | async-done | bytes 1179664 | tf_op jit(solution)/shard_map/psum | solution.py:139
  (456 shorter events, 198.7 us)
Async XLA Ops:
  7.2 558.9 %all-reduce.19.cloned.1.call-start = ((), (), s32[]{:S(2)}) async-start(), calls=%async_computation | async-start | bytes 2621440 | tf_op jit(solution)/shard_map/psum | solution.py:139
  8.4 21.6 %collective-permute-start.17 = (bf16[64,1,256]{2,1,0:T(2,128)(2,1)S(1)}, bf16[64,1,256]{2,1,0:T(2,128)(2,1)S(1)}, u32[]{:S(2)}, u32[]{:S(2)}) collective-permute-start(bf16[64,1,256]{2,1,0:T(2,128)(2,1)S(1)} %get-tuple-element.43), channel_id=1, source_target_pairs={{0,1},{1,2},{2,3},{3,4},{4,5},{5,6},{6,7},{7,8},{8,9},{9,10},{10,1... | collective-permute-start | bytes 98312 | tf_op jit(solution)/shard_map/ppermute | solution.py:16
  13.0 17.0 %collective-permute-start.18 = (bf16[64,1,256]{2,1,0:T(2,128)(2,1)S(1)}, bf16[64,1,256]{2,1,0:T(2,128)(2,1)S(1)}, u32[]{:S(2)}, u32[]{:S(2)}) collective-permute-start(bf16[64,1,256]{2,1,0:T(2,128)(2,1)S(1)} %get-tuple-element.44), channel_id=1, source_target_pairs={{1,0},{2,1},{3,2},{4,3},{5,4},{6,5},{7,6},{8,7},{9,8},{10,9},{11,1... | collective-permute-start | bytes 98312 | tf_op jit(solution)/shard_map/ppermute | solution.py:19
  16.1 16.1 %collective-permute-start = (bf16[64,1,256]{2,1,0:T(2,128)(2,1)S(1)}, bf16[64,1,256]{2,1,0:T(2,128)(2,1)S(1)}, u32[]{:S(2)}, u32[]{:S(2)}) collective-permute-start(bf16[64,1,256]{2,1,0:T(2,128)(2,1)S(1)} %get-tuple-element.59), channel_id=1, source_target_pairs={{0,1},{1,2},{2,3},{3,4},{4,5},{5,6},{6,7},{7,8},{8,9},{9,10},{10,1... | collective-permute-start | bytes 98312 | tf_op jit(solution)/shard_map/ppermute | solution.py:16
  19.7 13.5 %collective-permute-start.1 = (bf16[64,1,256]{2,1,0:T(2,128)(2,1)S(1)}, bf16[64,1,256]{2,1,0:T(2,128)(2,1)S(1)}, u32[]{:S(2)}, u32[]{:S(2)}) collective-permute-start(bf16[64,1,256]{2,1,0:T(2,128)(2,1)S(1)} %get-tuple-element.60), channel_id=1, source_target_pairs={{1,0},{2,1},{3,2},{4,3},{5,4},{6,5},{7,6},{8,7},{9,8},{10,9},{11,1... | collective-permute-start | bytes 98312 | tf_op jit(solution)/shard_map/ppermute | solution.py:19
  62.4 7.3 %collective-permute-start.6 = (bf16[64,1,256]{2,1,0:T(2,128)(2,1)}, bf16[64,1,256]{2,1,0:T(2,128)(2,1)}, u32[]{:S(2)}, u32[]{:S(2)}) collective-permute-start(bf16[64,1,256]{2,1,0:T(2,128)(2,1)} %get-tuple-element.53), channel_id=1, source_target_pairs={{0,1},{1,2},{2,3},{3,4},{4,5},{5,6},{6,7},{7,8},{8,9},{9,10},{10,1... | collective-permute-start | bytes 98312 | tf_op jit(solution)/shard_map/ppermute | solution.py:16
  80.6 7.5 %collective-permute-start.8 = (bf16[64,1,256]{2,1,0:T(2,128)(2,1)}, bf16[64,1,256]{2,1,0:T(2,128)(2,1)S(1)}, u32[]{:S(2)}, u32[]{:S(2)}) collective-permute-start(bf16[64,1,256]{2,1,0:T(2,128)(2,1)} %get-tuple-element.51), channel_id=1, source_target_pairs={{0,1},{1,2},{2,3},{3,4},{4,5},{5,6},{6,7},{7,8},{8,9},{9,10},{10,1... | collective-permute-start | bytes 98312 | tf_op jit(solution)/shard_map/ppermute | solution.py:16
  82.7 11.5 %collective-permute-start.9 = (bf16[64,1,256]{2,1,0:T(2,128)(2,1)}, bf16[64,1,256]{2,1,0:T(2,128)(2,1)S(1)}, u32[]{:S(2)}, u32[]{:S(2)}) collective-permute-start(bf16[64,1,256]{2,1,0:T(2,128)(2,1)} %get-tuple-element.52), channel_id=1, source_target_pairs={{1,0},{2,1},{3,2},{4,3},{5,4},{6,5},{7,6},{8,7},{9,8},{10,9},{11,1... | collective-permute-start | bytes 98312 | tf_op jit(solution)/shard_map/ppermute | solution.py:19
  100.9 7.0 %collective-permute-start.10 = (bf16[64,1,256]{2,1,0:T(2,128)(2,1)}, bf16[64,1,256]{2,1,0:T(2,128)(2,1)}, u32[]{:S(2)}, u32[]{:S(2)}) collective-permute-start(bf16[64,1,256]{2,1,0:T(2,128)(2,1)} %get-tuple-element.49), channel_id=1, source_target_pairs={{0,1},{1,2},{2,3},{3,4},{4,5},{5,6},{6,7},{7,8},{8,9},{9,10},{10,1... | collective-permute-start | bytes 98312 | tf_op jit(solution)/shard_map/ppermute | solution.py:16
  121.8 7.6 %collective-permute-start.12 = (bf16[64,1,256]{2,1,0:T(2,128)(2,1)}, bf16[64,1,256]{2,1,0:T(2,128)(2,1)}, u32[]{:S(2)}, u32[]{:S(2)}) collective-permute-start(bf16[64,1,256]{2,1,0:T(2,128)(2,1)} %get-tuple-element.47), channel_id=1, source_target_pairs={{0,1},{1,2},{2,3},{3,4},{4,5},{5,6},{6,7},{7,8},{8,9},{9,10},{10,1... | collective-permute-start | bytes 98312 | tf_op jit(solution)/shard_map/ppermute | solution.py:16
  123.7 8.0 %collective-permute-start.13 = (bf16[64,1,256]{2,1,0:T(2,128)(2,1)}, bf16[64,1,256]{2,1,0:T(2,128)(2,1)}, u32[]{:S(2)}, u32[]{:S(2)}) collective-permute-start(bf16[64,1,256]{2,1,0:T(2,128)(2,1)} %get-tuple-element.48), channel_id=1, source_target_pairs={{1,0},{2,1},{3,2},{4,3},{5,4},{6,5},{7,6},{8,7},{9,8},{10,9},{11,1... | collective-permute-start | bytes 98312 | tf_op jit(solution)/shard_map/ppermute | solution.py:19
  142.1 7.6 %collective-permute-start.15 = (bf16[64,1,256]{2,1,0:T(2,128)(2,1)}, bf16[64,1,256]{2,1,0:T(2,128)(2,1)S(1)}, u32[]{:S(2)}, u32[]{:S(2)}) collective-permute-start(bf16[64,1,256]{2,1,0:T(2,128)(2,1)} %get-tuple-element.46), channel_id=1, source_target_pairs={{1,0},{2,1},{3,2},{4,3},{5,4},{6,5},{7,6},{8,7},{9,8},{10,9},{11,1... | collective-permute-start | bytes 98312 | tf_op jit(solution)/shard_map/ppermute | solution.py:19
  154.0 17.5 %collective-permute-start.19 = (bf16[64,1,256]{2,1,0:T(2,128)(2,1)}, bf16[64,1,256]{2,1,0:T(2,128)(2,1)}, u32[]{:S(2)}, u32[]{:S(2)}) collective-permute-start(bf16[64,1,256]{2,1,0:T(2,128)(2,1)} %get-tuple-element.41), channel_id=1, source_target_pairs={{0,1},{1,2},{2,3},{3,4},{4,5},{5,6},{6,7},{7,8},{8,9},{9,10},{10,1... | collective-permute-start | bytes 98312 | tf_op jit(solution)/shard_map/ppermute | solution.py:16
  155.9 15.6 %collective-permute-start.20 = (bf16[64,1,256]{2,1,0:T(2,128)(2,1)}, bf16[64,1,256]{2,1,0:T(2,128)(2,1)}, u32[]{:S(2)}, u32[]{:S(2)}) collective-permute-start(bf16[64,1,256]{2,1,0:T(2,128)(2,1)} %get-tuple-element.42), channel_id=1, source_target_pairs={{1,0},{2,1},{3,2},{4,3},{5,4},{6,5},{7,6},{8,7},{9,8},{10,9},{11,1... | collective-permute-start | bytes 98312 | tf_op jit(solution)/shard_map/ppermute | solution.py:19
  167.5 178.8 %collective-permute-start.16 = (f32[64,4,256]{2,1,0:T(4,128)}, f32[64,4,256]{2,1,0:T(4,128)}, u32[]{:S(2)}, u32[]{:S(2)}) collective-permute-start(f32[64,4,256]{2,1,0:T(4,128)} %add.189), channel_id=1, source_target_pairs={{0,32},{32,64},{64,96},{96,128},{128,160},{160,192},{192,224},{1,3... | collective-permute-start | bytes 786440 | tf_op jit(solution)/shard_map/ppermute | solution.py:27
  178.2 10.8 %collective-permute-start.21 = (bf16[64,1,256]{2,1,0:T(2,128)(2,1)}, bf16[64,1,256]{2,1,0:T(2,128)(2,1)}, u32[]{:S(2)}, u32[]{:S(2)}) collective-permute-start(bf16[64,1,256]{2,1,0:T(2,128)(2,1)} %get-tuple-element.39), channel_id=1, source_target_pairs={{0,1},{1,2},{2,3},{3,4},{4,5},{5,6},{6,7},{7,8},{8,9},{9,10},{10,1... | collective-permute-start | bytes 98312 | tf_op jit(solution)/shard_map/ppermute | solution.py:16
  200.4 7.1 %collective-permute-start.24 = (bf16[64,1,256]{2,1,0:T(2,128)(2,1)}, bf16[64,1,256]{2,1,0:T(2,128)(2,1)}, u32[]{:S(2)}, u32[]{:S(2)}) collective-permute-start(bf16[64,1,256]{2,1,0:T(2,128)(2,1)} %get-tuple-element.38), channel_id=1, source_target_pairs={{1,0},{2,1},{3,2},{4,3},{5,4},{6,5},{7,6},{8,7},{9,8},{10,9},{11,1... | collective-permute-start | bytes 98312 | tf_op jit(solution)/shard_map/ppermute | solution.py:19
  216.0 7.2 %collective-permute-start.25 = (bf16[64,1,256]{2,1,0:T(2,128)(2,1)}, bf16[64,1,256]{2,1,0:T(2,128)(2,1)}, u32[]{:S(2)}, u32[]{:S(2)}) collective-permute-start(bf16[64,1,256]{2,1,0:T(2,128)(2,1)} %get-tuple-element.35), channel_id=1, source_target_pairs={{0,1},{1,2},{2,3},{3,4},{4,5},{5,6},{6,7},{7,8},{8,9},{9,10},{10,1... | collective-permute-start | bytes 98312 | tf_op jit(solution)/shard_map/ppermute | solution.py:16
  218.2 8.3 %collective-permute-start.26 = (bf16[64,1,256]{2,1,0:T(2,128)(2,1)}, bf16[64,1,256]{2,1,0:T(2,128)(2,1)}, u32[]{:S(2)}, u32[]{:S(2)}) collective-permute-start(bf16[64,1,256]{2,1,0:T(2,128)(2,1)} %get-tuple-element.36), channel_id=1, source_target_pairs={{1,0},{2,1},{3,2},{4,3},{5,4},{6,5},{7,6},{8,7},{9,8},{10,9},{11,1... | collective-permute-start | bytes 98312 | tf_op jit(solution)/shard_map/ppermute | solution.py:19
  235.5 8.7 %collective-permute-start.27 = (bf16[64,1,256]{2,1,0:T(2,128)(2,1)}, bf16[64,1,256]{2,1,0:T(2,128)(2,1)}, u32[]{:S(2)}, u32[]{:S(2)}) collective-permute-start(bf16[64,1,256]{2,1,0:T(2,128)(2,1)} %get-tuple-element.33), channel_id=1, source_target_pairs={{0,1},{1,2},{2,3},{3,4},{4,5},{5,6},{6,7},{7,8},{8,9},{9,10},{10,1... | collective-permute-start | bytes 98312 | tf_op jit(solution)/shard_map/ppermute | solution.py:16
  237.5 10.1 %collective-permute-start.28 = (bf16[64,1,256]{2,1,0:T(2,128)(2,1)}, bf16[64,1,256]{2,1,0:T(2,128)(2,1)}, u32[]{:S(2)}, u32[]{:S(2)}) collective-permute-start(bf16[64,1,256]{2,1,0:T(2,128)(2,1)} %get-tuple-element.34), channel_id=1, source_target_pairs={{1,0},{2,1},{3,2},{4,3},{5,4},{6,5},{7,6},{8,7},{9,8},{10,9},{11,1... | collective-permute-start | bytes 98312 | tf_op jit(solution)/shard_map/ppermute | solution.py:19
  269.3 71.7 %collective-permute-start.31 = (bf16[64,1,256]{2,1,0:T(2,128)(2,1)S(1)}, bf16[64,1,256]{2,1,0:T(2,128)(2,1)S(1)}, u32[]{:S(2)}, u32[]{:S(2)}) collective-permute-start(bf16[64,1,256]{2,1,0:T(2,128)(2,1)S(1)} %get-tuple-element.29), channel_id=1, source_target_pairs={{0,1},{1,2},{2,3},{3,4},{4,5},{5,6},{6,7},{7,8},{8,9},{9,10},{10,1... | collective-permute-start | bytes 98312 | tf_op jit(solution)/shard_map/ppermute | solution.py:16
  271.5 69.5 %collective-permute-start.32 = (bf16[64,1,256]{2,1,0:T(2,128)(2,1)S(1)}, bf16[64,1,256]{2,1,0:T(2,128)(2,1)S(1)}, u32[]{:S(2)}, u32[]{:S(2)}) collective-permute-start(bf16[64,1,256]{2,1,0:T(2,128)(2,1)S(1)} %get-tuple-element.30), channel_id=1, source_target_pairs={{1,0},{2,1},{3,2},{4,3},{5,4},{6,5},{7,6},{8,7},{9,8},{10,9},{11,1... | collective-permute-start | bytes 98312 | tf_op jit(solution)/shard_map/ppermute | solution.py:19
  344.4 8.1 %collective-permute-start.33 = (f32[64,4,256]{2,1,0:T(4,128)S(1)}, f32[64,4,256]{2,1,0:T(4,128)S(1)}, u32[]{:S(2)}, u32[]{:S(2)}) collective-permute-start(f32[64,4,256]{2,1,0:T(4,128)S(1)} %add.196), channel_id=1, source_target_pairs={{32,0},{64,32},{96,64},{128,96},{160,128},{192,160},{224,192},{33,... | collective-permute-start | bytes 786440 | tf_op jit(solution)/shard_map/ppermute | solution.py:27
  (69 other events, 364.0 us)
Sparse Core Ops, SparseCore 0:
  274.7 291.3 all-reduce.18
where the time goes:
time: 586 us; the launch traced here: 576 us
  waiting for transfers between devices  254 us (43%)
  starting transfers between devices  88.9 us (15%)
  local copies, waits for them, and re-layouts  66.5 us (11%)
  blocking collectives  66.4 us (11%)
  other arithmetic  56.6 us (10%)
  matrix products  27.2 us (5%)
  between operations  16.2 us (3%)
    psum x1, waiting for transfers between devices, body(): lax.psum((stack_one, stack_two, stack_bias), 'space')  213 us
    psum x1, blocking collectives, body(): lax.psum((stack_one, stack_two, stack_bias), 'space')  66.4 us
    ppermute x16, starting transfers between devices, extended(): lax.ppermute(lax.slice_in_dim(block, block.shape[dim] - width, None, axis...  45.6 us
    ppermute x16, starting transfers between devices, extended(): lax.ppermute(lax.slice_in_dim(block, 0, width, axis=dim), axis, backward)  37.9 us
    ppermute x16, waiting for transfers between devices, extended(): lax.ppermute(lax.slice_in_dim(block, 0, width, axis=dim), axis, backward)  35.7 us
    unnamed x234, local copies, waits for them, and re-layouts  32.3 us
    unnamed x40, other arithmetic  25.9 us
    concatenate x16, other arithmetic, extended(): block = jnp.concatenate([low, block, high], axis=dim)  15.3 us
  transfers between devices with their start and end apart: 35, of which 14 were waited for; matrix products, arithmetic and copies ran while one was open for 15% of the time, Pallas kernels for 0%

commit v1 on v0

v1 whole, which is shorter than its diff:
```python
import functools
import math

import jax
import jax.numpy as jnp
from jax import lax
from jax.experimental import pallas as pl
from jax.experimental.pallas import tpu as pltpu
from jax.sharding import PartitionSpec as P


STEP = 0.25
F32 = jnp.float32
BF16 = jnp.bfloat16
VMEM = pltpu.VMEM


def lanes(j, breadth, rows=1):
    return slice(j * breadth, (j + rows) * breadth)


def put_stack(dst, j, row):
    chans, breadth = row.shape
    col = lax.broadcasted_iota(jnp.int32, row.shape, 1)
    left = jnp.where(col == 0, 0.0, pltpu.roll(row, 1, axis=1))
    right = jnp.where(col == breadth - 1, 0.0, pltpu.roll(row, breadth - 1, axis=1))
    dst[0:chans, lanes(j, breadth)] = left.astype(BF16)
    dst[chans : 2 * chans, lanes(j, breadth)] = row.astype(BF16)
    dst[2 * chans : 3 * chans, lanes(j, breadth)] = right.astype(BF16)


def conv(src, first, rows, weight, chans, breadth):
    one = two = None
    for j in range(0, rows + 2, 2):
        both = jnp.dot(weight, src[:, lanes(first + j, breadth, 2)], preferred_element_type=F32)
        for half in range(2):
            z = both[:, lanes(half, breadth)]
            k = j + half - 2
            if k >= 0:
                yield k, two + z[2 * chans :]
            two = one + z[chans : 2 * chans] if one is not None else None
            one = z[:chans]


def place():
    index = lax.axis_index("space")
    return index % 2 == 0, index > 0, index < lax.axis_size("space") - 1


def halo_rows(core, chip, even, breadth, row, depth=4, base=0):
    if row < 0:
        at = lanes(base + row + depth, breadth)
        return jnp.where(even, chip[:, at], core[:, at]).astype(F32)
    at = lanes(base + row - 4, breadth)
    return jnp.where(even, core[:, at], chip[:, at]).astype(F32)


def put_edges(near, far, base, even, breadth, rows):
    for k in range(2):
        below, above = rows[k].astype(BF16), rows[k + 2].astype(BF16)
        at = lanes(base + k, breadth)
        near[:, at] = jnp.where(even, above, below)
        far[:, at] = jnp.where(even, below, above)


def gate(value, row, low, high):
    if row < 0:
        return jnp.where(low, value, 0.0)
    if row >= 4:
        return jnp.where(high, value, 0.0)
    return value


def softplus(value):
    return jnp.maximum(value, 0.0) + jnp.log1p(jnp.exp(-jnp.abs(value)))


def entry_kernel(field, flat, flat16):
    _, _, height, breadth = field.shape
    for r in range(height):
        at = lanes(r, breadth)
        value = field[0, :, r, :]
        flat[:, at] = value
        flat16[:, at] = value.astype(BF16)


def prepare_kernel(q, w1, w2, bias, q4, b3, forward, columns):
    _, _, height, breadth = q.shape
    for r in range(height):
        at = lanes(r, breadth)
        value = q[0, :, r, :]
        q4[:, at] = value
        b3[:, at] = (STEP * value).astype(BF16)
    layers, chans, _ = w1.shape
    wide = 3 * chans
    for l in range(layers):
        for which, w in enumerate((w1, w2)):
            for dy in range(3):
                forward[l, which, dy * chans : (dy + 1) * chans, :] = w[l, :, dy * wide : (dy + 1) * wide]
    rows = jnp.concatenate([bias[...], jnp.zeros((8 - layers, chans), F32)], axis=0)
    columns[...] = jnp.concatenate([rows, jnp.zeros((8, 128 - chans), F32)], axis=1).T


def turn_kernel(w1, w2, backward):
    layers, chans, _ = w1.shape
    for l in range(layers):
        for which, w in enumerate((w1, w2)):
            turned = w[l].astype(F32).T
            for e in range(3):
                blocks = [turned[(8 - 3 * e - s) * chans : (9 - 3 * e - s) * chans] for s in range(3)]
                backward[l, which, e * chans : (e + 1) * chans, :] = jnp.concatenate(blocks, axis=1).astype(BF16)


def forward_kernel(pos, state, core, chip, weights, bias, b, out, near, far, out16, xa, aa, xb, ab, xs, mid):
    chans, breadth = state.shape[0], state.shape[1] // 4
    even, low, high = place()

    def start(row):
        if 0 <= row < 4:
            return state[:, lanes(row, breadth)]
        return halo_rows(core, chip, even, breadth, row)

    for row in range(-4, 8):
        put_stack(xs, row + 4, start(row))
    xa[...] = xs[:, lanes(3, breadth, 6)]
    offset = bias[0:chans, pos : pos + 1]
    for k, value in conv(xs, 0, 10, weights[pos, 0], chans, breadth):
        put_stack(aa, k, gate(softplus(value + offset), k - 3, low, high))
    for k, value in conv(aa, 0, 8, weights[pos, 1], chans, breadth):
        row = k - 2
        value = gate(start(row) + STEP * value, row, low, high)
        put_stack(xs, k, value)
        mid[:, lanes(k, breadth)] = value
    xb[...] = xs[:, lanes(1, breadth, 6)]
    offset = bias[0:chans, pos + 1 : pos + 2]
    for k, value in conv(xs, 0, 6, weights[pos + 1, 0], chans, breadth):
        put_stack(ab, k, gate(softplus(value + offset), k - 1, low, high))
    for k, value in conv(ab, 0, 4, weights[pos + 1, 1], chans, breadth):
        value = mid[:, lanes(k + 2, breadth)] + STEP * value
        if out is None:
            out16[:, lanes(k, breadth)] = value.astype(BF16)
        else:
            out[:, lanes(k, breadth)] = value
            near[:, lanes(k, breadth)] = value.astype(BF16)
            far[:, lanes(k, breadth)] = value.astype(BF16)
    if out is not None:
        put_edges(near, far, 4, even, breadth, [b[:, lanes(k, breadth)] for k in range(4)])


def slope(stack, j, chans, breadth):
    return 1.0 - jnp.exp(-stack[chans : 2 * chans, lanes(j, breadth)].astype(F32))


def single_kernel(pos, skip, base, adjoint, core, chip, hidden, weights, final, outs, e16, bs, es):
    chans, breadth = adjoint.shape[0], adjoint.shape[1] // 4
    even, low, high = place()
    for row in range(-2, 6):
        if 0 <= row < 4:
            value = STEP * adjoint[:, lanes(row, breadth)]
            if final is not None:
                outs[2][:, lanes(row, breadth)] = value.astype(BF16)
        else:
            value = halo_rows(core, chip, even, breadth, row, 2, base)
        put_stack(bs, row + 2, value)
    for k, value in conv(bs, 0, 6, weights[pos, 1], chans, breadth):
        row = k - 1
        value = gate(value * slope(hidden, k + skip, chans, breadth), row, low, high)
        if 0 <= row < 4:
            e16[:, lanes(row, breadth)] = value.astype(BF16)
        put_stack(es, k, value)
    for k, value in conv(es, 0, 4, weights[pos, 0], chans, breadth):
        at = lanes(k, breadth)
        value = adjoint[:, at] + value
        if final is None:
            outs[0][:, at] = value
            outs[1][:, at] = (STEP * value).astype(BF16)
        else:
            value = value.astype(BF16)
            outs[0][:, at] = jnp.where(even_group(), final[:, at], value)
            outs[1][:, at] = jnp.where(even_group(), value, final[:, at])


def even_group():
    return lax.axis_index("depth") % 2 == 0


def double_kernel(pos, adjoint, core, chip, ha, hb, weights, out, near, far, ba16, ea16, bb16, eb16, bs, es, mid):
    chans, breadth = adjoint.shape[0], adjoint.shape[1] // 4
    even, low, high = place()
    for row in range(-4, 8):
        if 0 <= row < 4:
            value = STEP * adjoint[:, lanes(row, breadth)]
            ba16[:, lanes(row, breadth)] = value.astype(BF16)
        else:
            value = halo_rows(core, chip, even, breadth, row)
        put_stack(bs, row + 4, value)
    for k, value in conv(bs, 0, 10, weights[pos, 1], chans, breadth):
        row = k - 3
        value = gate(value * slope(ha, k, chans, breadth), row, low, high)
        if 0 <= row < 4:
            ea16[:, lanes(row, breadth)] = value.astype(BF16)
        put_stack(es, k, value)
    for k, value in conv(es, 0, 8, weights[pos, 0], chans, breadth):
        row = k - 2
        if 0 <= row < 4:
            value = adjoint[:, lanes(row, breadth)] + value
        else:
            value = 4.0 * halo_rows(core, chip, even, breadth, row) + value
        value = gate(value, row, low, high)
        mid[:, lanes(k, breadth)] = value
        value = STEP * value
        if 0 <= row < 4:
            bb16[:, lanes(row, breadth)] = value.astype(BF16)
        put_stack(bs, k, value)
    for k, value in conv(bs, 0, 6, weights[pos - 1, 1], chans, breadth):
        row = k - 1
        value = gate(value * slope(hb, k, chans, breadth), row, low, high)
        if 0 <= row < 4:
            eb16[:, lanes(row, breadth)] = value.astype(BF16)
        put_stack(es, k, value)
    rows = []
    for k, value in conv(es, 0, 4, weights[pos - 1, 0], chans, breadth):
        value = mid[:, lanes(k + 2, breadth)] + value
        out[:, lanes(k, breadth)] = value
        rows.append(STEP * value)
    put_edges(near, far, 0, even, breadth, rows)


def outer(left, right):
    return lax.dot_general(left, right, (((1,), (1,)), ((), ())), preferred_element_type=F32)


def grad_kernel(skip, b, hidden, e, inputs, pay, bd, ed):
    chans, breadth = b.shape[0], b.shape[1] // 4
    for src, dst in ((b, bd), (e, ed)):
        dst[...] = jnp.zeros_like(dst)
        for dy in range(3):
            dst[dy * chans : (dy + 1) * chans, lanes(dy, breadth, 4)] = src[...]
    two = outer(bd[...], hidden[:, lanes(skip, breadth, 6)])
    one = outer(ed[...], inputs[...])
    both = jnp.concatenate([two, one], axis=1)
    for c in range(8):
        for t in range(3):
            pay[c, 24 * t : 24 * t + 24, :] = both[24 * c : 24 * c + 24, 128 * t : 128 * t + 128]
        pay[c, 72:80, :] = jnp.zeros((8, 128), F32)
    ones = jnp.ones((8, e.shape[1]), BF16)
    pay[0, 72:73, 0:chans] = outer(ones, e[...])[0:1]


def packed(total):
    body = total[..., 0:72, :].astype(BF16)
    tail = total[..., 72:80, :]
    bias = tail[..., 0:1, :] + tail[..., 1:2, :]
    head = bias.astype(BF16).astype(F32)
    row = lax.broadcasted_iota(jnp.int32, tail.shape, tail.ndim - 2)
    tail = jnp.where(row == 0, head, jnp.where(row == 1, bias - head, 0.0))
    return body, tail.astype(BF16)


def where_am_i():
    index = lax.axis_index("space")
    return index % 2, (index // 2) % 4, index // 8


def split_kernel(g0, g1, g2, g3, send, keep):
    core, _, _ = where_am_i()
    for k in range(8):
        for at, low, high in ((k, g0, g2), (k + 8, g1, g3)):
            a, b = low[k], high[k]
            keep[at] = jnp.where(core == 0, a, b)
            body, tail = packed(jnp.where(core == 0, b, a))
            send[at, 0:72] = body
            send[at, 72:80] = tail


def spread_kernel(axis, keep_in, *refs):
    *parts, keep, send1, send2, send3 = refs
    mine = where_am_i()[axis]
    count = keep.shape[0]
    for k, dst in enumerate((keep, send1, send2, send3)):
        other = mine ^ k
        for n in range(count):
            at = other * count + n
            total = keep_in[at]
            for part in parts:
                total = total + part[at].astype(F32)
            if k == 0:
                dst[n] = total
            else:
                body, tail = packed(total)
                dst[n, 0:72] = body
                dst[n, 72:80] = tail


def total_kernel(keep, part1, part2, part3, out):
    total = keep[0] + part1[0].astype(F32) + part2[0].astype(F32) + part3[0].astype(F32)
    body, tail = packed(total)
    out[0, 0:72] = body
    out[0, 72:80] = tail


def join_kernel(axis, own, part1, part2, part3, out):
    mine = where_am_i()[axis]
    count = own.shape[0]
    for k, src in enumerate((own, part1, part2, part3)):
        for n in range(count):
            out[(mine ^ k) * count + n] = src[n]


def points_kernel(c, q, pair, far, points, adjoints):
    _, _, height, breadth = c.shape
    group = lax.axis_index("depth")
    first, last = group == 0, group == lax.axis_size("depth") - 1
    for r in range(height):
        at = lanes(r, breadth)
        a, b = pair[:, at].astype(F32), far[:, at].astype(F32)
        points[0, :, r, :] = jnp.where(first, c[0, :, r, :], jnp.where(even_group(), b, a))
        adjoints[0, :, r, :] = jnp.where(last, q[0, :, r, :], jnp.where(even_group(), a, b))


def exit_kernel(scale, own, part, one, two, bias):
    chans = one.shape[1]
    core, _, _ = where_am_i()
    wide = 3 * chans
    for l in range(one.shape[0]):
        base = 8 * (l % 2)

        def piece(k, rows, width=128):
            a, b = own[base + k, rows, 0:width].astype(F32), part[base + k, rows, 0:width].astype(F32)
            return jnp.where(core == l // 2, a, b)

        cols = [
            jnp.concatenate([piece(k, slice(24 * t, 24 * t + 24)) for k in range(8)], axis=0)
            for t in range(3)
        ]
        full = jnp.concatenate(cols, axis=1) * scale
        for dy in range(3):
            rows = full[dy * chans : (dy + 1) * chans]
            two[l, :, dy * wide : (dy + 1) * wide] = rows[:, :wide]
            one[l, :, dy * wide : (dy + 1) * wide] = rows[:, wide:]
        low = piece(0, slice(72, 74), chans)
        bias[l : l + 1, :] = (low[0:1] + low[1:2]) * scale


def call(kernel, outs, args, scratch=(), flops=0):
    size = sum(math.prod(a.shape) * a.dtype.itemsize for a in (*args, *outs))
    return pl.pallas_call(
        kernel,
        out_shape=outs,
        in_specs=[pl.BlockSpec(memory_space=VMEM) for _ in args],
        out_specs=[pl.BlockSpec(memory_space=VMEM) for _ in outs],
        scratch_shapes=list(scratch),
        cost_estimate=pl.CostEstimate(flops=flops, bytes_accessed=size, transcendentals=0),
        compiler_params=pltpu.CompilerParams(vmem_limit_bytes=40 << 20),
    )(*args)


def swaps(near, far):
    count = lax.axis_size("space")
    core = [(i, i ^ 1) for i in range(count)]
    chip = [(i, i + 1 if i % 2 else i - 1) for i in range(1, count - 1)]
    far = lax.ppermute(far, "space", chip)
    near = lax.ppermute(near, "space", core)
    return near, far


def partner(value, mask):
    return lax.ppermute(value, "space", [(i, i ^ mask) for i in range(lax.axis_size("space"))])


def pairs_of_groups(block, first):
    count = lax.axis_size("depth")
    pairs = [(i, i + 1) for i in range(first, count - 1, 2)]
    return lax.ppermute(block, "depth", pairs + [(b, a) for a, b in pairs])


def body(c_points, adjoint_points, conv1_weight, conv2_weight, bias1):
    _, chans, height, breadth = c_points.shape
    layers = conv1_weight.shape[0]
    tiles = lax.axis_size("space")
    scale = 1.0 / math.sqrt(height * tiles * breadth)
    pix = height * breadth
    wide = 3 * chans
    S = jax.ShapeDtypeStruct
    tile32, tile16 = S((chans, pix), F32), S((chans, pix), BF16)
    rows16 = lambda rows: S((chans, rows * breadth), BF16)
    stack = lambda rows: S((wide, rows * breadth), BF16)
    row_flops = 2 * wide * wide * breadth

    s0, s0h = call(entry_kernel, [tile32, tile16], [c_points])
    near1, far1 = swaps(s0h, s0h)
    mats = S((layers, 2, wide, wide), BF16)
    q4, b3, fw, bias = call(
        prepare_kernel, [tile32, tile16, mats, S((128, 8), F32)], [adjoint_points, conv1_weight, conv2_weight, bias1]
    )
    bw = call(turn_kernel, [mats], [conv1_weight, conv2_weight])[0]

    def forward(pos, state, core, chip, last):
        saved = [stack(6), stack(10), stack(6), stack(6)]
        if last:
            outs = [tile16, *saved]
            kernel = lambda st, co, ch, w, b, *rest: forward_kernel(pos, st, co, ch, w, b, None, None, None, None, *rest)
            args = [state, core, chip, fw, bias]
        else:
            outs = [tile32, rows16(6), rows16(6), *saved]

            def kernel(st, co, ch, w, b, edge, out, near, far, *rest):
                forward_kernel(pos, st, co, ch, w, b, edge, out, near, far, None, *rest)

            args = [state, core, chip, fw, bias, b3]
        return call(
            kernel,
            outs,
            args,
            [VMEM((wide, 12 * breadth), BF16), VMEM((chans, 8 * breadth), F32)],
            flops=36 * row_flops,
        )

    s2, near2, far2, x0, a0, x1, a1 = forward(0, s0, near1, far1, False)
    near2, far2 = swaps(near2, far2)
    f16, x2, a2, x3, a3 = forward(2, s2, near2, far2, True)

    def single(pos, skip, base, adjoint, core, chip, hidden, final):
        outs = [tile32, tile16] if final is None else [tile16] * 3
        args = [adjoint, core, chip, hidden, bw]

        def kernel(*refs):
            given, refs = refs[: len(args)], refs[len(args) :]
            held = None if final is None else given[5]
            results, rest = refs[: len(outs)], refs[len(outs) :]
            single_kernel(pos, skip, base, *given[:5], held, results, *rest)

        if final is not None:
            args.append(final)
        return call(
            kernel,
            [*outs, tile16],
            args,
            [VMEM((wide, 8 * breadth), BF16), VMEM((wide, 6 * breadth), BF16)],
            flops=14 * row_flops,
        )

    def grads(skip, b, hidden, e, inputs):
        return call(
            functools.partial(grad_kernel, skip),
            [S((8, 80, 128), F32)],
            [b, hidden, e, inputs],
            [VMEM((wide, 6 * breadth), BF16)] * 2,
            flops=12 * row_flops,
        )[0]

    q3, b2h, e3 = single(3, 0, 4, q4, near2, far2, a3, None)
    near3, far3 = swaps(b2h, b2h)
    g3 = grads(0, b3, a3, e3, x3)
    q1, near4, far4, b2, e2, b1, e1 = call(
        functools.partial(double_kernel, 2),
        [tile32, rows16(2), rows16(2), tile16, tile16, tile16, tile16],
        [q3, near3, far3, a2, a1, bw],
        [VMEM((wide, 12 * breadth), BF16), VMEM((wide, 10 * breadth), BF16), VMEM((chans, 8 * breadth), F32)],
        flops=36 * row_flops,
    )
    near4, far4, g3 = lax.optimization_barrier((near4, far4, g3))
    near4, far4 = swaps(near4, far4)
    g2 = grads(2, b2, a2, e2, x2)
    g1 = grads(0, b1, a1, e1, x1)
    pair, far, b0, e0 = single(0, 2, 0, q1, near4, far4, a0, f16)
    g0 = grads(2, b0, a0, e0, x0)

    def chunks(n, kind):
        return S((n, 80, 128), kind)

    send, keep = call(split_kernel, [chunks(16, BF16), chunks(16, F32)], [g0, g1, g2, g3])
    parts = [partner(send, 1)]
    for axis, step, count in ((1, 2, 4), (2, 8, 1)):
        keep, *sends = call(
            functools.partial(spread_kernel, axis), [chunks(count, F32)] + [chunks(count, BF16)] * 3, [keep, *parts]
        )
        parts = [partner(value, step * (k + 1)) for k, value in enumerate(sends)]
    far = pairs_of_groups(far, 1)
    pair = pairs_of_groups(pair, 0)
    mine = call(total_kernel, [chunks(1, BF16)], [keep, *parts])[0]
    parts = [partner(mine, 8 * (k + 1)) for k in range(3)]
    mine = call(functools.partial(join_kernel, 2), [chunks(4, BF16)], [mine, *parts])[0]
    mine, pair, far = lax.optimization_barrier((mine, pair, far))
    parts = [partner(mine, 2 * (k + 1)) for k in range(3)]
    points, adjoints = call(
        points_kernel, [S(c_points.shape, F32), S(c_points.shape, F32)], [c_points, adjoint_points, pair, far]
    )
    mine = call(functools.partial(join_kernel, 1), [chunks(16, BF16)], [mine, *parts])[0]
    mine, points, adjoints = lax.optimization_barrier((mine, points, adjoints))
    grad = S(conv1_weight.shape, F32)
    one, two, vec = call(
        functools.partial(exit_kernel, scale), [grad, grad, S(bias1.shape, F32)], [mine, partner(mine, 1)]
    )
    return points, adjoints, one, two, vec


def solution(mesh):
    in_specs = (
        P("depth", None, "space", None),
        P("depth", None, "space", None),
        P("depth", None, None),
        P("depth", None, None),
        P("depth", None),
    )
    out_specs = in_specs[:2] + (P("depth", None, None), P("depth", None, None), P("depth", None))

    def run(*args):
        return tuple(body(*args))

    return jax.shard_map(run, mesh=mesh, in_specs=in_specs, out_specs=out_specs, check_vma=False)
```

time: 586 us -> 93.2 us (0.16)
  the two profiles are of different devices: /device:TPU:1 before, /device:TPU:7 now
where the time goes in v1:
time: 93.2 us; the launch traced here: 92.9 us
  starting transfers between devices  54.2 us (58%)
  waiting for transfers between devices  19.5 us (21%)
  Pallas kernels  14.5 us (16%)
  local copies, waits for them, and re-layouts  3.63 us (4%)
  between operations  0.97 us (1%)
    ppermute x14, starting transfers between devices, partner(): lax.ppermute(value, 'space', [(i, i ^ mask) for i in range(lax.axis_size(...  27.7 us
    ppermute x4, starting transfers between devices, swaps(): far = lax.ppermute(far, 'space', chip)  15.5 us
    pallas_call x20, Pallas kernels, call(): pl.pallas_call(kernel, out_shape=outs, in_specs=[pl.BlockSpec(memory_spac...  14.5 us
    ppermute x14, waiting for transfers between devices, partner(): lax.ppermute(value, 'space', [(i, i ^ mask) for i in range(lax.axis_size(...  14 us
    ppermute x2, starting transfers between devices, pairs_of_groups(): return lax.ppermute(block, 'depth', pairs + [(b, a) for a, b in pairs])  10 us
    ppermute x4, waiting for transfers between devices, swaps(): far = lax.ppermute(far, 'space', chip)  5.53 us
    unnamed x16, local copies, waits for them, and re-layouts  3.63 us
  transfers between devices with their start and end apart: 24, of which 12 were waited for; matrix products, arithmetic and copies ran while one was open for 0% of the time, Pallas kernels for 5%

profile of v1, /device:TPU:7, one launch (start us, length us, event | category | flops | bytes accessed | tf_op | source)
XLA Modules:
  0.0 92.9 jit_solution(5639196599886206007)
XLA Ops:
  2.7 3.1 %collective-permute-start.1 = (bf16[64,1024]{1,0:T(8,128)(2,1)S(1)}, bf16[64,1024]{1,0:T(8,128)(2,1)S(1)}, u32[]{:S(2)}, u32[]{:S(2)}) collective-permute-start(bf16[64,1024]{1,0:T(8,128)(2,1)S(1)} %get-tuple-element.63), channel_id=1, source_target_pairs={{1,2},{2,1},{3,4},{4,3},{5,6},{6,5},{7,8},{8,7},{9,10},{10,9},{11,... | collective-permute-start | bytes 393224 | tf_op jit(solution)/shard_map/ppermute | solution.py:362
  9.3 2.1 %shard_map.94 = (f32[64,1024]{1,0:T(8,128)S(1)}, bf16[64,1536]{1,0:T(8,128)(2,1)S(1)}, bf16[64,1536]{1,0:T(8,128)(2,1)S(1)}, bf16[192,1536]{1,0:T(8,128)(2,1)S(1...) custom-call(f32[64,1024]{1,0:T(8,128)S(1)} %get-tuple-element.62.st, ...), custom_call_target="tpu_custom_call" | custom-call | flops 679477248 | bytes 4657152 | tf_op jit(solution)/shard_map/pallas_call | solution.py:347
  11.5 3.6 %collective-permute-start.3 = (bf16[64,1536]{1,0:T(8,128)(2,1)S(1)}, bf16[64,1536]{1,0:T(8,128)(2,1)S(1)}, u32[]{:S(2)}, u32[]{:S(2)}) collective-permute-start(bf16[64,1536]{1,0:T(8,128)(2,1)S(1)} %get-tuple-element.68), channel_id=1, source_target_pairs={{1,2},{2,1},{3,4},{4,3},{5,6},{6,5},{7,8},{8,7},{9,10},{10,9},{11,... | collective-permute-start | bytes 589832 | tf_op jit(solution)/shard_map/ppermute | solution.py:362
  15.7 2.8 %collective-permute-done.3.ch.refs_2_ = bf16[64,1536]{1,0:T(8,128)(2,1)S(1)} collective-permute-done((bf16[64,1536]{1,0:T(8,128)(2,1)S(1)}, bf16[64,1536]{1,0:T(8,128)(2,1)S(1)}, u32[]{:S(2)}, u32[]{:S(2)}) %collective-permute-start.3) | collective-permute-done | bytes 196640 | tf_op jit(solution)/shard_map/ppermute | solution.py:362
  18.5 2.1 %shard_map.95 = (bf16[64,1024]{1,0:T(8,128)(2,1)S(1)}, bf16[192,1536]{1,0:T(8,128)(2,1)S(1)}, bf16[192,2560]{1,0:T(8,128)(2,1)S(1)}, bf16[192,1536]{1,0:T(8,128)(2,1)S(1)}, bf16[192,1536]{1,0:T(8,128)(2,1)S(1)}) custom-call(f32[64,1024]{1,0:T(8,128)S(1)} %get-tuple-element.69.st, bf16[64,1536]{1,0:T(8,128)(2,1)S(1)} %collective-permute-done.2.co.refs_1_, ...), custom_call_target="tpu_custom_call" | custom-call | flops 679477248 | bytes 4132864 | tf_op jit(solution)/shard_map/pallas_call | solution.py:347
  21.6 3.7 %collective-permute-start.5 = (bf16[64,1024]{1,0:T(8,128)(2,1)S(1)}, bf16[64,1024]{1,0:T(8,128)(2,1)S(1)}, u32[]{:S(2)}, u32[]{:S(2)}) collective-permute-start(bf16[64,1024]{1,0:T(8,128)(2,1)S(1)} %get-tuple-element.72), channel_id=1, source_target_pairs={{1,2},{2,1},{3,4},{4,3},{5,6},{6,5},{7,8},{8,7},{9,10},{10,9},{11,... | collective-permute-start | bytes 393224 | tf_op jit(solution)/shard_map/ppermute | solution.py:362
  25.9 2.1 %collective-permute-done.5.chip = bf16[64,1024]{1,0:T(8,128)(2,1)S(1)} collective-permute-done((bf16[64,1024]{1,0:T(8,128)(2,1)S(1)}, bf16[64,1024]{1,0:T(8,128)(2,1)S(1)}, u32[]{:S(2)}, u32[]{:S(2)}) %collective-permute-start.5) | collective-permute-done | bytes 131104 | tf_op jit(solution)/shard_map/ppermute | solution.py:362
  28.0 1.9 %shard_map.98 = (f32[64,1024]{1,0:T(8,128)S(1)}, bf16[64,512]{1,0:T(8,128)(2,1)S(1)}, bf16[64,512]{1,0:T(8,128)(2,1)S(1)}, bf16[64,1024]{1,0:T(8,128)(2,1)S(1)},...) custom-call(f32[64,1024]{1,0:T(8,128)S(1)} %get-tuple-element.71.adjoint, ...), custom_call_target="tpu_custom_call" | custom-call | flops 679477248 | bytes 3604480 | tf_op jit(solution)/shard_map/pallas_call | solution.py:347
  30.0 5.1 %collective-permute-start.7 = (bf16[64,512]{1,0:T(8,128)(2,1)S(1)}, bf16[64,512]{1,0:T(8,128)(2,1)S(1)}, u32[]{:S(2)}, u32[]{:S(2)}) collective-permute-start(bf16[64,512]{1,0:T(8,128)(2,1)S(1)} %get-tuple-element.81), channel_id=1, source_target_pairs={{1,2},{2,1},{3,4},{4,3},{5,6},{6,5},{7,8},{8,7},{9,10},{10,9},{11,... | collective-permute-start | bytes 196616 | tf_op jit(solution)/shard_map/ppermute | solution.py:362
  39.2 9.4 %collective-permute-start.19 = (bf16[64,1024]{1,0:T(8,128)(2,1)S(1)}, bf16[64,1024]{1,0:T(8,128)(2,1)S(1)}, u32[]{:S(2)}, u32[]{:S(2)}) collective-permute-start(bf16[64,1024]{1,0:T(8,128)(2,1)S(1)} %get-tuple-element.105), channel_id=1, source_target_pairs={{32,64},{96,128},{160,192},{64,32},{128,96},{192,160},{33,65},{97,... | collective-permute-start | bytes 393224 | tf_op jit(solution)/shard_map/ppermute | solution.py:374
  48.7 7.3 %collective-permute-start.10 = (bf16[4,80,128]{2,1,0:T(8,128)(2,1)S(1)}, bf16[4,80,128]{2,1,0:T(8,128)(2,1)S(1)}, u32[]{:S(2)}, u32[]{:S(2)}) collective-permute-start(bf16[4,80,128]{2,1,0:T(8,128)(2,1)S(1)} %get-tuple-element.98), channel_id=1, source_target_pairs={{0,4},{1,5},{2,6},{3,7},{4,0},{5,1},{6,2},{7,3},{8,12},{9,13},{10,... | collective-permute-start | bytes 245768 | tf_op jit(solution)/shard_map/ppermute | solution.py:368
  56.0 2.4 %collective-permute-start.11 = (bf16[4,80,128]{2,1,0:T(8,128)(2,1)S(1)}, bf16[4,80,128]{2,1,0:T(8,128)(2,1)S(1)}, u32[]{:S(2)}, u32[]{:S(2)}) collective-permute-start(bf16[4,80,128]{2,1,0:T(8,128)(2,1)S(1)} %get-tuple-element.99), channel_id=1, source_target_pairs={{0,6},{1,7},{2,4},{3,5},{4,2},{5,3},{6,0},{7,1},{8,14},{9,15},{10,... | collective-permute-start | bytes 245768 | tf_op jit(solution)/shard_map/ppermute | solution.py:368
  58.9 2.1 %collective-permute-done.11.refs_2_ = bf16[4,80,128]{2,1,0:T(8,128)(2,1)S(1)} collective-permute-done((bf16[4,80,128]{2,1,0:T(8,128)(2,1)S(1)}, bf16[4,80,128]{2,1,0:T(8,128)(2,1)S(1)}, u32[]{:S(2)}, u32[]{:S(2)}) %collective-permute-start.11) | collective-permute-done | bytes 81952 | tf_op jit(solution)/shard_map/ppermute | solution.py:368
  61.0 1.5 %collective-permute-done.9.refs_0_ = bf16[4,80,128]{2,1,0:T(8,128)(2,1)S(1)} collective-permute-done((bf16[4,80,128]{2,1,0:T(8,128)(2,1)S(1)}, bf16[4,80,128]{2,1,0:T(8,128)(2,1)S(1)}, u32[]{:S(2)}, u32[]{:S(2)}) %collective-permute-start.9) | collective-permute-done | bytes 81952 | tf_op jit(solution)/shard_map/ppermute | solution.py:368
  62.5 1.5 %collective-permute-start.12 = (bf16[1,80,128]{2,1,0:T(8,128)(2,1)S(1)}, bf16[1,80,128]{2,1,0:T(8,128)(2,1)S(1)}, u32[]{:S(2)}, u32[]{:S(2)}) collective-permute-start(bf16[1,80,128]{2,1,0:T(8,128)(2,1)S(1)} %get-tuple-element.101), channel_id=1, source_target_pairs={{0,8},{1,9},{2,10},{3,11},{4,12},{5,13},{6,14},{7,15},{8,0},{9,1},... | collective-permute-start | bytes 61448 | tf_op jit(solution)/shard_map/ppermute | solution.py:368
  64.0 1.3 %collective-permute-start.13 = (bf16[1,80,128]{2,1,0:T(8,128)(2,1)S(1)}, bf16[1,80,128]{2,1,0:T(8,128)(2,1)S(1)}, u32[]{:S(2)}, u32[]{:S(2)}) collective-permute-start(bf16[1,80,128]{2,1,0:T(8,128)(2,1)S(1)} %get-tuple-element.102), channel_id=1, source_target_pairs={{0,16},{1,17},{2,18},{3,19},{4,20},{5,21},{6,22},{7,23},{8,24},{9,... | collective-permute-start | bytes 61448 | tf_op jit(solution)/shard_map/ppermute | solution.py:368
  66.2 1.4 %collective-permute-done.13.part2 = bf16[1,80,128]{2,1,0:T(8,128)(2,1)S(1)} collective-permute-done((bf16[1,80,128]{2,1,0:T(8,128)(2,1)S(1)}, bf16[1,80,128]{2,1,0:T(8,128)(2,1)S(1)}, u32[]{:S(2)}, u32[]{:S(2)}) %collective-permute-start.13) | collective-permute-done | bytes 20512 | tf_op jit(solution)/shard_map/ppermute | solution.py:368
  67.6 2.4 %collective-permute-done.14.part3 = bf16[1,80,128]{2,1,0:T(8,128)(2,1)S(1)} collective-permute-done((bf16[1,80,128]{2,1,0:T(8,128)(2,1)S(1)}, bf16[1,80,128]{2,1,0:T(8,128)(2,1)S(1)}, u32[]{:S(2)}, u32[]{:S(2)}) %collective-permute-start.14) | collective-permute-done | bytes 20512 | tf_op jit(solution)/shard_map/ppermute | solution.py:368
  71.0 2.6 %collective-permute-start.17 = (bf16[1,80,128]{2,1,0:T(8,128)(2,1)S(1)}, bf16[1,80,128]{2,1,0:T(8,128)(2,1)S(1)}, u32[]{:S(2)}, u32[]{:S(2)}) collective-permute-start(bf16[1,80,128]{2,1,0:T(8,128)(2,1)S(1)} %shard_map.107.own), channel_id=1, source_target_pairs={{0,24},{1,25},{2,26},{3,27},{4,28},{5,29},{6,30},{7,31},{8,16},{9,... | collective-permute-start | bytes 61448 | tf_op jit(solution)/shard_map/ppermute | solution.py:368
  73.7 1.9 %collective-permute-done.17.part3 = bf16[1,80,128]{2,1,0:T(8,128)(2,1)S(1)} collective-permute-done((bf16[1,80,128]{2,1,0:T(8,128)(2,1)S(1)}, bf16[1,80,128]{2,1,0:T(8,128)(2,1)S(1)}, u32[]{:S(2)}, u32[]{:S(2)}) %collective-permute-start.17) | collective-permute-done | bytes 20512 | tf_op jit(solution)/shard_map/ppermute | solution.py:368
  75.9 3.8 %collective-permute-start.21 = (bf16[4,80,128]{2,1,0:T(8,128)(2,1)S(1)}, bf16[4,80,128]{2,1,0:T(8,128)(2,1)S(1)}, u32[]{:S(2)}, u32[]{:S(2)}) collective-permute-start(bf16[4,80,128]{2,1,0:T(8,128)(2,1)S(1)} %shard_map.108.own), channel_id=1, source_target_pairs={{0,4},{1,5},{2,6},{3,7},{4,0},{5,1},{6,2},{7,3},{8,12},{9,13},{10,... | collective-permute-start | bytes 245768 | tf_op jit(solution)/shard_map/ppermute | solution.py:368
  80.8 1.6 %collective-permute-done.21.part2 = bf16[4,80,128]{2,1,0:T(8,128)(2,1)S(1)} collective-permute-done((bf16[4,80,128]{2,1,0:T(8,128)(2,1)S(1)}, bf16[4,80,128]{2,1,0:T(8,128)(2,1)S(1)}, u32[]{:S(2)}, u32[]{:S(2)}) %collective-permute-start.21) | collective-permute-done | bytes 81952 | tf_op jit(solution)/shard_map/ppermute | solution.py:368
  82.3 1.8 %collective-permute-done.22.part3 = bf16[4,80,128]{2,1,0:T(8,128)(2,1)S(1)} collective-permute-done((bf16[4,80,128]{2,1,0:T(8,128)(2,1)S(1)}, bf16[4,80,128]{2,1,0:T(8,128)(2,1)S(1)}, u32[]{:S(2)}, u32[]{:S(2)}) %collective-permute-start.22) | collective-permute-done | bytes 81952 | tf_op jit(solution)/shard_map/ppermute | solution.py:368
  84.2 6.1 %collective-permute-start.23 = (bf16[16,80,128]{2,1,0:T(8,128)(2,1)S(1)}, bf16[16,80,128]{2,1,0:T(8,128)(2,1)S(1)}, u32[]{:S(2)}, u32[]{:S(2)}) collective-permute-start(bf16[16,80,128]{2,1,0:T(8,128)(2,1)S(1)} %shard_map.109.own), channel_id=1, source_target_pairs={{0,1},{1,0},{2,3},{3,2},{4,5},{5,4},{6,7},{7,6},{8,9},{9,8},{10,11... | collective-permute-start | bytes 983048 | tf_op jit(solution)/shard_map/ppermute | solution.py:368
  (60 shorter events, 18.2 us)
Async XLA Ops:
  2.0 7.3 %collective-permute-start = (bf16[64,1024]{1,0:T(8,128)(2,1)S(1)}, bf16[64,1024]{1,0:T(8,128)(2,1)S(1)}, u32[]{:S(2)}, u32[]{:S(2)}) collective-permute-start(bf16[64,1024]{1,0:T(8,128)(2,1)S(1)} %get-tuple-element.63), channel_id=1, source_target_pairs={{0,1},{1,0},{2,3},{3,2},{4,5},{5,4},{6,7},{7,6},{8,9},{9,8},{10,11... | collective-permute-start | bytes 393224 | tf_op jit(solution)/shard_map/ppermute | solution.py:363
  2.7 6.5 %collective-permute-start.1 = (bf16[64,1024]{1,0:T(8,128)(2,1)S(1)}, bf16[64,1024]{1,0:T(8,128)(2,1)S(1)}, u32[]{:S(2)}, u32[]{:S(2)}) collective-permute-start(bf16[64,1024]{1,0:T(8,128)(2,1)S(1)} %get-tuple-element.63), channel_id=1, source_target_pairs={{1,2},{2,1},{3,4},{4,3},{5,6},{6,5},{7,8},{8,7},{9,10},{10,9},{11,... | collective-permute-start | bytes 393224 | tf_op jit(solution)/shard_map/ppermute | solution.py:362
  11.4 4.2 %collective-permute-start.2 = (bf16[64,1536]{1,0:T(8,128)(2,1)S(1)}, bf16[64,1536]{1,0:T(8,128)(2,1)S(1)}, u32[]{:S(2)}, u32[]{:S(2)}) collective-permute-start(bf16[64,1536]{1,0:T(8,128)(2,1)S(1)} %get-tuple-element.67), channel_id=1, source_target_pairs={{0,1},{1,0},{2,3},{3,2},{4,5},{5,4},{6,7},{7,6},{8,9},{9,8},{10,11... | collective-permute-start | bytes 589832 | tf_op jit(solution)/shard_map/ppermute | solution.py:363
  11.5 7.0 %collective-permute-start.3 = (bf16[64,1536]{1,0:T(8,128)(2,1)S(1)}, bf16[64,1536]{1,0:T(8,128)(2,1)S(1)}, u32[]{:S(2)}, u32[]{:S(2)}) collective-permute-start(bf16[64,1536]{1,0:T(8,128)(2,1)S(1)} %get-tuple-element.68), channel_id=1, source_target_pairs={{1,2},{2,1},{3,4},{4,3},{5,6},{6,5},{7,8},{8,7},{9,10},{10,9},{11,... | collective-permute-start | bytes 589832 | tf_op jit(solution)/shard_map/ppermute | solution.py:362
  21.5 4.3 %collective-permute-start.4 = (bf16[64,1024]{1,0:T(8,128)(2,1)S(1)}, bf16[64,1024]{1,0:T(8,128)(2,1)S(1)}, u32[]{:S(2)}, u32[]{:S(2)}) collective-permute-start(bf16[64,1024]{1,0:T(8,128)(2,1)S(1)} %get-tuple-element.72), channel_id=1, source_target_pairs={{0,1},{1,0},{2,3},{3,2},{4,5},{5,4},{6,7},{7,6},{8,9},{9,8},{10,11... | collective-permute-start | bytes 393224 | tf_op jit(solution)/shard_map/ppermute | solution.py:363
  21.6 6.3 %collective-permute-start.5 = (bf16[64,1024]{1,0:T(8,128)(2,1)S(1)}, bf16[64,1024]{1,0:T(8,128)(2,1)S(1)}, u32[]{:S(2)}, u32[]{:S(2)}) collective-permute-start(bf16[64,1024]{1,0:T(8,128)(2,1)S(1)} %get-tuple-element.72), channel_id=1, source_target_pairs={{1,2},{2,1},{3,4},{4,3},{5,6},{6,5},{7,8},{8,7},{9,10},{10,9},{11,... | collective-permute-start | bytes 393224 | tf_op jit(solution)/shard_map/ppermute | solution.py:362
  29.9 6.4 %collective-permute-start.6 = (bf16[64,512]{1,0:T(8,128)(2,1)S(1)}, bf16[64,512]{1,0:T(8,128)(2,1)S(1)}, u32[]{:S(2)}, u32[]{:S(2)}) collective-permute-start(bf16[64,512]{1,0:T(8,128)(2,1)S(1)} %get-tuple-element.80), channel_id=1, source_target_pairs={{0,1},{1,0},{2,3},{3,2},{4,5},{5,4},{6,7},{7,6},{8,9},{9,8},{10,11... | collective-permute-start | bytes 196616 | tf_op jit(solution)/shard_map/ppermute | solution.py:363
  30.0 6.9 %collective-permute-start.7 = (bf16[64,512]{1,0:T(8,128)(2,1)S(1)}, bf16[64,512]{1,0:T(8,128)(2,1)S(1)}, u32[]{:S(2)}, u32[]{:S(2)}) collective-permute-start(bf16[64,512]{1,0:T(8,128)(2,1)S(1)} %get-tuple-element.81), channel_id=1, source_target_pairs={{1,2},{2,1},{3,4},{4,3},{5,6},{6,5},{7,8},{8,7},{9,10},{10,9},{11,... | collective-permute-start | bytes 196616 | tf_op jit(solution)/shard_map/ppermute | solution.py:362
  38.5 10.1 %collective-permute-start.8 = (bf16[16,80,128]{2,1,0:T(8,128)(2,1)S(1)}, bf16[16,80,128]{2,1,0:T(8,128)(2,1)S(1)}, u32[]{:S(2)}, u32[]{:S(2)}) collective-permute-start(bf16[16,80,128]{2,1,0:T(8,128)(2,1)S(1)} %get-tuple-element.95), channel_id=1, source_target_pairs={{0,1},{1,0},{2,3},{3,2},{4,5},{5,4},{6,7},{7,6},{8,9},{9,8},{10,11... | collective-permute-start | bytes 983048 | tf_op jit(solution)/shard_map/ppermute | solution.py:368
  38.6 37.1 %collective-permute-start.18 = (bf16[64,1024]{1,0:T(8,128)(2,1)S(1)}, bf16[64,1024]{1,0:T(8,128)(2,1)S(1)}, u32[]{:S(2)}, u32[]{:S(2)}) collective-permute-start(bf16[64,1024]{1,0:T(8,128)(2,1)S(1)} %get-tuple-element.104), channel_id=1, source_target_pairs={{0,32},{64,96},{128,160},{192,224},{32,0},{96,64},{160,128},{224,1... | collective-permute-start | bytes 393224 | tf_op jit(solution)/shard_map/ppermute | solution.py:374
  39.2 36.5 %collective-permute-start.19 = (bf16[64,1024]{1,0:T(8,128)(2,1)S(1)}, bf16[64,1024]{1,0:T(8,128)(2,1)S(1)}, u32[]{:S(2)}, u32[]{:S(2)}) collective-permute-start(bf16[64,1024]{1,0:T(8,128)(2,1)S(1)} %get-tuple-element.105), channel_id=1, source_target_pairs={{32,64},{96,128},{160,192},{64,32},{128,96},{192,160},{33,65},{97,... | collective-permute-start | bytes 393224 | tf_op jit(solution)/shard_map/ppermute | solution.py:374
  48.7 10.2 %collective-permute-start.10 = (bf16[4,80,128]{2,1,0:T(8,128)(2,1)S(1)}, bf16[4,80,128]{2,1,0:T(8,128)(2,1)S(1)}, u32[]{:S(2)}, u32[]{:S(2)}) collective-permute-start(bf16[4,80,128]{2,1,0:T(8,128)(2,1)S(1)} %get-tuple-element.98), channel_id=1, source_target_pairs={{0,4},{1,5},{2,6},{3,7},{4,0},{5,1},{6,2},{7,3},{8,12},{9,13},{10,... | collective-permute-start | bytes 245768 | tf_op jit(solution)/shard_map/ppermute | solution.py:368
  56.0 4.9 %collective-permute-start.11 = (bf16[4,80,128]{2,1,0:T(8,128)(2,1)S(1)}, bf16[4,80,128]{2,1,0:T(8,128)(2,1)S(1)}, u32[]{:S(2)}, u32[]{:S(2)}) collective-permute-start(bf16[4,80,128]{2,1,0:T(8,128)(2,1)S(1)} %get-tuple-element.99), channel_id=1, source_target_pairs={{0,6},{1,7},{2,4},{3,5},{4,2},{5,3},{6,0},{7,1},{8,14},{9,15},{10,... | collective-permute-start | bytes 245768 | tf_op jit(solution)/shard_map/ppermute | solution.py:368
  58.4 4.0 %collective-permute-start.9 = (bf16[4,80,128]{2,1,0:T(8,128)(2,1)S(1)}, bf16[4,80,128]{2,1,0:T(8,128)(2,1)S(1)}, u32[]{:S(2)}, u32[]{:S(2)}) collective-permute-start(bf16[4,80,128]{2,1,0:T(8,128)(2,1)S(1)} %get-tuple-element.97), channel_id=1, source_target_pairs={{0,2},{1,3},{2,0},{3,1},{4,6},{5,7},{6,4},{7,5},{8,10},{9,11},{10,... | collective-permute-start | bytes 245768 | tf_op jit(solution)/shard_map/ppermute | solution.py:368
  62.5 3.7 %collective-permute-start.12 = (bf16[1,80,128]{2,1,0:T(8,128)(2,1)S(1)}, bf16[1,80,128]{2,1,0:T(8,128)(2,1)S(1)}, u32[]{:S(2)}, u32[]{:S(2)}) collective-permute-start(bf16[1,80,128]{2,1,0:T(8,128)(2,1)S(1)} %get-tuple-element.101), channel_id=1, source_target_pairs={{0,8},{1,9},{2,10},{3,11},{4,12},{5,13},{6,14},{7,15},{8,0},{9,1},... | collective-permute-start | bytes 61448 | tf_op jit(solution)/shard_map/ppermute | solution.py:368
  64.0 3.6 %collective-permute-start.13 = (bf16[1,80,128]{2,1,0:T(8,128)(2,1)S(1)}, bf16[1,80,128]{2,1,0:T(8,128)(2,1)S(1)}, u32[]{:S(2)}, u32[]{:S(2)}) collective-permute-start(bf16[1,80,128]{2,1,0:T(8,128)(2,1)S(1)} %get-tuple-element.102), channel_id=1, source_target_pairs={{0,16},{1,17},{2,18},{3,19},{4,20},{5,21},{6,22},{7,23},{8,24},{9,... | collective-permute-start | bytes 61448 | tf_op jit(solution)/shard_map/ppermute | solution.py:368
  65.4 4.6 %collective-permute-start.14 = (bf16[1,80,128]{2,1,0:T(8,128)(2,1)S(1)}, bf16[1,80,128]{2,1,0:T(8,128)(2,1)S(1)}, u32[]{:S(2)}, u32[]{:S(2)}) collective-permute-start(bf16[1,80,128]{2,1,0:T(8,128)(2,1)S(1)} %get-tuple-element.103), channel_id=1, source_target_pairs={{0,24},{1,25},{2,26},{3,27},{4,28},{5,29},{6,30},{7,31},{8,16},{9,... | collective-permute-start | bytes 61448 | tf_op jit(solution)/shard_map/ppermute | solution.py:368
  70.0 3.6 %collective-permute-start.15 = (bf16[1,80,128]{2,1,0:T(8,128)(2,1)S(1)}, bf16[1,80,128]{2,1,0:T(8,128)(2,1)S(1)}, u32[]{:S(2)}, u32[]{:S(2)}) collective-permute-start(bf16[1,80,128]{2,1,0:T(8,128)(2,1)S(1)} %shard_map.107.own), channel_id=1, source_target_pairs={{0,8},{1,9},{2,10},{3,11},{4,12},{5,13},{6,14},{7,15},{8,0},{9,1},... | collective-permute-start | bytes 61448 | tf_op jit(solution)/shard_map/ppermute | solution.py:368
  70.1 3.6 %collective-permute-start.16 = (bf16[1,80,128]{2,1,0:T(8,128)(2,1)S(1)}, bf16[1,80,128]{2,1,0:T(8,128)(2,1)S(1)}, u32[]{:S(2)}, u32[]{:S(2)}) collective-permute-start(bf16[1,80,128]{2,1,0:T(8,128)(2,1)S(1)} %shard_map.107.own), channel_id=1, source_target_pairs={{0,16},{1,17},{2,18},{3,19},{4,20},{5,21},{6,22},{7,23},{8,24},{9,... | collective-permute-start | bytes 61448 | tf_op jit(solution)/shard_map/ppermute | solution.py:368
  71.0 4.6 %collective-permute-start.17 = (bf16[1,80,128]{2,1,0:T(8,128)(2,1)S(1)}, bf16[1,80,128]{2,1,0:T(8,128)(2,1)S(1)}, u32[]{:S(2)}, u32[]{:S(2)}) collective-permute-start(bf16[1,80,128]{2,1,0:T(8,128)(2,1)S(1)} %shard_map.107.own), channel_id=1, source_target_pairs={{0,24},{1,25},{2,26},{3,27},{4,28},{5,29},{6,30},{7,31},{8,16},{9,... | collective-permute-start | bytes 61448 | tf_op jit(solution)/shard_map/ppermute | solution.py:368
  75.7 5.1 %collective-permute-start.20 = (bf16[4,80,128]{2,1,0:T(8,128)(2,1)S(1)}, bf16[4,80,128]{2,1,0:T(8,128)(2,1)S(1)}, u32[]{:S(2)}, u32[]{:S(2)}) collective-permute-start(bf16[4,80,128]{2,1,0:T(8,128)(2,1)S(1)} %shard_map.108.own), channel_id=1, source_target_pairs={{0,2},{1,3},{2,0},{3,1},{4,6},{5,7},{6,4},{7,5},{8,10},{9,11},{10,... | collective-permute-start | bytes 245768 | tf_op jit(solution)/shard_map/ppermute | solution.py:368
  75.9 6.5 %collective-permute-start.21 = (bf16[4,80,128]{2,1,0:T(8,128)(2,1)S(1)}, bf16[4,80,128]{2,1,0:T(8,128)(2,1)S(1)}, u32[]{:S(2)}, u32[]{:S(2)}) collective-permute-start(bf16[4,80,128]{2,1,0:T(8,128)(2,1)S(1)} %shard_map.108.own), channel_id=1, source_target_pairs={{0,4},{1,5},{2,6},{3,7},{4,0},{5,1},{6,2},{7,3},{8,12},{9,13},{10,... | collective-permute-start | bytes 245768 | tf_op jit(solution)/shard_map/ppermute | solution.py:368
  79.6 4.5 %collective-permute-start.22 = (bf16[4,80,128]{2,1,0:T(8,128)(2,1)S(1)}, bf16[4,80,128]{2,1,0:T(8,128)(2,1)S(1)}, u32[]{:S(2)}, u32[]{:S(2)}) collective-permute-start(bf16[4,80,128]{2,1,0:T(8,128)(2,1)S(1)} %shard_map.108.own), channel_id=1, source_target_pairs={{0,6},{1,7},{2,4},{3,5},{4,2},{5,3},{6,0},{7,1},{8,14},{9,15},{10,... | collective-permute-start | bytes 245768 | tf_op jit(solution)/shard_map/ppermute | solution.py:368
  84.2 7.3 %collective-permute-start.23 = (bf16[16,80,128]{2,1,0:T(8,128)(2,1)S(1)}, bf16[16,80,128]{2,1,0:T(8,128)(2,1)S(1)}, u32[]{:S(2)}, u32[]{:S(2)}) collective-permute-start(bf16[16,80,128]{2,1,0:T(8,128)(2,1)S(1)} %shard_map.109.own), channel_id=1, source_target_pairs={{0,1},{1,0},{2,3},{3,2},{4,5},{5,4},{6,7},{7,6},{8,9},{9,8},{10,11... | collective-permute-start | bytes 983048 | tf_op jit(solution)/shard_map/ppermute | solution.py:368
  (8 other events, 37.8 us)

commit v2 on v1

--- a/solution.py
+++ b/solution.py
@@ -273,17 +273,12 @@
             send[at, 72:80] = tail
 
 
-def spread_kernel(axis, keep_in, *refs):
-    *parts, keep, send1, send2, send3 = refs
-    mine = where_am_i()[axis]
-    count = keep.shape[0]
-    for k, dst in enumerate((keep, send1, send2, send3)):
-        other = mine ^ k
-        for n in range(count):
-            at = other * count + n
-            total = keep_in[at]
-            for part in parts:
-                total = total + part[at].astype(F32)
+def spread_kernel(keep_in, part, keep, *sends):
+    _, mine, _ = where_am_i()
+    for k, dst in enumerate((keep, *sends)):
+        for n in range(4):
+            at = (mine ^ k) * 4 + n
+            total = keep_in[at] + part[at].astype(F32)
             if k == 0:
                 dst[n] = total
             else:
@@ -292,11 +287,12 @@
                 dst[n, 72:80] = tail
 
 
-def total_kernel(keep, part1, part2, part3, out):
-    total = keep[0] + part1[0].astype(F32) + part2[0].astype(F32) + part3[0].astype(F32)
-    body, tail = packed(total)
-    out[0, 0:72] = body
-    out[0, 72:80] = tail
+def total_kernel(own, part1, part2, part3, out):
+    for n in range(out.shape[0]):
+        pairs = own[n].astype(F32) + part1[n].astype(F32), part2[n].astype(F32) + part3[n].astype(F32)
+        body, tail = packed(pairs[0] + pairs[1])
+        out[n, 0:72] = body
+        out[n, 72:80] = tail
 
 
 def join_kernel(axis, own, part1, part2, part3, out):
@@ -470,17 +466,13 @@
         return S((n, 80, 128), kind)
 
     send, keep = call(split_kernel, [chunks(16, BF16), chunks(16, F32)], [g0, g1, g2, g3])
-    parts = [partner(send, 1)]
-    for axis, step, count in ((1, 2, 4), (2, 8, 1)):
-        keep, *sends = call(
-            functools.partial(spread_kernel, axis), [chunks(count, F32)] + [chunks(count, BF16)] * 3, [keep, *parts]
-        )
-        parts = [partner(value, step * (k + 1)) for k, value in enumerate(sends)]
+    keep, *sends = call(spread_kernel, [chunks(4, F32)] + [chunks(4, BF16)] * 3, [keep, partner(send, 1)])
+    parts = [partner(value, 2 * (k + 1)) for k, value in enumerate(sends)]
     far = pairs_of_groups(far, 1)
     pair = pairs_of_groups(pair, 0)
-    mine = call(total_kernel, [chunks(1, BF16)], [keep, *parts])[0]
+    mine = call(total_kernel, [chunks(4, BF16)], [keep, *parts])[0]
     parts = [partner(mine, 8 * (k + 1)) for k in range(3)]
-    mine = call(functools.partial(join_kernel, 2), [chunks(4, BF16)], [mine, *parts])[0]
+    mine = call(total_kernel, [chunks(4, BF16)], [mine, *parts])[0]
     mine, pair, far = lax.optimization_barrier((mine, pair, far))
     parts = [partner(mine, 2 * (k + 1)) for k in range(3)]
     points, adjoints = call(

time: 93.2 us -> 85.5 us (0.917)
  starting transfers between devices: 54.2 us -> 45.5 us
  waiting for transfers between devices: 19.5 us -> 20.5 us
    ppermute x14 -> x11, starting transfers between devices: 27.7 us -> 19.1 us  [partner(): lax.ppermute(value, 'space', [(i, i ^ mask) for i in range(lax.axis_size(...]
    ppermute x14 -> x11, waiting for transfers between devices: 14 us -> 15 us  [partner(): lax.ppermute(value, 'space', [(i, i ^ mask) for i in range(lax.axis_size(...]
    pallas_call x20 -> x19, Pallas kernels: 14.5 us -> 14.5 us  [call(): pl.pallas_call(kernel, out_shape=outs, in_specs=[pl.BlockSpec(memory_spac...]
  transfers between devices with their start and end apart: 24 -> 21, of which waited for: 12 -> 8; matrix products, arithmetic and copies ran while one was open for 0% -> 0% of each run, Pallas kernels for 5% -> 5%
where the time goes in v2:
time: 85.5 us; the launch traced here: 85.2 us
  starting transfers between devices  45.5 us (53%)
  waiting for transfers between devices  20.5 us (24%)
  Pallas kernels  14.5 us (17%)
  local copies, waits for them, and re-layouts  3.63 us (4%)
  between operations  0.97 us (1%)
    ppermute x11, starting transfers between devices, partner(): lax.ppermute(value, 'space', [(i, i ^ mask) for i in range(lax.axis_size(...  19.1 us
    ppermute x4, starting transfers between devices, swaps(): far = lax.ppermute(far, 'space', chip)  15.5 us
    ppermute x11, waiting for transfers between devices, partner(): lax.ppermute(value, 'space', [(i, i ^ mask) for i in range(lax.axis_size(...  15 us
    pallas_call x19, Pallas kernels, call(): pl.pallas_call(kernel, out_shape=outs, in_specs=[pl.BlockSpec(memory_spac...  14.5 us
    ppermute x2, starting transfers between devices, pairs_of_groups(): return lax.ppermute(block, 'depth', pairs + [(b, a) for a, b in pairs])  9.9 us
    ppermute x4, waiting for transfers between devices, swaps(): far = lax.ppermute(far, 'space', chip)  5.53 us
    unnamed x16, local copies, waits for them, and re-layouts  3.63 us
  transfers between devices with their start and end apart: 21, of which 8 were waited for; matrix products, arithmetic and copies ran while one was open for 0% of the time, Pallas kernels for 5%

profile of v2, /device:TPU:7, one launch (start us, length us, event | category | flops | bytes accessed | tf_op | source)
XLA Modules:
  0.0 85.2 jit_solution(12654617600062852249)
XLA Ops:
  0.7 1.0 %copy-done.5 = f32[1,64,4,256]{3,2,1,0:T(4,128)S(1)} copy-done((f32[1,64,4,256]{3,2,1,0:T(4,128)S(1)}, f32[1,64,4,256]{3,2,1,0:T(4,128)}, u32[]{:S(2)}) %copy-start.5) | copy-done | bytes 262168
  2.7 3.1 %collective-permute-start.1 = (bf16[64,1024]{1,0:T(8,128)(2,1)S(1)}, bf16[64,1024]{1,0:T(8,128)(2,1)S(1)}, u32[]{:S(2)}, u32[]{:S(2)}) collective-permute-start(bf16[64,1024]{1,0:T(8,128)(2,1)S(1)} %get-tuple-element.59), channel_id=1, source_target_pairs={{1,2},{2,1},{3,4},{4,3},{5,6},{6,5},{7,8},{8,7},{9,10},{10,9},{11,... | collective-permute-start | bytes 393224 | tf_op jit(solution)/shard_map/ppermute | solution.py:358
  9.3 2.1 %shard_map.94 = (f32[64,1024]{1,0:T(8,128)S(1)}, bf16[64,1536]{1,0:T(8,128)(2,1)S(1)}, bf16[64,1536]{1,0:T(8,128)(2,1)S(1)}, bf16[192,1536]{1,0:T(8,128)(2,1)S(1...) custom-call(f32[64,1024]{1,0:T(8,128)S(1)} %get-tuple-element.58.st, ...), custom_call_target="tpu_custom_call" | custom-call | flops 679477248 | bytes 4657152 | tf_op jit(solution)/shard_map/pallas_call | solution.py:343
  11.5 3.6 %collective-permute-start.3 = (bf16[64,1536]{1,0:T(8,128)(2,1)S(1)}, bf16[64,1536]{1,0:T(8,128)(2,1)S(1)}, u32[]{:S(2)}, u32[]{:S(2)}) collective-permute-start(bf16[64,1536]{1,0:T(8,128)(2,1)S(1)} %get-tuple-element.64), channel_id=1, source_target_pairs={{1,2},{2,1},{3,4},{4,3},{5,6},{6,5},{7,8},{8,7},{9,10},{10,9},{11,... | collective-permute-start | bytes 589832 | tf_op jit(solution)/shard_map/ppermute | solution.py:358
  15.7 2.8 %collective-permute-done.3.ch.refs_2_ = bf16[64,1536]{1,0:T(8,128)(2,1)S(1)} collective-permute-done((bf16[64,1536]{1,0:T(8,128)(2,1)S(1)}, bf16[64,1536]{1,0:T(8,128)(2,1)S(1)}, u32[]{:S(2)}, u32[]{:S(2)}) %collective-permute-start.3) | collective-permute-done | bytes 196640 | tf_op jit(solution)/shard_map/ppermute | solution.py:358
  18.5 2.1 %shard_map.95 = (bf16[64,1024]{1,0:T(8,128)(2,1)S(1)}, bf16[192,1536]{1,0:T(8,128)(2,1)S(1)}, bf16[192,2560]{1,0:T(8,128)(2,1)S(1)}, bf16[192,1536]{1,0:T(8,128)(2,1)S(1)}, bf16[192,1536]{1,0:T(8,128)(2,1)S(1)}) custom-call(f32[64,1024]{1,0:T(8,128)S(1)} %get-tuple-element.65.st, bf16[64,1536]{1,0:T(8,128)(2,1)S(1)} %collective-permute-done.2.co.refs_1_, ...), custom_call_target="tpu_custom_call" | custom-call | flops 679477248 | bytes 4132864 | tf_op jit(solution)/shard_map/pallas_call | solution.py:343
  21.6 3.7 %collective-permute-start.5 = (bf16[64,1024]{1,0:T(8,128)(2,1)S(1)}, bf16[64,1024]{1,0:T(8,128)(2,1)S(1)}, u32[]{:S(2)}, u32[]{:S(2)}) collective-permute-start(bf16[64,1024]{1,0:T(8,128)(2,1)S(1)} %get-tuple-element.68), channel_id=1, source_target_pairs={{1,2},{2,1},{3,4},{4,3},{5,6},{6,5},{7,8},{8,7},{9,10},{10,9},{11,... | collective-permute-start | bytes 393224 | tf_op jit(solution)/shard_map/ppermute | solution.py:358
  25.9 2.1 %collective-permute-done.5.chip = bf16[64,1024]{1,0:T(8,128)(2,1)S(1)} collective-permute-done((bf16[64,1024]{1,0:T(8,128)(2,1)S(1)}, bf16[64,1024]{1,0:T(8,128)(2,1)S(1)}, u32[]{:S(2)}, u32[]{:S(2)}) %collective-permute-start.5) | collective-permute-done | bytes 131104 | tf_op jit(solution)/shard_map/ppermute | solution.py:358
  28.0 1.9 %shard_map.98 = (f32[64,1024]{1,0:T(8,128)S(1)}, bf16[64,512]{1,0:T(8,128)(2,1)S(1)}, bf16[64,512]{1,0:T(8,128)(2,1)S(1)}, bf16[64,1024]{1,0:T(8,128)(2,1)S(1)},...) custom-call(f32[64,1024]{1,0:T(8,128)S(1)} %get-tuple-element.67.adjoint, ...), custom_call_target="tpu_custom_call" | custom-call | flops 679477248 | bytes 3604480 | tf_op jit(solution)/shard_map/pallas_call | solution.py:343
  30.0 5.1 %collective-permute-start.7 = (bf16[64,512]{1,0:T(8,128)(2,1)S(1)}, bf16[64,512]{1,0:T(8,128)(2,1)S(1)}, u32[]{:S(2)}, u32[]{:S(2)}) collective-permute-start(bf16[64,512]{1,0:T(8,128)(2,1)S(1)} %get-tuple-element.77), channel_id=1, source_target_pairs={{1,2},{2,1},{3,4},{4,3},{5,6},{6,5},{7,8},{8,7},{9,10},{10,9},{11,... | collective-permute-start | bytes 196616 | tf_op jit(solution)/shard_map/ppermute | solution.py:358
  38.6 1.6 %collective-permute-done.8.part = bf16[16,80,128]{2,1,0:T(8,128)(2,1)S(1)} collective-permute-done((bf16[16,80,128]{2,1,0:T(8,128)(2,1)S(1)}, bf16[16,80,128]{2,1,0:T(8,128)(2,1)S(1)}, u32[]{:S(2)}, u32[]{:S(2)}) %collective-permute-start.8) | collective-permute-done | bytes 327712 | tf_op jit(solution)/shard_map/ppermute | solution.py:364
  40.3 7.4 %collective-permute-start.10 = (bf16[4,80,128]{2,1,0:T(8,128)(2,1)S(1)}, bf16[4,80,128]{2,1,0:T(8,128)(2,1)S(1)}, u32[]{:S(2)}, u32[]{:S(2)}) collective-permute-start(bf16[4,80,128]{2,1,0:T(8,128)(2,1)S(1)} %get-tuple-element.94), channel_id=1, source_target_pairs={{0,4},{1,5},{2,6},{3,7},{4,0},{5,1},{6,2},{7,3},{8,12},{9,13},{10,... | collective-permute-start | bytes 245768 | tf_op jit(solution)/shard_map/ppermute | solution.py:364
  47.6 2.4 %collective-permute-start.11 = (bf16[4,80,128]{2,1,0:T(8,128)(2,1)S(1)}, bf16[4,80,128]{2,1,0:T(8,128)(2,1)S(1)}, u32[]{:S(2)}, u32[]{:S(2)}) collective-permute-start(bf16[4,80,128]{2,1,0:T(8,128)(2,1)S(1)} %get-tuple-element.95), channel_id=1, source_target_pairs={{0,6},{1,7},{2,4},{3,5},{4,2},{5,3},{6,0},{7,1},{8,14},{9,15},{10,... | collective-permute-start | bytes 245768 | tf_op jit(solution)/shard_map/ppermute | solution.py:364
  51.0 9.4 %collective-permute-start.16 = (bf16[64,1024]{1,0:T(8,128)(2,1)S(1)}, bf16[64,1024]{1,0:T(8,128)(2,1)S(1)}, u32[]{:S(2)}, u32[]{:S(2)}) collective-permute-start(bf16[64,1024]{1,0:T(8,128)(2,1)S(1)} %get-tuple-element.97), channel_id=1, source_target_pairs={{32,64},{96,128},{160,192},{64,32},{128,96},{192,160},{33,65},{97,... | collective-permute-start | bytes 393224 | tf_op jit(solution)/shard_map/ppermute | solution.py:370
  62.1 2.1 %collective-permute-start.14 = (bf16[4,80,128]{2,1,0:T(8,128)(2,1)S(1)}, bf16[4,80,128]{2,1,0:T(8,128)(2,1)S(1)}, u32[]{:S(2)}, u32[]{:S(2)}) collective-permute-start(bf16[4,80,128]{2,1,0:T(8,128)(2,1)S(1)} %shard_map.106.own), channel_id=1, source_target_pairs={{0,24},{1,25},{2,26},{3,27},{4,28},{5,29},{6,30},{7,31},{8,16},{9,... | collective-permute-start | bytes 245768 | tf_op jit(solution)/shard_map/ppermute | solution.py:364
  64.1 8.6 %collective-permute-done.12.part1 = bf16[4,80,128]{2,1,0:T(8,128)(2,1)S(1)} collective-permute-done((bf16[4,80,128]{2,1,0:T(8,128)(2,1)S(1)}, bf16[4,80,128]{2,1,0:T(8,128)(2,1)S(1)}, u32[]{:S(2)}, u32[]{:S(2)}) %collective-permute-start.12) | collective-permute-done | bytes 81952 | tf_op jit(solution)/shard_map/ppermute | solution.py:364
  73.6 1.8 %collective-permute-start.18 = (bf16[4,80,128]{2,1,0:T(8,128)(2,1)S(1)}, bf16[4,80,128]{2,1,0:T(8,128)(2,1)S(1)}, u32[]{:S(2)}, u32[]{:S(2)}) collective-permute-start(bf16[4,80,128]{2,1,0:T(8,128)(2,1)S(1)} %shard_map.107.own), channel_id=1, source_target_pairs={{0,4},{1,5},{2,6},{3,7},{4,0},{5,1},{6,2},{7,3},{8,12},{9,13},{10,... | collective-permute-start | bytes 245768 | tf_op jit(solution)/shard_map/ppermute | solution.py:364
  75.4 1.4 %collective-permute-start.19 = (bf16[4,80,128]{2,1,0:T(8,128)(2,1)S(1)}, bf16[4,80,128]{2,1,0:T(8,128)(2,1)S(1)}, u32[]{:S(2)}, u32[]{:S(2)}) collective-permute-start(bf16[4,80,128]{2,1,0:T(8,128)(2,1)S(1)} %shard_map.107.own), channel_id=1, source_target_pairs={{0,6},{1,7},{2,4},{3,5},{4,2},{5,3},{6,0},{7,1},{8,14},{9,15},{10,... | collective-permute-start | bytes 245768 | tf_op jit(solution)/shard_map/ppermute | solution.py:364
  76.7 1.1 %shard_map.109 = (f32[1,64,4,256]{3,2,1,0:T(4,128)}, f32[1,64,4,256]{3,2,1,0:T(4,128)}) custom-call(f32[1,64,4,256]{3,2,1,0:T(4,128)S(1)} %copy-done.6, f32[1,64,4,256]{3,2,1,0:T(4,128)S(1)} %copy-done.4, bf16[64,1024]{1,0:T(8,128)(2,1)S(1)} %collective-permute-done.15.pair, bf16[64,1024]{1,0:T(8,128)(2,1)S(1)} %collective-permute-done.16.far), custom_call_target="tpu_custom_call" | custom-call | bytes 1310720 | tf_op jit(solution)/shard_map/pallas_call | solution.py:343
  77.9 1.7 %collective-permute-done.18.part2 = bf16[4,80,128]{2,1,0:T(8,128)(2,1)S(1)} collective-permute-done((bf16[4,80,128]{2,1,0:T(8,128)(2,1)S(1)}, bf16[4,80,128]{2,1,0:T(8,128)(2,1)S(1)}, u32[]{:S(2)}, u32[]{:S(2)}) %collective-permute-start.18) | collective-permute-done | bytes 81952 | tf_op jit(solution)/shard_map/ppermute | solution.py:364
  79.6 1.8 %collective-permute-done.19.part3 = bf16[4,80,128]{2,1,0:T(8,128)(2,1)S(1)} collective-permute-done((bf16[4,80,128]{2,1,0:T(8,128)(2,1)S(1)}, bf16[4,80,128]{2,1,0:T(8,128)(2,1)S(1)}, u32[]{:S(2)}, u32[]{:S(2)}) %collective-permute-start.19) | collective-permute-done | bytes 81952 | tf_op jit(solution)/shard_map/ppermute | solution.py:364
  81.4 1.2 %collective-permute-start.20 = (bf16[16,80,128]{2,1,0:T(8,128)(2,1)S(1)}, bf16[16,80,128]{2,1,0:T(8,128)(2,1)S(1)}, u32[]{:S(2)}, u32[]{:S(2)}) collective-permute-start(bf16[16,80,128]{2,1,0:T(8,128)(2,1)S(1)} %shard_map.108.own), channel_id=1, source_target_pairs={{0,1},{1,0},{2,3},{3,2},{4,5},{5,4},{6,7},{7,6},{8,9},{9,8},{10,11... | collective-permute-start | bytes 983048 | tf_op jit(solution)/shard_map/ppermute | solution.py:364
  82.6 1.3 %collective-permute-done.20.part = bf16[16,80,128]{2,1,0:T(8,128)(2,1)S(1)} collective-permute-done((bf16[16,80,128]{2,1,0:T(8,128)(2,1)S(1)}, bf16[16,80,128]{2,1,0:T(8,128)(2,1)S(1)}, u32[]{:S(2)}, u32[]{:S(2)}) %collective-permute-start.20) | collective-permute-done | bytes 327712 | tf_op jit(solution)/shard_map/ppermute | solution.py:364
  83.8 1.3 %shard_map.110 = (f32[4,64,576]{2,1,0:T(8,128)}, f32[4,64,576]{2,1,0:T(8,128)}, f32[4,64]{1,0:T(4,128)}) custom-call(bf16[16,80,128]{2,1,0:T(8,128)(2,1)S(1)} %shard_map.108.own, bf16[16,80,128]{2,1,0:T(8,128)(2,1)S(1)} %collective-permute-done.20.part), custom_call_target="tpu_custom_call" | custom-call | bytes 1836032 | tf_op jit(solution)/shard_map/pallas_call | solution.py:343
  (53 shorter events, 13.7 us)
Async XLA Ops:
  2.0 7.3 %collective-permute-start = (bf16[64,1024]{1,0:T(8,128)(2,1)S(1)}, bf16[64,1024]{1,0:T(8,128)(2,1)S(1)}, u32[]{:S(2)}, u32[]{:S(2)}) collective-permute-start(bf16[64,1024]{1,0:T(8,128)(2,1)S(1)} %get-tuple-element.59), channel_id=1, source_target_pairs={{0,1},{1,0},{2,3},{3,2},{4,5},{5,4},{6,7},{7,6},{8,9},{9,8},{10,11... | collective-permute-start | bytes 393224 | tf_op jit(solution)/shard_map/ppermute | solution.py:359
  2.7 6.5 %collective-permute-start.1 = (bf16[64,1024]{1,0:T(8,128)(2,1)S(1)}, bf16[64,1024]{1,0:T(8,128)(2,1)S(1)}, u32[]{:S(2)}, u32[]{:S(2)}) collective-permute-start(bf16[64,1024]{1,0:T(8,128)(2,1)S(1)} %get-tuple-element.59), channel_id=1, source_target_pairs={{1,2},{2,1},{3,4},{4,3},{5,6},{6,5},{7,8},{8,7},{9,10},{10,9},{11,... | collective-permute-start | bytes 393224 | tf_op jit(solution)/shard_map/ppermute | solution.py:358
  9.3 5.9 %copy-start.1 = (bf16[4,64,576]{2,1,0:T(8,128)(2,1)S(1)}, bf16[4,64,576]{2,1,0:T(8,128)(2,1)}, u32[]{:S(2)}) copy-start(bf16[4,64,576]{2,1,0:T(8,128)(2,1)} %w1.3) | copy-start | bytes 884740
  9.3 5.8 %copy-start.3 = (bf16[4,64,576]{2,1,0:T(8,128)(2,1)S(1)}, bf16[4,64,576]{2,1,0:T(8,128)(2,1)}, u32[]{:S(2)}) copy-start(bf16[4,64,576]{2,1,0:T(8,128)(2,1)} %w2.3) | copy-start | bytes 884740
  11.4 4.2 %collective-permute-start.2 = (bf16[64,1536]{1,0:T(8,128)(2,1)S(1)}, bf16[64,1536]{1,0:T(8,128)(2,1)S(1)}, u32[]{:S(2)}, u32[]{:S(2)}) collective-permute-start(bf16[64,1536]{1,0:T(8,128)(2,1)S(1)} %get-tuple-element.63), channel_id=1, source_target_pairs={{0,1},{1,0},{2,3},{3,2},{4,5},{5,4},{6,7},{7,6},{8,9},{9,8},{10,11... | collective-permute-start | bytes 589832 | tf_op jit(solution)/shard_map/ppermute | solution.py:359
  11.5 7.0 %collective-permute-start.3 = (bf16[64,1536]{1,0:T(8,128)(2,1)S(1)}, bf16[64,1536]{1,0:T(8,128)(2,1)S(1)}, u32[]{:S(2)}, u32[]{:S(2)}) collective-permute-start(bf16[64,1536]{1,0:T(8,128)(2,1)S(1)} %get-tuple-element.64), channel_id=1, source_target_pairs={{1,2},{2,1},{3,4},{4,3},{5,6},{6,5},{7,8},{8,7},{9,10},{10,9},{11,... | collective-permute-start | bytes 589832 | tf_op jit(solution)/shard_map/ppermute | solution.py:358
  21.5 4.3 %collective-permute-start.4 = (bf16[64,1024]{1,0:T(8,128)(2,1)S(1)}, bf16[64,1024]{1,0:T(8,128)(2,1)S(1)}, u32[]{:S(2)}, u32[]{:S(2)}) collective-permute-start(bf16[64,1024]{1,0:T(8,128)(2,1)S(1)} %get-tuple-element.68), channel_id=1, source_target_pairs={{0,1},{1,0},{2,3},{3,2},{4,5},{5,4},{6,7},{7,6},{8,9},{9,8},{10,11... | collective-permute-start | bytes 393224 | tf_op jit(solution)/shard_map/ppermute | solution.py:359
  21.6 6.3 %collective-permute-start.5 = (bf16[64,1024]{1,0:T(8,128)(2,1)S(1)}, bf16[64,1024]{1,0:T(8,128)(2,1)S(1)}, u32[]{:S(2)}, u32[]{:S(2)}) collective-permute-start(bf16[64,1024]{1,0:T(8,128)(2,1)S(1)} %get-tuple-element.68), channel_id=1, source_target_pairs={{1,2},{2,1},{3,4},{4,3},{5,6},{6,5},{7,8},{8,7},{9,10},{10,9},{11,... | collective-permute-start | bytes 393224 | tf_op jit(solution)/shard_map/ppermute | solution.py:358
  29.9 6.4 %collective-permute-start.6 = (bf16[64,512]{1,0:T(8,128)(2,1)S(1)}, bf16[64,512]{1,0:T(8,128)(2,1)S(1)}, u32[]{:S(2)}, u32[]{:S(2)}) collective-permute-start(bf16[64,512]{1,0:T(8,128)(2,1)S(1)} %get-tuple-element.76), channel_id=1, source_target_pairs={{0,1},{1,0},{2,3},{3,2},{4,5},{5,4},{6,7},{7,6},{8,9},{9,8},{10,11... | collective-permute-start | bytes 196616 | tf_op jit(solution)/shard_map/ppermute | solution.py:359
  30.0 6.9 %collective-permute-start.7 = (bf16[64,512]{1,0:T(8,128)(2,1)S(1)}, bf16[64,512]{1,0:T(8,128)(2,1)S(1)}, u32[]{:S(2)}, u32[]{:S(2)}) collective-permute-start(bf16[64,512]{1,0:T(8,128)(2,1)S(1)} %get-tuple-element.77), channel_id=1, source_target_pairs={{1,2},{2,1},{3,4},{4,3},{5,6},{6,5},{7,8},{8,7},{9,10},{10,9},{11,... | collective-permute-start | bytes 196616 | tf_op jit(solution)/shard_map/ppermute | solution.py:358
  38.5 1.7 %collective-permute-start.8 = (bf16[16,80,128]{2,1,0:T(8,128)(2,1)S(1)}, bf16[16,80,128]{2,1,0:T(8,128)(2,1)S(1)}, u32[]{:S(2)}, u32[]{:S(2)}) collective-permute-start(bf16[16,80,128]{2,1,0:T(8,128)(2,1)S(1)} %get-tuple-element.91), channel_id=1, source_target_pairs={{0,1},{1,0},{2,3},{3,2},{4,5},{5,4},{6,7},{7,6},{8,9},{9,8},{10,11... | collective-permute-start | bytes 983048 | tf_op jit(solution)/shard_map/ppermute | solution.py:364
  40.3 20.1 %collective-permute-start.10 = (bf16[4,80,128]{2,1,0:T(8,128)(2,1)S(1)}, bf16[4,80,128]{2,1,0:T(8,128)(2,1)S(1)}, u32[]{:S(2)}, u32[]{:S(2)}) collective-permute-start(bf16[4,80,128]{2,1,0:T(8,128)(2,1)S(1)} %get-tuple-element.94), channel_id=1, source_target_pairs={{0,4},{1,5},{2,6},{3,7},{4,0},{5,1},{6,2},{7,3},{8,12},{9,13},{10,... | collective-permute-start | bytes 245768 | tf_op jit(solution)/shard_map/ppermute | solution.py:364
  47.6 12.8 %collective-permute-start.11 = (bf16[4,80,128]{2,1,0:T(8,128)(2,1)S(1)}, bf16[4,80,128]{2,1,0:T(8,128)(2,1)S(1)}, u32[]{:S(2)}, u32[]{:S(2)}) collective-permute-start(bf16[4,80,128]{2,1,0:T(8,128)(2,1)S(1)} %get-tuple-element.95), channel_id=1, source_target_pairs={{0,6},{1,7},{2,4},{3,5},{4,2},{5,3},{6,0},{7,1},{8,14},{9,15},{10,... | collective-permute-start | bytes 245768 | tf_op jit(solution)/shard_map/ppermute | solution.py:364
  50.0 10.4 %collective-permute-start.9 = (bf16[4,80,128]{2,1,0:T(8,128)(2,1)S(1)}, bf16[4,80,128]{2,1,0:T(8,128)(2,1)S(1)}, u32[]{:S(2)}, u32[]{:S(2)}) collective-permute-start(bf16[4,80,128]{2,1,0:T(8,128)(2,1)S(1)} %get-tuple-element.93), channel_id=1, source_target_pairs={{0,2},{1,3},{2,0},{3,1},{4,6},{5,7},{6,4},{7,5},{8,10},{9,11},{10,... | collective-permute-start | bytes 245768 | tf_op jit(solution)/shard_map/ppermute | solution.py:364
  50.5 22.3 %collective-permute-start.15 = (bf16[64,1024]{1,0:T(8,128)(2,1)S(1)}, bf16[64,1024]{1,0:T(8,128)(2,1)S(1)}, u32[]{:S(2)}, u32[]{:S(2)}) collective-permute-start(bf16[64,1024]{1,0:T(8,128)(2,1)S(1)} %get-tuple-element.96), channel_id=1, source_target_pairs={{0,32},{64,96},{128,160},{192,224},{32,0},{96,64},{160,128},{224,1... | collective-permute-start | bytes 393224 | tf_op jit(solution)/shard_map/ppermute | solution.py:370
  51.0 21.8 %collective-permute-start.16 = (bf16[64,1024]{1,0:T(8,128)(2,1)S(1)}, bf16[64,1024]{1,0:T(8,128)(2,1)S(1)}, u32[]{:S(2)}, u32[]{:S(2)}) collective-permute-start(bf16[64,1024]{1,0:T(8,128)(2,1)S(1)} %get-tuple-element.97), channel_id=1, source_target_pairs={{32,64},{96,128},{160,192},{64,32},{128,96},{192,160},{33,65},{97,... | collective-permute-start | bytes 393224 | tf_op jit(solution)/shard_map/ppermute | solution.py:370
  60.5 16.3 %copy-start.6 = (f32[1,64,4,256]{3,2,1,0:T(4,128)S(1)}, f32[1,64,4,256]{3,2,1,0:T(4,128)}, u32[]{:S(2)}) copy-start(f32[1,64,4,256]{3,2,1,0:T(4,128)} %c.1) | copy-start | bytes 786436
  60.5 12.2 %collective-permute-start.12 = (bf16[4,80,128]{2,1,0:T(8,128)(2,1)S(1)}, bf16[4,80,128]{2,1,0:T(8,128)(2,1)S(1)}, u32[]{:S(2)}, u32[]{:S(2)}) collective-permute-start(bf16[4,80,128]{2,1,0:T(8,128)(2,1)S(1)} %shard_map.106.own), channel_id=1, source_target_pairs={{0,8},{1,9},{2,10},{3,11},{4,12},{5,13},{6,14},{7,15},{8,0},{9,1},... | collective-permute-start | bytes 245768 | tf_op jit(solution)/shard_map/ppermute | solution.py:364
  61.3 11.4 %collective-permute-start.13 = (bf16[4,80,128]{2,1,0:T(8,128)(2,1)S(1)}, bf16[4,80,128]{2,1,0:T(8,128)(2,1)S(1)}, u32[]{:S(2)}, u32[]{:S(2)}) collective-permute-start(bf16[4,80,128]{2,1,0:T(8,128)(2,1)S(1)} %shard_map.106.own), channel_id=1, source_target_pairs={{0,16},{1,17},{2,18},{3,19},{4,20},{5,21},{6,22},{7,23},{8,24},{9,... | collective-permute-start | bytes 245768 | tf_op jit(solution)/shard_map/ppermute | solution.py:364
  62.1 10.7 %collective-permute-start.14 = (bf16[4,80,128]{2,1,0:T(8,128)(2,1)S(1)}, bf16[4,80,128]{2,1,0:T(8,128)(2,1)S(1)}, u32[]{:S(2)}, u32[]{:S(2)}) collective-permute-start(bf16[4,80,128]{2,1,0:T(8,128)(2,1)S(1)} %shard_map.106.own), channel_id=1, source_target_pairs={{0,24},{1,25},{2,26},{3,27},{4,28},{5,29},{6,30},{7,31},{8,16},{9,... | collective-permute-start | bytes 245768 | tf_op jit(solution)/shard_map/ppermute | solution.py:364
  72.8 5.1 %collective-permute-start.17 = (bf16[4,80,128]{2,1,0:T(8,128)(2,1)S(1)}, bf16[4,80,128]{2,1,0:T(8,128)(2,1)S(1)}, u32[]{:S(2)}, u32[]{:S(2)}) collective-permute-start(bf16[4,80,128]{2,1,0:T(8,128)(2,1)S(1)} %shard_map.107.own), channel_id=1, source_target_pairs={{0,2},{1,3},{2,0},{3,1},{4,6},{5,7},{6,4},{7,5},{8,10},{9,11},{10,... | collective-permute-start | bytes 245768 | tf_op jit(solution)/shard_map/ppermute | solution.py:364
  73.6 6.0 %collective-permute-start.18 = (bf16[4,80,128]{2,1,0:T(8,128)(2,1)S(1)}, bf16[4,80,128]{2,1,0:T(8,128)(2,1)S(1)}, u32[]{:S(2)}, u32[]{:S(2)}) collective-permute-start(bf16[4,80,128]{2,1,0:T(8,128)(2,1)S(1)} %shard_map.107.own), channel_id=1, source_target_pairs={{0,4},{1,5},{2,6},{3,7},{4,0},{5,1},{6,2},{7,3},{8,12},{9,13},{10,... | collective-permute-start | bytes 245768 | tf_op jit(solution)/shard_map/ppermute | solution.py:364
  75.4 6.0 %collective-permute-start.19 = (bf16[4,80,128]{2,1,0:T(8,128)(2,1)S(1)}, bf16[4,80,128]{2,1,0:T(8,128)(2,1)S(1)}, u32[]{:S(2)}, u32[]{:S(2)}) collective-permute-start(bf16[4,80,128]{2,1,0:T(8,128)(2,1)S(1)} %shard_map.107.own), channel_id=1, source_target_pairs={{0,6},{1,7},{2,4},{3,5},{4,2},{5,3},{6,0},{7,1},{8,14},{9,15},{10,... | collective-permute-start | bytes 245768 | tf_op jit(solution)/shard_map/ppermute | solution.py:364
  81.4 2.4 %collective-permute-start.20 = (bf16[16,80,128]{2,1,0:T(8,128)(2,1)S(1)}, bf16[16,80,128]{2,1,0:T(8,128)(2,1)S(1)}, u32[]{:S(2)}, u32[]{:S(2)}) collective-permute-start(bf16[16,80,128]{2,1,0:T(8,128)(2,1)S(1)} %shard_map.108.own), channel_id=1, source_target_pairs={{0,1},{1,0},{2,3},{3,2},{4,5},{5,4},{6,7},{7,6},{8,9},{9,8},{10,11... | collective-permute-start | bytes 983048 | tf_op jit(solution)/shard_map/ppermute | solution.py:364
  (5 other events, 8.9 us)

commit v3 on v2

--- a/solution.py
+++ b/solution.py
@@ -42,32 +42,41 @@
             one = z[:chans]
 
 
-def place():
+def even_tile():
+    return lax.axis_index("space") % 2 == 0
+
+
+def halo_rows(core, chip, even, breadth, row, depth=4, base=(0, 0)):
+    at = row + depth if row < 0 else row - 4
+    near = core[:, lanes(base[0] + at, breadth)]
+    far = chip[:, lanes(base[1] + at, breadth)]
+    return (jnp.where(even, far, near) if row < 0 else jnp.where(even, near, far)).astype(F32)
+
+
+def wide_rows(own, core, chip, edge, even, breadth, row):
+    if 0 <= row < 4:
+        return own[:, lanes(row, breadth)]
+    at = row + 8 if row < 0 else row - 4
+    far = chip[:, lanes(at, breadth)]
+    if row < 0:
+        near = edge[:, lanes(at, breadth)] if at < 4 else core[:, lanes(at - 4, breadth)]
+        return jnp.where(even, far, near).astype(F32)
+    near = core[:, lanes(at, breadth)] if at < 4 else edge[:, lanes(at - 4, breadth)]
+    return jnp.where(even, near, far).astype(F32)
+
+
+def put_edge(dst, base, for_above, rows, breadth):
+    for k in range(2):
+        value = jnp.where(for_above, rows[k + 2].astype(BF16), rows[k].astype(BF16))
+        dst[:, lanes(base + k, breadth)] = value
+
+
+def gate(value, row):
     index = lax.axis_index("space")
-    return index % 2 == 0, index > 0, index < lax.axis_size("space") - 1
-
-
-def halo_rows(core, chip, even, breadth, row, depth=4, base=0):
     if row < 0:
-        at = lanes(base + row + depth, breadth)
-        return jnp.where(even, chip[:, at], core[:, at]).astype(F32)
-    at = lanes(base + row - 4, breadth)
-    return jnp.where(even, core[:, at], chip[:, at]).astype(F32)
-
-
-def put_edges(near, far, base, even, breadth, rows):
-    for k in range(2):
-        below, above = rows[k].astype(BF16), rows[k + 2].astype(BF16)
-        at = lanes(base + k, breadth)
-        near[:, at] = jnp.where(even, above, below)
-        far[:, at] = jnp.where(even, below, above)
-
-
-def gate(value, row, low, high):
-    if row < 0:
-        return jnp.where(low, value, 0.0)
+        return jnp.where(index >= (3 - row) // 4, value, 0.0)
     if row >= 4:
-        return jnp.where(high, value, 0.0)
+        return jnp.where(index + row // 4 < lax.axis_size("space"), value, 0.0)
     return value
 
 
@@ -84,13 +93,31 @@
         flat16[:, at] = value.astype(BF16)
 
 
-def prepare_kernel(q, w1, w2, bias, q4, b3, forward, columns):
+def adjoint_kernel(q, q4, b3):
     _, _, height, breadth = q.shape
     for r in range(height):
         at = lanes(r, breadth)
         value = q[0, :, r, :]
         q4[:, at] = value
         b3[:, at] = (STEP * value).astype(BF16)
+
+
+def pack_kernel(own, core, b, out):
+    even = even_tile()
+    breadth = own.shape[1] // 4
+    out[:, lanes(0, breadth, 4)] = jnp.where(even, own[...], core[...])
+    out[:, lanes(4, breadth, 4)] = jnp.where(even, core[...], own[...])
+    put_edge(out, 8, jnp.logical_not(even), [b[:, lanes(k, breadth)] for k in range(4)], breadth)
+
+
+def pass_kernel(chip, b, out):
+    even = even_tile()
+    breadth = b.shape[1] // 4
+    out[:, lanes(0, breadth, 4)] = jnp.where(even, chip[:, lanes(4, breadth, 4)], chip[:, lanes(0, breadth, 4)])
+    put_edge(out, 4, even, [b[:, lanes(k, breadth)] for k in range(4)], breadth)
+
+
+def prepare_kernel(w1, w2, bias, forward, columns):
     layers, chans, _ = w1.shape
     wide = 3 * chans
     for l in range(layers):
@@ -111,40 +138,32 @@
                 backward[l, which, e * chans : (e + 1) * chans, :] = jnp.concatenate(blocks, axis=1).astype(BF16)
 
 
-def forward_kernel(pos, state, core, chip, weights, bias, b, out, near, far, out16, xa, aa, xb, ab, xs, mid):
+def forward_kernel(state, core, chip, edge, weights, bias, out, *refs):
+    inputs, hidden, (xs, wide_a, mid) = refs[0:4], refs[4:8], refs[8:]
     chans, breadth = state.shape[0], state.shape[1] // 4
-    even, low, high = place()
-
-    def start(row):
-        if 0 <= row < 4:
-            return state[:, lanes(row, breadth)]
-        return halo_rows(core, chip, even, breadth, row)
-
-    for row in range(-4, 8):
-        put_stack(xs, row + 4, start(row))
-    xa[...] = xs[:, lanes(3, breadth, 6)]
-    offset = bias[0:chans, pos : pos + 1]
-    for k, value in conv(xs, 0, 10, weights[pos, 0], chans, breadth):
-        put_stack(aa, k, gate(softplus(value + offset), k - 3, low, high))
-    for k, value in conv(aa, 0, 8, weights[pos, 1], chans, breadth):
-        row = k - 2
-        value = gate(start(row) + STEP * value, row, low, high)
-        put_stack(xs, k, value)
-        mid[:, lanes(k, breadth)] = value
-    xb[...] = xs[:, lanes(1, breadth, 6)]
-    offset = bias[0:chans, pos + 1 : pos + 2]
-    for k, value in conv(xs, 0, 6, weights[pos + 1, 0], chans, breadth):
-        put_stack(ab, k, gate(softplus(value + offset), k - 1, low, high))
-    for k, value in conv(ab, 0, 4, weights[pos + 1, 1], chans, breadth):
-        value = mid[:, lanes(k + 2, breadth)] + STEP * value
-        if out is None:
-            out16[:, lanes(k, breadth)] = value.astype(BF16)
-        else:
-            out[:, lanes(k, breadth)] = value
-            near[:, lanes(k, breadth)] = value.astype(BF16)
-            far[:, lanes(k, breadth)] = value.astype(BF16)
-    if out is not None:
-        put_edges(near, far, 4, even, breadth, [b[:, lanes(k, breadth)] for k in range(4)])
+    even = even_tile()
+    start = functools.partial(wide_rows, state, core, chip, edge, even, breadth)
+    for row in range(-8, 12):
+        put_stack(xs, row + 8, start(row))
+    for pos in range(4):
+        reach = 8 - 2 * pos
+        inputs[pos][...] = xs[:, lanes(reach - 1, breadth, 6)]
+        offset = bias[0:chans, pos : pos + 1]
+        dst = wide_a if pos < 2 else hidden[pos]
+        for k, value in conv(xs, 0, 2 + 2 * reach, weights[pos, 0], chans, breadth):
+            put_stack(dst, k, gate(softplus(value + offset), k + 1 - reach))
+        if pos < 2:
+            hidden[pos][...] = dst[:, lanes(reach - 2, breadth, 6)]
+        for k, value in conv(dst, 0, 2 * reach, weights[pos, 1], chans, breadth):
+            row = k + 2 - reach
+            at = lanes(row + 6, breadth)
+            value = (mid[:, at] if pos else start(row)) + STEP * value
+            if pos == 3:
+                out[:, lanes(row, breadth)] = value.astype(BF16)
+            else:
+                value = gate(value, row)
+                put_stack(xs, k, value)
+                mid[:, at] = value
 
 
 def slope(stack, j, chans, breadth):
@@ -153,7 +172,7 @@
 
 def single_kernel(pos, skip, base, adjoint, core, chip, hidden, weights, final, outs, e16, bs, es):
     chans, breadth = adjoint.shape[0], adjoint.shape[1] // 4
-    even, low, high = place()
+    even = even_tile()
     for row in range(-2, 6):
         if 0 <= row < 4:
             value = STEP * adjoint[:, lanes(row, breadth)]
@@ -164,7 +183,7 @@
         put_stack(bs, row + 2, value)
     for k, value in conv(bs, 0, 6, weights[pos, 1], chans, breadth):
         row = k - 1
-        value = gate(value * slope(hidden, k + skip, chans, breadth), row, low, high)
+        value = gate(value * slope(hidden, k + skip, chans, breadth), row)
         if 0 <= row < 4:
             e16[:, lanes(row, breadth)] = value.astype(BF16)
         put_stack(es, k, value)
@@ -186,7 +205,7 @@
 
 def double_kernel(pos, adjoint, core, chip, ha, hb, weights, out, near, far, ba16, ea16, bb16, eb16, bs, es, mid):
     chans, breadth = adjoint.shape[0], adjoint.shape[1] // 4
-    even, low, high = place()
+    even = even_tile()
     for row in range(-4, 8):
         if 0 <= row < 4:
             value = STEP * adjoint[:, lanes(row, breadth)]
@@ -196,7 +215,7 @@
         put_stack(bs, row + 4, value)
     for k, value in conv(bs, 0, 10, weights[pos, 1], chans, breadth):
         row = k - 3
-        value = gate(value * slope(ha, k, chans, breadth), row, low, high)
+        value = gate(value * slope(ha, k, chans, breadth), row)
         if 0 <= row < 4:
             ea16[:, lanes(row, breadth)] = value.astype(BF16)
         put_stack(es, k, value)
@@ -206,7 +225,7 @@
             value = adjoint[:, lanes(row, breadth)] + value
         else:
             value = 4.0 * halo_rows(core, chip, even, breadth, row) + value
-        value = gate(value, row, low, high)
+        value = gate(value, row)
         mid[:, lanes(k, breadth)] = value
         value = STEP * value
         if 0 <= row < 4:
@@ -214,7 +233,7 @@
         put_stack(bs, k, value)
     for k, value in conv(bs, 0, 6, weights[pos - 1, 1], chans, breadth):
         row = k - 1
-        value = gate(value * slope(hb, k, chans, breadth), row, low, high)
+        value = gate(value * slope(hb, k, chans, breadth), row)
         if 0 <= row < 4:
             eb16[:, lanes(row, breadth)] = value.astype(BF16)
         put_stack(es, k, value)
@@ -223,7 +242,8 @@
         value = mid[:, lanes(k + 2, breadth)] + value
         out[:, lanes(k, breadth)] = value
         rows.append(STEP * value)
-    put_edges(near, far, 0, even, breadth, rows)
+    put_edge(near, 0, even, rows, breadth)
+    put_edge(far, 0, jnp.logical_not(even), rows, breadth)
 
 
 def outer(left, right):
@@ -351,13 +371,18 @@
     )(*args)
 
 
+def swap_cores(value):
+    return lax.ppermute(value, "space", [(i, i ^ 1) for i in range(lax.axis_size("space"))])
+
+
+def swap_chips(value):
+    count = lax.axis_size("space")
+    return lax.ppermute(value, "space", [(i, i + 1 if i % 2 else i - 1) for i in range(1, count - 1)])
+
+
 def swaps(near, far):
-    count = lax.axis_size("space")
-    core = [(i, i ^ 1) for i in range(count)]
-    chip = [(i, i + 1 if i % 2 else i - 1) for i in range(1, count - 1)]
-    far = lax.ppermute(far, "space", chip)
-    near = lax.ppermute(near, "space", core)
-    return near, far
+    far = swap_chips(far)
+    return swap_cores(near), far
 
 
 def partner(value, mask):
@@ -384,37 +409,21 @@
     row_flops = 2 * wide * wide * breadth
 
     s0, s0h = call(entry_kernel, [tile32, tile16], [c_points])
-    near1, far1 = swaps(s0h, s0h)
+    near1 = swap_cores(s0h)
+    q4, b3 = call(adjoint_kernel, [tile32, tile16], [adjoint_points])
+    far1 = swap_chips(call(pack_kernel, [rows16(10)], [s0h, near1, b3])[0])
     mats = S((layers, 2, wide, wide), BF16)
-    q4, b3, fw, bias = call(
-        prepare_kernel, [tile32, tile16, mats, S((128, 8), F32)], [adjoint_points, conv1_weight, conv2_weight, bias1]
+    fw, bias = call(prepare_kernel, [mats, S((128, 8), F32)], [conv1_weight, conv2_weight, bias1])
+    bw = call(turn_kernel, [mats], [conv1_weight, conv2_weight])[0]
+    far1, fw, bias, bw = lax.optimization_barrier((far1, fw, bias, bw))
+    near2 = swap_cores(call(pass_kernel, [rows16(6)], [far1, b3])[0])
+    f16, x0, x1, x2, x3, a0, a1, a2, a3 = call(
+        forward_kernel,
+        [tile16, *[stack(6)] * 4, stack(6), stack(6), stack(10), stack(6)],
+        [s0, near1, far1, near2, fw, bias],
+        [VMEM((wide, 20 * breadth), BF16), VMEM((wide, 18 * breadth), BF16), VMEM((chans, 16 * breadth), F32)],
+        flops=104 * row_flops,
     )
-    bw = call(turn_kernel, [mats], [conv1_weight, conv2_weight])[0]
-
-    def forward(pos, state, core, chip, last):
-        saved = [stack(6), stack(10), stack(6), stack(6)]
-        if last:
-            outs = [tile16, *saved]
-            kernel = lambda st, co, ch, w, b, *rest: forward_kernel(pos, st, co, ch, w, b, None, None, None, None, *rest)
-            args = [state, core, chip, fw, bias]
-        else:
-            outs = [tile32, rows16(6), rows16(6), *saved]
-
-            def kernel(st, co, ch, w, b, edge, out, near, far, *rest):
-                forward_kernel(pos, st, co, ch, w, b, edge, out, near, far, None, *rest)
-
-            args = [state, core, chip, fw, bias, b3]
-        return call(
-            kernel,
-            outs,
-            args,
-            [VMEM((wide, 12 * breadth), BF16), VMEM((chans, 8 * breadth), F32)],
-            flops=36 * row_flops,
-        )
-
-    s2, near2, far2, x0, a0, x1, a1 = forward(0, s0, near1, far1, False)
-    near2, far2 = swaps(near2, far2)
-    f16, x2, a2, x3, a3 = forward(2, s2, near2, far2, True)
 
     def single(pos, skip, base, adjoint, core, chip, hidden, final):
         outs = [tile32, tile16] if final is None else [tile16] * 3
@@ -445,7 +454,7 @@
             flops=12 * row_flops,
         )[0]
 
-    q3, b2h, e3 = single(3, 0, 4, q4, near2, far2, a3, None)
+    q3, b2h, e3 = single(3, 0, (4, 8), q4, near2, far1, a3, None)
     near3, far3 = swaps(b2h, b2h)
     g3 = grads(0, b3, a3, e3, x3)
     q1, near4, far4, b2, e2, b1, e1 = call(
@@ -459,8 +468,8 @@
     near4, far4 = swaps(near4, far4)
     g2 = grads(2, b2, a2, e2, x2)
     g1 = grads(0, b1, a1, e1, x1)
-    pair, far, b0, e0 = single(0, 2, 0, q1, near4, far4, a0, f16)
-    g0 = grads(2, b0, a0, e0, x0)
+    pair, far, b0, e0 = single(0, 0, (0, 0), q1, near4, far4, a0, f16)
+    g0 = grads(0, b0, a0, e0, x0)
 
     def chunks(n, kind):
         return S((n, 80, 128), kind)

time: 85.5 us -> 81.5 us (0.953)
  starting transfers between devices: 45.5 us -> 41.6 us
  local copies, waits for them, and re-layouts: 3.63 us -> 0.97 us
  waiting for transfers between devices: 20.5 us -> 22.2 us
  Pallas kernels: 14.5 us -> 15.5 us
    ppermute x8 -> x7, starting transfers between devices: 16.5 us -> 11.8 us  [the longest x3 10.8 us: swap_chips(): lax.ppermute(value, 'space', [(i, i + 1 if i % 2 else i - 1) for i in ran...]
    ppermute x8 -> x7, waiting for transfers between devices: 5.55 us -> 9 us  [the longest x3 7.05 us: swap_chips(): lax.ppermute(value, 'space', [(i, i + 1 if i % 2 else i - 1) for i in ran...]
    unnamed x16 -> x12, local copies, waits for them, and re-layouts: 3.63 us -> 0.97 us
    ppermute x11, waiting for transfers between devices: 15 us -> 13.2 us  [partner(): lax.ppermute(value, 'space', [(i, i ^ mask) for i in range(lax.axis_size(...]
    pallas_call x19 -> x21, Pallas kernels: 14.5 us -> 15.5 us  [call(): pl.pallas_call(kernel, out_shape=outs, in_specs=[pl.BlockSpec(memory_spac...]
  transfers between devices with their start and end apart: 21 -> 20, of which waited for: 8 -> 11; matrix products, arithmetic and copies ran while one was open for 0% -> 0% of each run, Pallas kernels for 5% -> 5%
where the time goes in v3:
time: 81.5 us; the launch traced here: 81.2 us
  starting transfers between devices  41.6 us (51%)
  waiting for transfers between devices  22.2 us (27%)
  Pallas kernels  15.5 us (19%)
  local copies, waits for them, and re-layouts  0.97 us (1%)
  between operations  0.91 us (1%)
    ppermute x11, starting transfers between devices, partner(): lax.ppermute(value, 'space', [(i, i ^ mask) for i in range(lax.axis_size(...  19.8 us
    pallas_call x21, Pallas kernels, call(): pl.pallas_call(kernel, out_shape=outs, in_specs=[pl.BlockSpec(memory_spac...  15.5 us
    ppermute x11, waiting for transfers between devices, partner(): lax.ppermute(value, 'space', [(i, i ^ mask) for i in range(lax.axis_size(...  13.2 us
    ppermute x3, starting transfers between devices, swap_chips(): lax.ppermute(value, 'space', [(i, i + 1 if i % 2 else i - 1) for i in ran...  10.8 us
    ppermute x2, starting transfers between devices, pairs_of_groups(): return lax.ppermute(block, 'depth', pairs + [(b, a) for a, b in pairs])  9.94 us
    ppermute x3, waiting for transfers between devices, swap_chips(): lax.ppermute(value, 'space', [(i, i + 1 if i % 2 else i - 1) for i in ran...  7.05 us
    ppermute x4, waiting for transfers between devices, swap_cores(): lax.ppermute(value, 'space', [(i, i ^ 1) for i in range(lax.axis_size('sp...  1.96 us
  transfers between devices with their start and end apart: 20, of which 11 were waited for; matrix products, arithmetic and copies ran while one was open for 0% of the time, Pallas kernels for 5%

profile of v3, /device:TPU:7, one launch (start us, length us, event | category | flops | bytes accessed | tf_op | source)
XLA Modules:
  0.0 81.2 jit_solution(17995899138612289523)
XLA Ops:
  0.6 0.9 %copy-done.2 = f32[1,64,4,256]{3,2,1,0:T(4,128)S(1)} copy-done((f32[1,64,4,256]{3,2,1,0:T(4,128)S(1)}, f32[1,64,4,256]{3,2,1,0:T(4,128)}, u32[]{:S(2)}) %copy-start.2) | copy-done | bytes 262168
  3.7 3.6 %collective-permute-start.1 = (bf16[64,2560]{1,0:T(8,128)(2,1)S(1)}, bf16[64,2560]{1,0:T(8,128)(2,1)S(1)}, u32[]{:S(2)}, u32[]{:S(2)}) collective-permute-start(bf16[64,2560]{1,0:T(8,128)(2,1)S(1)} %shard_map.94), channel_id=1, source_target_pairs={{1,2},{2,1},{3,4},{4,3},{5,6},{6,5},{7,8},{8,7},{9,10},{10,9},{11,... | collective-permute-start | bytes 983048 | tf_op jit(solution)/shard_map/ppermute | solution.py:380
  8.1 4.2 %collective-permute-done.1.chip.refs_2_ = bf16[64,2560]{1,0:T(8,128)(2,1)S(1)} collective-permute-done((bf16[64,2560]{1,0:T(8,128)(2,1)S(1)}, bf16[64,2560]{1,0:T(8,128)(2,1)S(1)}, u32[]{:S(2)}, u32[]{:S(2)}) %collective-permute-start.1) | collective-permute-done | bytes 327712 | tf_op jit(solution)/shard_map/ppermute | solution.py:380
  12.4 1.4 %collective-permute-done.2.edge.refs_1_ = bf16[64,1536]{1,0:T(8,128)(2,1)S(1)} collective-permute-done((bf16[64,1536]{1,0:T(8,128)(2,1)S(1)}, bf16[64,1536]{1,0:T(8,128)(2,1)S(1)}, u32[]{:S(2)}, u32[]{:S(2)}) %collective-permute-start.2) | collective-permute-done | bytes 196640 | tf_op jit(solution)/shard_map/ppermute | solution.py:375
  13.8 5.3 %shard_map.98 = (bf16[64,1024]{1,0:T(8,128)(2,1)S(1)}, bf16[192,1536]{1,0:T(8,128)(2,1)S(1)}, bf16[192,1536]{1,0:T(8,128)(2,1)S(1)}, bf16[192,1536]{1,0:T(8,128)...) custom-call(f32[64,1024]{1,0:T(8,128)S(1)} %get-tuple-element.64.sta, ...), custom_call_target="tpu_custom_call" | custom-call | flops 1962934272 | bytes 6754304 | tf_op jit(solution)/shard_map/pallas_call | solution.py:363
  20.1 3.5 %collective-permute-start.4 = (bf16[64,1024]{1,0:T(8,128)(2,1)S(1)}, bf16[64,1024]{1,0:T(8,128)(2,1)S(1)}, u32[]{:S(2)}, u32[]{:S(2)}) collective-permute-start(bf16[64,1024]{1,0:T(8,128)(2,1)S(1)} %get-tuple-element.70), channel_id=1, source_target_pairs={{1,2},{2,1},{3,4},{4,3},{5,6},{6,5},{7,8},{8,7},{9,10},{10,9},{11,... | collective-permute-start | bytes 393224 | tf_op jit(solution)/shard_map/ppermute | solution.py:380
  24.2 2.2 %collective-permute-done.4.chip = bf16[64,1024]{1,0:T(8,128)(2,1)S(1)} collective-permute-done((bf16[64,1024]{1,0:T(8,128)(2,1)S(1)}, bf16[64,1024]{1,0:T(8,128)(2,1)S(1)}, u32[]{:S(2)}, u32[]{:S(2)}) %collective-permute-start.4) | collective-permute-done | bytes 131104 | tf_op jit(solution)/shard_map/ppermute | solution.py:380
  26.3 1.9 %shard_map.100 = (f32[64,1024]{1,0:T(8,128)S(1)}, bf16[64,512]{1,0:T(8,128)(2,1)S(1)}, bf16[64,512]{1,0:T(8,128)(2,1)S(1)}, bf16[64,1024]{1,0:T(8,128)(2,1)S(1)}...) custom-call(f32[64,1024]{1,0:T(8,128)S(1)} %get-tuple-element.69.adjoint, ...), custom_call_target="tpu_custom_call" | custom-call | flops 679477248 | bytes 3604480 | tf_op jit(solution)/shard_map/pallas_call | solution.py:363
  28.4 3.8 %collective-permute-start.6 = (bf16[64,512]{1,0:T(8,128)(2,1)S(1)}, bf16[64,512]{1,0:T(8,128)(2,1)S(1)}, u32[]{:S(2)}, u32[]{:S(2)}) collective-permute-start(bf16[64,512]{1,0:T(8,128)(2,1)S(1)} %get-tuple-element.79), channel_id=1, source_target_pairs={{1,2},{2,1},{3,4},{4,3},{5,6},{6,5},{7,8},{8,7},{9,10},{10,9},{11,... | collective-permute-start | bytes 196616 | tf_op jit(solution)/shard_map/ppermute | solution.py:380
  35.6 1.6 %collective-permute-done.7.part = bf16[16,80,128]{2,1,0:T(8,128)(2,1)S(1)} collective-permute-done((bf16[16,80,128]{2,1,0:T(8,128)(2,1)S(1)}, bf16[16,80,128]{2,1,0:T(8,128)(2,1)S(1)}, u32[]{:S(2)}, u32[]{:S(2)}) %collective-permute-start.7) | collective-permute-done | bytes 327712 | tf_op jit(solution)/shard_map/ppermute | solution.py:389
  37.3 2.7 %collective-permute-start.8 = (bf16[4,80,128]{2,1,0:T(8,128)(2,1)S(1)}, bf16[4,80,128]{2,1,0:T(8,128)(2,1)S(1)}, u32[]{:S(2)}, u32[]{:S(2)}) collective-permute-start(bf16[4,80,128]{2,1,0:T(8,128)(2,1)S(1)} %get-tuple-element.95), channel_id=1, source_target_pairs={{0,2},{1,3},{2,0},{3,1},{4,6},{5,7},{6,4},{7,5},{8,10},{9,11},{10,... | collective-permute-start | bytes 245768 | tf_op jit(solution)/shard_map/ppermute | solution.py:389
  40.1 7.6 %collective-permute-start.9 = (bf16[4,80,128]{2,1,0:T(8,128)(2,1)S(1)}, bf16[4,80,128]{2,1,0:T(8,128)(2,1)S(1)}, u32[]{:S(2)}, u32[]{:S(2)}) collective-permute-start(bf16[4,80,128]{2,1,0:T(8,128)(2,1)S(1)} %get-tuple-element.96), channel_id=1, source_target_pairs={{0,4},{1,5},{2,6},{3,7},{4,0},{5,1},{6,2},{7,3},{8,12},{9,13},{10,... | collective-permute-start | bytes 245768 | tf_op jit(solution)/shard_map/ppermute | solution.py:389
  48.2 9.4 %collective-permute-start.15 = (bf16[64,1024]{1,0:T(8,128)(2,1)S(1)}, bf16[64,1024]{1,0:T(8,128)(2,1)S(1)}, u32[]{:S(2)}, u32[]{:S(2)}) collective-permute-start(bf16[64,1024]{1,0:T(8,128)(2,1)S(1)} %get-tuple-element.99), channel_id=1, source_target_pairs={{32,64},{96,128},{160,192},{64,32},{128,96},{192,160},{33,65},{97,... | collective-permute-start | bytes 393224 | tf_op jit(solution)/shard_map/ppermute | solution.py:395
  57.7 1.7 %collective-permute-start.13 = (bf16[4,80,128]{2,1,0:T(8,128)(2,1)S(1)}, bf16[4,80,128]{2,1,0:T(8,128)(2,1)S(1)}, u32[]{:S(2)}, u32[]{:S(2)}) collective-permute-start(bf16[4,80,128]{2,1,0:T(8,128)(2,1)S(1)} %shard_map.108.own), channel_id=1, source_target_pairs={{0,24},{1,25},{2,26},{3,27},{4,28},{5,29},{6,30},{7,31},{8,16},{9,... | collective-permute-start | bytes 245768 | tf_op jit(solution)/shard_map/ppermute | solution.py:389
  59.7 1.6 %collective-permute-start.11 = (bf16[4,80,128]{2,1,0:T(8,128)(2,1)S(1)}, bf16[4,80,128]{2,1,0:T(8,128)(2,1)S(1)}, u32[]{:S(2)}, u32[]{:S(2)}) collective-permute-start(bf16[4,80,128]{2,1,0:T(8,128)(2,1)S(1)} %shard_map.108.own), channel_id=1, source_target_pairs={{0,8},{1,9},{2,10},{3,11},{4,12},{5,13},{6,14},{7,15},{8,0},{9,1},... | collective-permute-start | bytes 245768 | tf_op jit(solution)/shard_map/ppermute | solution.py:389
  61.3 2.4 %collective-permute-done.13.part3 = bf16[4,80,128]{2,1,0:T(8,128)(2,1)S(1)} collective-permute-done((bf16[4,80,128]{2,1,0:T(8,128)(2,1)S(1)}, bf16[4,80,128]{2,1,0:T(8,128)(2,1)S(1)}, u32[]{:S(2)}, u32[]{:S(2)}) %collective-permute-start.13) | collective-permute-done | bytes 81952 | tf_op jit(solution)/shard_map/ppermute | solution.py:389
  63.7 6.1 %collective-permute-done.12.part2 = bf16[4,80,128]{2,1,0:T(8,128)(2,1)S(1)} collective-permute-done((bf16[4,80,128]{2,1,0:T(8,128)(2,1)S(1)}, bf16[4,80,128]{2,1,0:T(8,128)(2,1)S(1)}, u32[]{:S(2)}, u32[]{:S(2)}) %collective-permute-start.12) | collective-permute-done | bytes 81952 | tf_op jit(solution)/shard_map/ppermute | solution.py:389
  69.8 1.4 %collective-permute-start.18 = (bf16[4,80,128]{2,1,0:T(8,128)(2,1)S(1)}, bf16[4,80,128]{2,1,0:T(8,128)(2,1)S(1)}, u32[]{:S(2)}, u32[]{:S(2)}) collective-permute-start(bf16[4,80,128]{2,1,0:T(8,128)(2,1)S(1)} %shard_map.109.own), channel_id=1, source_target_pairs={{0,6},{1,7},{2,4},{3,5},{4,2},{5,3},{6,0},{7,1},{8,14},{9,15},{10,... | collective-permute-start | bytes 245768 | tf_op jit(solution)/shard_map/ppermute | solution.py:389
  71.9 1.3 %collective-permute-start.16 = (bf16[4,80,128]{2,1,0:T(8,128)(2,1)S(1)}, bf16[4,80,128]{2,1,0:T(8,128)(2,1)S(1)}, u32[]{:S(2)}, u32[]{:S(2)}) collective-permute-start(bf16[4,80,128]{2,1,0:T(8,128)(2,1)S(1)} %shard_map.109.own), channel_id=1, source_target_pairs={{0,2},{1,3},{2,0},{3,1},{4,6},{5,7},{6,4},{7,5},{8,10},{9,11},{10,... | collective-permute-start | bytes 245768 | tf_op jit(solution)/shard_map/ppermute | solution.py:389
  73.2 1.1 %shard_map.111 = (f32[1,64,4,256]{3,2,1,0:T(4,128)}, f32[1,64,4,256]{3,2,1,0:T(4,128)}) custom-call(f32[1,64,4,256]{3,2,1,0:T(4,128)S(1)} %copy-done.3, f32[1,64,4,256]{3,2,1,0:T(4,128)S(1)} %copy-done.4, bf16[64,1024]{1,0:T(8,128)(2,1)S(1)} %collective-permute-done.14.pair, bf16[64,1024]{1,0:T(8,128)(2,1)S(1)} %collective-permute-done.15.far), custom_call_target="tpu_custom_call" | custom-call | bytes 1310720 | tf_op jit(solution)/shard_map/pallas_call | solution.py:363
  74.4 1.7 %collective-permute-done.17.part2 = bf16[4,80,128]{2,1,0:T(8,128)(2,1)S(1)} collective-permute-done((bf16[4,80,128]{2,1,0:T(8,128)(2,1)S(1)}, bf16[4,80,128]{2,1,0:T(8,128)(2,1)S(1)}, u32[]{:S(2)}, u32[]{:S(2)}) %collective-permute-start.17) | collective-permute-done | bytes 81952 | tf_op jit(solution)/shard_map/ppermute | solution.py:389
  76.2 2.4 %collective-permute-start.19 = (bf16[16,80,128]{2,1,0:T(8,128)(2,1)S(1)}, bf16[16,80,128]{2,1,0:T(8,128)(2,1)S(1)}, u32[]{:S(2)}, u32[]{:S(2)}) collective-permute-start(bf16[16,80,128]{2,1,0:T(8,128)(2,1)S(1)} %shard_map.110.own), channel_id=1, source_target_pairs={{0,1},{1,0},{2,3},{3,2},{4,5},{5,4},{6,7},{7,6},{8,9},{9,8},{10,11... | collective-permute-start | bytes 983048 | tf_op jit(solution)/shard_map/ppermute | solution.py:389
  78.6 1.3 %collective-permute-done.19.part = bf16[16,80,128]{2,1,0:T(8,128)(2,1)S(1)} collective-permute-done((bf16[16,80,128]{2,1,0:T(8,128)(2,1)S(1)}, bf16[16,80,128]{2,1,0:T(8,128)(2,1)S(1)}, u32[]{:S(2)}, u32[]{:S(2)}) %collective-permute-start.19) | collective-permute-done | bytes 327712 | tf_op jit(solution)/shard_map/ppermute | solution.py:389
  79.9 1.3 %shard_map.112 = (f32[4,64,576]{2,1,0:T(8,128)}, f32[4,64,576]{2,1,0:T(8,128)}, f32[4,64]{1,0:T(4,128)}) custom-call(bf16[16,80,128]{2,1,0:T(8,128)(2,1)S(1)} %shard_map.110.own, bf16[16,80,128]{2,1,0:T(8,128)(2,1)S(1)} %collective-permute-done.19.part), custom_call_target="tpu_custom_call" | custom-call | bytes 1836032 | tf_op jit(solution)/shard_map/pallas_call | solution.py:363
  (49 shorter events, 10.0 us)
Async XLA Ops:
  1.9 1.7 %collective-permute-start = (bf16[64,1024]{1,0:T(8,128)(2,1)S(1)}, bf16[64,1024]{1,0:T(8,128)(2,1)S(1)}, u32[]{:S(2)}, u32[]{:S(2)}) collective-permute-start(bf16[64,1024]{1,0:T(8,128)(2,1)S(1)} %get-tuple-element.59.own), channel_id=1, source_target_pairs={{0,1},{1,0},{2,3},{3,2},{4,5},{5,4},{6,7},{7,6},{8,9},{9,8},{10,11... | collective-permute-start | bytes 393224 | tf_op jit(solution)/shard_map/ppermute | solution.py:375
  3.7 3.7 %copy-start = (bf16[4,64,576]{2,1,0:T(8,128)(2,1)S(1)}, bf16[4,64,576]{2,1,0:T(8,128)(2,1)}, u32[]{:S(2)}) copy-start(bf16[4,64,576]{2,1,0:T(8,128)(2,1)} %w1.3) | copy-start | bytes 884740
  3.7 3.7 %copy-start.1 = (bf16[4,64,576]{2,1,0:T(8,128)(2,1)S(1)}, bf16[4,64,576]{2,1,0:T(8,128)(2,1)}, u32[]{:S(2)}) copy-start(bf16[4,64,576]{2,1,0:T(8,128)(2,1)} %w2.3) | copy-start | bytes 884740
  3.7 4.1 %copy-start.5 = (f32[4,64]{1,0:T(4,128)S(1)}, f32[4,64]{1,0:T(4,128)}, u32[]{:S(2)}) copy-start(f32[4,64]{1,0:T(4,128)} %bias.1) | copy-start | bytes 3076
  3.7 8.5 %collective-permute-start.1 = (bf16[64,2560]{1,0:T(8,128)(2,1)S(1)}, bf16[64,2560]{1,0:T(8,128)(2,1)S(1)}, u32[]{:S(2)}, u32[]{:S(2)}) collective-permute-start(bf16[64,2560]{1,0:T(8,128)(2,1)S(1)} %shard_map.94), channel_id=1, source_target_pairs={{1,2},{2,1},{3,4},{4,3},{5,6},{6,5},{7,8},{8,7},{9,10},{10,9},{11,... | collective-permute-start | bytes 983048 | tf_op jit(solution)/shard_map/ppermute | solution.py:380
  12.3 1.5 %collective-permute-start.2 = (bf16[64,1536]{1,0:T(8,128)(2,1)S(1)}, bf16[64,1536]{1,0:T(8,128)(2,1)S(1)}, u32[]{:S(2)}, u32[]{:S(2)}) collective-permute-start(bf16[64,1536]{1,0:T(8,128)(2,1)S(1)} %shard_map.97), channel_id=1, source_target_pairs={{0,1},{1,0},{2,3},{3,2},{4,5},{5,4},{6,7},{7,6},{8,9},{9,8},{10,11... | collective-permute-start | bytes 589832 | tf_op jit(solution)/shard_map/ppermute | solution.py:375
  20.1 6.3 %collective-permute-start.4 = (bf16[64,1024]{1,0:T(8,128)(2,1)S(1)}, bf16[64,1024]{1,0:T(8,128)(2,1)S(1)}, u32[]{:S(2)}, u32[]{:S(2)}) collective-permute-start(bf16[64,1024]{1,0:T(8,128)(2,1)S(1)} %get-tuple-element.70), channel_id=1, source_target_pairs={{1,2},{2,1},{3,4},{4,3},{5,6},{6,5},{7,8},{8,7},{9,10},{10,9},{11,... | collective-permute-start | bytes 393224 | tf_op jit(solution)/shard_map/ppermute | solution.py:380
  23.5 2.8 %collective-permute-start.3 = (bf16[64,1024]{1,0:T(8,128)(2,1)S(1)}, bf16[64,1024]{1,0:T(8,128)(2,1)S(1)}, u32[]{:S(2)}, u32[]{:S(2)}) collective-permute-start(bf16[64,1024]{1,0:T(8,128)(2,1)S(1)} %get-tuple-element.70), channel_id=1, source_target_pairs={{0,1},{1,0},{2,3},{3,2},{4,5},{5,4},{6,7},{7,6},{8,9},{9,8},{10,11... | collective-permute-start | bytes 393224 | tf_op jit(solution)/shard_map/ppermute | solution.py:375
  28.3 5.0 %collective-permute-start.5 = (bf16[64,512]{1,0:T(8,128)(2,1)S(1)}, bf16[64,512]{1,0:T(8,128)(2,1)S(1)}, u32[]{:S(2)}, u32[]{:S(2)}) collective-permute-start(bf16[64,512]{1,0:T(8,128)(2,1)S(1)} %get-tuple-element.78), channel_id=1, source_target_pairs={{0,1},{1,0},{2,3},{3,2},{4,5},{5,4},{6,7},{7,6},{8,9},{9,8},{10,11... | collective-permute-start | bytes 196616 | tf_op jit(solution)/shard_map/ppermute | solution.py:375
  28.4 5.6 %collective-permute-start.6 = (bf16[64,512]{1,0:T(8,128)(2,1)S(1)}, bf16[64,512]{1,0:T(8,128)(2,1)S(1)}, u32[]{:S(2)}, u32[]{:S(2)}) collective-permute-start(bf16[64,512]{1,0:T(8,128)(2,1)S(1)} %get-tuple-element.79), channel_id=1, source_target_pairs={{1,2},{2,1},{3,4},{4,3},{5,6},{6,5},{7,8},{8,7},{9,10},{10,9},{11,... | collective-permute-start | bytes 196616 | tf_op jit(solution)/shard_map/ppermute | solution.py:380
  35.5 1.7 %collective-permute-start.7 = (bf16[16,80,128]{2,1,0:T(8,128)(2,1)S(1)}, bf16[16,80,128]{2,1,0:T(8,128)(2,1)S(1)}, u32[]{:S(2)}, u32[]{:S(2)}) collective-permute-start(bf16[16,80,128]{2,1,0:T(8,128)(2,1)S(1)} %get-tuple-element.93), channel_id=1, source_target_pairs={{0,1},{1,0},{2,3},{3,2},{4,5},{5,4},{6,7},{7,6},{8,9},{9,8},{10,11... | collective-permute-start | bytes 983048 | tf_op jit(solution)/shard_map/ppermute | solution.py:389
  37.3 20.3 %collective-permute-start.8 = (bf16[4,80,128]{2,1,0:T(8,128)(2,1)S(1)}, bf16[4,80,128]{2,1,0:T(8,128)(2,1)S(1)}, u32[]{:S(2)}, u32[]{:S(2)}) collective-permute-start(bf16[4,80,128]{2,1,0:T(8,128)(2,1)S(1)} %get-tuple-element.95), channel_id=1, source_target_pairs={{0,2},{1,3},{2,0},{3,1},{4,6},{5,7},{6,4},{7,5},{8,10},{9,11},{10,... | collective-permute-start | bytes 245768 | tf_op jit(solution)/shard_map/ppermute | solution.py:389
  40.1 17.6 %collective-permute-start.9 = (bf16[4,80,128]{2,1,0:T(8,128)(2,1)S(1)}, bf16[4,80,128]{2,1,0:T(8,128)(2,1)S(1)}, u32[]{:S(2)}, u32[]{:S(2)}) collective-permute-start(bf16[4,80,128]{2,1,0:T(8,128)(2,1)S(1)} %get-tuple-element.96), channel_id=1, source_target_pairs={{0,4},{1,5},{2,6},{3,7},{4,0},{5,1},{6,2},{7,3},{8,12},{9,13},{10,... | collective-permute-start | bytes 245768 | tf_op jit(solution)/shard_map/ppermute | solution.py:389
  47.6 10.0 %collective-permute-start.10 = (bf16[4,80,128]{2,1,0:T(8,128)(2,1)S(1)}, bf16[4,80,128]{2,1,0:T(8,128)(2,1)S(1)}, u32[]{:S(2)}, u32[]{:S(2)}) collective-permute-start(bf16[4,80,128]{2,1,0:T(8,128)(2,1)S(1)} %get-tuple-element.97), channel_id=1, source_target_pairs={{0,6},{1,7},{2,4},{3,5},{4,2},{5,3},{6,0},{7,1},{8,14},{9,15},{10,... | collective-permute-start | bytes 245768 | tf_op jit(solution)/shard_map/ppermute | solution.py:389
  47.7 22.2 %collective-permute-start.14 = (bf16[64,1024]{1,0:T(8,128)(2,1)S(1)}, bf16[64,1024]{1,0:T(8,128)(2,1)S(1)}, u32[]{:S(2)}, u32[]{:S(2)}) collective-permute-start(bf16[64,1024]{1,0:T(8,128)(2,1)S(1)} %get-tuple-element.98), channel_id=1, source_target_pairs={{0,32},{64,96},{128,160},{192,224},{32,0},{96,64},{160,128},{224,1... | collective-permute-start | bytes 393224 | tf_op jit(solution)/shard_map/ppermute | solution.py:395
  48.2 21.6 %collective-permute-start.15 = (bf16[64,1024]{1,0:T(8,128)(2,1)S(1)}, bf16[64,1024]{1,0:T(8,128)(2,1)S(1)}, u32[]{:S(2)}, u32[]{:S(2)}) collective-permute-start(bf16[64,1024]{1,0:T(8,128)(2,1)S(1)} %get-tuple-element.99), channel_id=1, source_target_pairs={{32,64},{96,128},{160,192},{64,32},{128,96},{192,160},{33,65},{97,... | collective-permute-start | bytes 393224 | tf_op jit(solution)/shard_map/ppermute | solution.py:395
  57.7 15.5 %copy-start.3 = (f32[1,64,4,256]{3,2,1,0:T(4,128)S(1)}, f32[1,64,4,256]{3,2,1,0:T(4,128)}, u32[]{:S(2)}) copy-start(f32[1,64,4,256]{3,2,1,0:T(4,128)} %c.1) | copy-start | bytes 786436
  57.7 6.0 %collective-permute-start.13 = (bf16[4,80,128]{2,1,0:T(8,128)(2,1)S(1)}, bf16[4,80,128]{2,1,0:T(8,128)(2,1)S(1)}, u32[]{:S(2)}, u32[]{:S(2)}) collective-permute-start(bf16[4,80,128]{2,1,0:T(8,128)(2,1)S(1)} %shard_map.108.own), channel_id=1, source_target_pairs={{0,24},{1,25},{2,26},{3,27},{4,28},{5,29},{6,30},{7,31},{8,16},{9,... | collective-permute-start | bytes 245768 | tf_op jit(solution)/shard_map/ppermute | solution.py:389
  59.4 10.4 %collective-permute-start.12 = (bf16[4,80,128]{2,1,0:T(8,128)(2,1)S(1)}, bf16[4,80,128]{2,1,0:T(8,128)(2,1)S(1)}, u32[]{:S(2)}, u32[]{:S(2)}) collective-permute-start(bf16[4,80,128]{2,1,0:T(8,128)(2,1)S(1)} %shard_map.108.own), channel_id=1, source_target_pairs={{0,16},{1,17},{2,18},{3,19},{4,20},{5,21},{6,22},{7,23},{8,24},{9,... | collective-permute-start | bytes 245768 | tf_op jit(solution)/shard_map/ppermute | solution.py:389
  59.7 10.0 %collective-permute-start.11 = (bf16[4,80,128]{2,1,0:T(8,128)(2,1)S(1)}, bf16[4,80,128]{2,1,0:T(8,128)(2,1)S(1)}, u32[]{:S(2)}, u32[]{:S(2)}) collective-permute-start(bf16[4,80,128]{2,1,0:T(8,128)(2,1)S(1)} %shard_map.108.own), channel_id=1, source_target_pairs={{0,8},{1,9},{2,10},{3,11},{4,12},{5,13},{6,14},{7,15},{8,0},{9,1},... | collective-permute-start | bytes 245768 | tf_op jit(solution)/shard_map/ppermute | solution.py:389
  69.8 4.6 %collective-permute-start.18 = (bf16[4,80,128]{2,1,0:T(8,128)(2,1)S(1)}, bf16[4,80,128]{2,1,0:T(8,128)(2,1)S(1)}, u32[]{:S(2)}, u32[]{:S(2)}) collective-permute-start(bf16[4,80,128]{2,1,0:T(8,128)(2,1)S(1)} %shard_map.109.own), channel_id=1, source_target_pairs={{0,6},{1,7},{2,4},{3,5},{4,2},{5,3},{6,0},{7,1},{8,14},{9,15},{10,... | collective-permute-start | bytes 245768 | tf_op jit(solution)/shard_map/ppermute | solution.py:389
  71.3 4.9 %collective-permute-start.17 = (bf16[4,80,128]{2,1,0:T(8,128)(2,1)S(1)}, bf16[4,80,128]{2,1,0:T(8,128)(2,1)S(1)}, u32[]{:S(2)}, u32[]{:S(2)}) collective-permute-start(bf16[4,80,128]{2,1,0:T(8,128)(2,1)S(1)} %shard_map.109.own), channel_id=1, source_target_pairs={{0,4},{1,5},{2,6},{3,7},{4,0},{5,1},{6,2},{7,3},{8,12},{9,13},{10,... | collective-permute-start | bytes 245768 | tf_op jit(solution)/shard_map/ppermute | solution.py:389
  71.9 4.3 %collective-permute-start.16 = (bf16[4,80,128]{2,1,0:T(8,128)(2,1)S(1)}, bf16[4,80,128]{2,1,0:T(8,128)(2,1)S(1)}, u32[]{:S(2)}, u32[]{:S(2)}) collective-permute-start(bf16[4,80,128]{2,1,0:T(8,128)(2,1)S(1)} %shard_map.109.own), channel_id=1, source_target_pairs={{0,2},{1,3},{2,0},{3,1},{4,6},{5,7},{6,4},{7,5},{8,10},{9,11},{10,... | collective-permute-start | bytes 245768 | tf_op jit(solution)/shard_map/ppermute | solution.py:389
  76.2 3.7 %collective-permute-start.19 = (bf16[16,80,128]{2,1,0:T(8,128)(2,1)S(1)}, bf16[16,80,128]{2,1,0:T(8,128)(2,1)S(1)}, u32[]{:S(2)}, u32[]{:S(2)}) collective-permute-start(bf16[16,80,128]{2,1,0:T(8,128)(2,1)S(1)} %shard_map.110.own), channel_id=1, source_target_pairs={{0,1},{1,0},{2,3},{3,2},{4,5},{5,4},{6,7},{7,6},{8,9},{9,8},{10,11... | collective-permute-start | bytes 983048 | tf_op jit(solution)/shard_map/ppermute | solution.py:389
  (2 other events, 2.1 us)

commit v4 on v3

--- a/solution.py
+++ b/solution.py
@@ -21,12 +21,14 @@
 
 def put_stack(dst, j, row):
     chans, breadth = row.shape
+    row = row.astype(BF16)
     col = lax.broadcasted_iota(jnp.int32, row.shape, 1)
-    left = jnp.where(col == 0, 0.0, pltpu.roll(row, 1, axis=1))
-    right = jnp.where(col == breadth - 1, 0.0, pltpu.roll(row, breadth - 1, axis=1))
-    dst[0:chans, lanes(j, breadth)] = left.astype(BF16)
-    dst[chans : 2 * chans, lanes(j, breadth)] = row.astype(BF16)
-    dst[2 * chans : 3 * chans, lanes(j, breadth)] = right.astype(BF16)
+    none = jnp.zeros((), BF16)
+    left = jnp.where(col == 0, none, pltpu.roll(row, 1, axis=1))
+    right = jnp.where(col == breadth - 1, none, pltpu.roll(row, breadth - 1, axis=1))
+    dst[0:chans, lanes(j, breadth)] = left
+    dst[chans : 2 * chans, lanes(j, breadth)] = row
+    dst[2 * chans : 3 * chans, lanes(j, breadth)] = right
 
 
 def conv(src, first, rows, weight, chans, breadth):
@@ -250,6 +252,9 @@
     return lax.dot_general(left, right, (((1,), (1,)), ((), ())), preferred_element_type=F32)
 
 
+CHUNK = 4 * 72 + 8
+
+
 def grad_kernel(skip, b, hidden, e, inputs, pay, bd, ed):
     chans, breadth = b.shape[0], b.shape[1] // 4
     for src, dst in ((b, bd), (e, ed)):
@@ -261,20 +266,22 @@
     both = jnp.concatenate([two, one], axis=1)
     for c in range(8):
         for t in range(3):
-            pay[c, 24 * t : 24 * t + 24, :] = both[24 * c : 24 * c + 24, 128 * t : 128 * t + 128]
-        pay[c, 72:80, :] = jnp.zeros((8, 128), F32)
+            at = 72 * (c % 4) + 24 * t
+            pay[c // 4, at : at + 24, :] = both[24 * c : 24 * c + 24, 128 * t : 128 * t + 128]
+    for c in range(2):
+        pay[c, 288:CHUNK, :] = jnp.zeros((8, 128), F32)
     ones = jnp.ones((8, e.shape[1]), BF16)
-    pay[0, 72:73, 0:chans] = outer(ones, e[...])[0:1]
-
-
-def packed(total):
-    body = total[..., 0:72, :].astype(BF16)
-    tail = total[..., 72:80, :]
-    bias = tail[..., 0:1, :] + tail[..., 1:2, :]
+    pay[0, 288:289, 0:chans] = outer(ones, e[...])[0:1]
+
+
+def put_packed(dst, at, total):
+    tail = total[288:CHUNK]
+    bias = tail[0:1] + tail[1:2]
     head = bias.astype(BF16).astype(F32)
-    row = lax.broadcasted_iota(jnp.int32, tail.shape, tail.ndim - 2)
+    row = lax.broadcasted_iota(jnp.int32, tail.shape, 0)
     tail = jnp.where(row == 0, head, jnp.where(row == 1, bias - head, 0.0))
-    return body, tail.astype(BF16)
+    dst[at, 0:288] = total[0:288].astype(BF16)
+    dst[at, 288:CHUNK] = tail.astype(BF16)
 
 
 def where_am_i():
@@ -284,43 +291,32 @@
 
 def split_kernel(g0, g1, g2, g3, send, keep):
     core, _, _ = where_am_i()
-    for k in range(8):
-        for at, low, high in ((k, g0, g2), (k + 8, g1, g3)):
+    for k in range(2):
+        for at, low, high in ((k, g0, g2), (k + 2, g1, g3)):
             a, b = low[k], high[k]
             keep[at] = jnp.where(core == 0, a, b)
-            body, tail = packed(jnp.where(core == 0, b, a))
-            send[at, 0:72] = body
-            send[at, 72:80] = tail
+            put_packed(send, at, jnp.where(core == 0, b, a))
 
 
 def spread_kernel(keep_in, part, keep, *sends):
     _, mine, _ = where_am_i()
     for k, dst in enumerate((keep, *sends)):
-        for n in range(4):
-            at = (mine ^ k) * 4 + n
-            total = keep_in[at] + part[at].astype(F32)
-            if k == 0:
-                dst[n] = total
-            else:
-                body, tail = packed(total)
-                dst[n, 0:72] = body
-                dst[n, 72:80] = tail
+        total = keep_in[mine ^ k] + part[mine ^ k].astype(F32)
+        if k == 0:
+            dst[0] = total
+        else:
+            put_packed(dst, 0, total)
 
 
 def total_kernel(own, part1, part2, part3, out):
-    for n in range(out.shape[0]):
-        pairs = own[n].astype(F32) + part1[n].astype(F32), part2[n].astype(F32) + part3[n].astype(F32)
-        body, tail = packed(pairs[0] + pairs[1])
-        out[n, 0:72] = body
-        out[n, 72:80] = tail
-
-
-def join_kernel(axis, own, part1, part2, part3, out):
-    mine = where_am_i()[axis]
-    count = own.shape[0]
+    pairs = own[0].astype(F32) + part1[0].astype(F32), part2[0].astype(F32) + part3[0].astype(F32)
+    put_packed(out, 0, pairs[0] + pairs[1])
+
+
+def join_kernel(own, part1, part2, part3, out):
+    _, mine, _ = where_am_i()
     for k, src in enumerate((own, part1, part2, part3)):
-        for n in range(count):
-            out[(mine ^ k) * count + n] = src[n]
+        out[mine ^ k] = src[0]
 
 
 def points_kernel(c, q, pair, far, points, adjoints):
@@ -334,28 +330,75 @@
         adjoints[0, :, r, :] = jnp.where(last, q[0, :, r, :], jnp.where(even_group(), a, b))
 
 
-def exit_kernel(scale, own, part, one, two, bias):
-    chans = one.shape[1]
-    core, _, _ = where_am_i()
+def lay_out(scale, src, base, one, two, wide_one, wide_two, sems):
+    chans = wide_one.shape[1]
     wide = 3 * chans
-    for l in range(one.shape[0]):
-        base = 8 * (l % 2)
-
-        def piece(k, rows, width=128):
-            a, b = own[base + k, rows, 0:width].astype(F32), part[base + k, rows, 0:width].astype(F32)
-            return jnp.where(core == l // 2, a, b)
-
-        cols = [
-            jnp.concatenate([piece(k, slice(24 * t, 24 * t + 24)) for k in range(8)], axis=0)
-            for t in range(3)
-        ]
+    copies = []
+    for l in range(2):
+        cols = []
+        for t in range(3):
+            at = [(2 * l + k // 4, 72 * (k % 4) + 24 * t) for k in range(8)]
+            cols.append(jnp.concatenate([src[c, r : r + 24, :].astype(F32) for c, r in at], axis=0))
         full = jnp.concatenate(cols, axis=1) * scale
         for dy in range(3):
             rows = full[dy * chans : (dy + 1) * chans]
-            two[l, :, dy * wide : (dy + 1) * wide] = rows[:, :wide]
-            one[l, :, dy * wide : (dy + 1) * wide] = rows[:, wide:]
-        low = piece(0, slice(72, 74), chans)
-        bias[l : l + 1, :] = (low[0:1] + low[1:2]) * scale
+            wide_two[l, :, dy * wide : (dy + 1) * wide] = rows[:, :wide]
+            wide_one[l, :, dy * wide : (dy + 1) * wide] = rows[:, wide:]
+        for k, (held, out) in enumerate(((wide_one, one), (wide_two, two))):
+            copy = pltpu.make_async_copy(held.at[l], out.at[base + l], sems.at[2 * l + k])
+            copy.start()
+            copies.append(copy)
+    return copies
+
+
+def exit_own_kernel(scale, own, one, two, wide_one, wide_two, sems):
+    core, _, _ = where_am_i()
+    for copy in lay_out(scale, own, 2 * core, one, two, wide_one, wide_two, sems):
+        copy.wait()
+
+
+def exit_other_kernel(scale, part, own, _one, _two, one, two, bias, wide_one, wide_two, sems, vec, sem):
+    core, _, _ = where_am_i()
+    chans = vec.shape[1]
+    for l in range(vec.shape[0]):
+        at = (2 * (l % 2), slice(288, 290), slice(0, chans))
+        low = jnp.where(core == l // 2, own[at].astype(F32), part[at].astype(F32))
+        vec[l : l + 1, :] = (low[0:1] + low[1:2]) * scale
+    last = pltpu.make_async_copy(vec, bias, sem)
+    last.start()
+    for copy in lay_out(scale, part, 2 * (1 - core), one, two, wide_one, wide_two, sems):
+        copy.wait()
+    last.wait()
+
+
+def exit_calls(scale, mine, part, grad, vec):
+    _, chans, wide = grad.shape
+    hbm = pl.BlockSpec(memory_space=pl.ANY)
+    near = pl.BlockSpec(memory_space=VMEM)
+    scratch = [VMEM((2, chans, wide), F32)] * 2 + [pltpu.SemaphoreType.DMA((4,))]
+    options = dict(
+        cost_estimate=pl.CostEstimate(flops=0, bytes_accessed=16 * chans * wide, transcendentals=0),
+        compiler_params=pltpu.CompilerParams(vmem_limit_bytes=40 << 20),
+    )
+    held = pl.pallas_call(
+        functools.partial(exit_own_kernel, scale),
+        out_shape=[grad, grad],
+        in_specs=[near],
+        out_specs=[hbm, hbm],
+        scratch_shapes=scratch,
+        name="exit_own",
+        **options,
+    )(mine)
+    return pl.pallas_call(
+        functools.partial(exit_other_kernel, scale),
+        out_shape=[grad, grad, vec],
+        in_specs=[near, near, hbm, hbm],
+        out_specs=[hbm, hbm, hbm],
+        scratch_shapes=[*scratch, VMEM(vec.shape, F32), pltpu.SemaphoreType.DMA],
+        input_output_aliases={2: 0, 3: 1},
+        name="exit_other",
+        **options,
+    )(part, mine, *held)
 
 
 def call(kernel, outs, args, scratch=(), flops=0):
@@ -448,7 +491,7 @@
     def grads(skip, b, hidden, e, inputs):
         return call(
             functools.partial(grad_kernel, skip),
-            [S((8, 80, 128), F32)],
+            [S((2, CHUNK, 128), F32)],
             [b, hidden, e, inputs],
             [VMEM((wide, 6 * breadth), BF16)] * 2,
             flops=12 * row_flops,
@@ -472,27 +515,25 @@
     g0 = grads(0, b0, a0, e0, x0)
 
     def chunks(n, kind):
-        return S((n, 80, 128), kind)
-
-    send, keep = call(split_kernel, [chunks(16, BF16), chunks(16, F32)], [g0, g1, g2, g3])
-    keep, *sends = call(spread_kernel, [chunks(4, F32)] + [chunks(4, BF16)] * 3, [keep, partner(send, 1)])
+        return S((n, CHUNK, 128), kind)
+
+    send, keep = call(split_kernel, [chunks(4, BF16), chunks(4, F32)], [g0, g1, g2, g3])
+    keep, *sends = call(spread_kernel, [chunks(1, F32)] + [chunks(1, BF16)] * 3, [keep, partner(send, 1)])
     parts = [partner(value, 2 * (k + 1)) for k, value in enumerate(sends)]
     far = pairs_of_groups(far, 1)
     pair = pairs_of_groups(pair, 0)
-    mine = call(total_kernel, [chunks(4, BF16)], [keep, *parts])[0]
+    mine = call(total_kernel, [chunks(1, BF16)], [keep, *parts])[0]
     parts = [partner(mine, 8 * (k + 1)) for k in range(3)]
-    mine = call(total_kernel, [chunks(4, BF16)], [mine, *parts])[0]
+    mine = call(total_kernel, [chunks(1, BF16)], [mine, *parts])[0]
     mine, pair, far = lax.optimization_barrier((mine, pair, far))
     parts = [partner(mine, 2 * (k + 1)) for k in range(3)]
     points, adjoints = call(
         points_kernel, [S(c_points.shape, F32), S(c_points.shape, F32)], [c_points, adjoint_points, pair, far]
     )
-    mine = call(functools.partial(join_kernel, 1), [chunks(16, BF16)], [mine, *parts])[0]
+    mine = call(join_kernel, [chunks(4, BF16)], [mine, *parts])[0]
     mine, points, adjoints = lax.optimization_barrier((mine, points, adjoints))
-    grad = S(conv1_weight.shape, F32)
-    one, two, vec = call(
-        functools.partial(exit_kernel, scale), [grad, grad, S(bias1.shape, F32)], [mine, partner(mine, 1)]
-    )
+    part = partner(mine, 1)
+    one, two, vec = exit_calls(scale, mine, part, S(conv1_weight.shape, F32), S(bias1.shape, F32))
     return points, adjoints, one, two, vec
 
 

time: 81.5 us -> 80 us (0.982)
  waiting for transfers between devices: 22.2 us -> 20.6 us
    pallas_call x0 -> x2, Pallas kernels: none -> 1.97 us  [the longest x1 0.99 us: exit_calls(): pl.pallas_call(functools.partial(exit_other_kernel, scale), out_shape=[gr...]
    pallas_call x21 -> x20, Pallas kernels: 15.5 us -> 13.7 us  [call(): pl.pallas_call(kernel, out_shape=outs, in_specs=[pl.BlockSpec(memory_spac...]
    ppermute x11, waiting for transfers between devices: 13.2 us -> 11.6 us  [partner(): lax.ppermute(value, 'space', [(i, i ^ mask) for i in range(lax.axis_size(...]
  transfers between devices with their start and end apart: 20 -> 20, of which waited for: 11 -> 11; matrix products, arithmetic and copies ran while one was open for 0% -> 0% of each run, Pallas kernels for 5% -> 6%
where the time goes in v4:
time: 80 us; the launch traced here: 79.8 us
  starting transfers between devices  41.5 us (52%)
  waiting for transfers between devices  20.6 us (26%)
  Pallas kernels  15.6 us (20%)
  between operations  1.07 us (1%)
  local copies, waits for them, and re-layouts  0.97 us (1%)
    ppermute x11, starting transfers between devices, partner(): lax.ppermute(value, 'space', [(i, i ^ mask) for i in range(lax.axis_size(...  19.7 us
    pallas_call x20, Pallas kernels, call(): pl.pallas_call(kernel, out_shape=outs, in_specs=[pl.BlockSpec(memory_spac...  13.7 us
    ppermute x11, waiting for transfers between devices, partner(): lax.ppermute(value, 'space', [(i, i ^ mask) for i in range(lax.axis_size(...  11.6 us
    ppermute x3, starting transfers between devices, swap_chips(): lax.ppermute(value, 'space', [(i, i + 1 if i % 2 else i - 1) for i in ran...  10.8 us
    ppermute x2, starting transfers between devices, pairs_of_groups(): return lax.ppermute(block, 'depth', pairs + [(b, a) for a, b in pairs])  9.96 us
    ppermute x3, waiting for transfers between devices, swap_chips(): lax.ppermute(value, 'space', [(i, i + 1 if i % 2 else i - 1) for i in ran...  7.04 us
    ppermute x4, waiting for transfers between devices, swap_cores(): lax.ppermute(value, 'space', [(i, i ^ 1) for i in range(lax.axis_size('sp...  1.96 us
  transfers between devices with their start and end apart: 20, of which 11 were waited for; matrix products, arithmetic and copies ran while one was open for 0% of the time, Pallas kernels for 6%

profile of v4, /device:TPU:7, one launch (start us, length us, event | category | flops | bytes accessed | tf_op | source)
XLA Modules:
  0.0 79.8 jit_solution(16811564638323586256)
XLA Ops:
  0.6 0.9 %copy-done.2 = f32[1,64,4,256]{3,2,1,0:T(4,128)S(1)} copy-done((f32[1,64,4,256]{3,2,1,0:T(4,128)S(1)}, f32[1,64,4,256]{3,2,1,0:T(4,128)}, u32[]{:S(2)}) %copy-start.2) | copy-done | bytes 262168
  3.7 3.6 %collective-permute-start.1 = (bf16[64,2560]{1,0:T(8,128)(2,1)S(1)}, bf16[64,2560]{1,0:T(8,128)(2,1)S(1)}, u32[]{:S(2)}, u32[]{:S(2)}) collective-permute-start(bf16[64,2560]{1,0:T(8,128)(2,1)S(1)} %shard_map.94), channel_id=1, source_target_pairs={{1,2},{2,1},{3,4},{4,3},{5,6},{6,5},{7,8},{8,7},{9,10},{10,9},{11,... | collective-permute-start | bytes 983048 | tf_op jit(solution)/shard_map/ppermute | solution.py:423
  8.1 4.2 %collective-permute-done.1.chip.refs_2_ = bf16[64,2560]{1,0:T(8,128)(2,1)S(1)} collective-permute-done((bf16[64,2560]{1,0:T(8,128)(2,1)S(1)}, bf16[64,2560]{1,0:T(8,128)(2,1)S(1)}, u32[]{:S(2)}, u32[]{:S(2)}) %collective-permute-start.1) | collective-permute-done | bytes 327712 | tf_op jit(solution)/shard_map/ppermute | solution.py:423
  12.4 1.4 %collective-permute-done.2.edge.refs_1_ = bf16[64,1536]{1,0:T(8,128)(2,1)S(1)} collective-permute-done((bf16[64,1536]{1,0:T(8,128)(2,1)S(1)}, bf16[64,1536]{1,0:T(8,128)(2,1)S(1)}, u32[]{:S(2)}, u32[]{:S(2)}) %collective-permute-start.2) | collective-permute-done | bytes 196640 | tf_op jit(solution)/shard_map/ppermute | solution.py:418
  13.8 4.8 %shard_map.98 = (bf16[64,1024]{1,0:T(8,128)(2,1)S(1)}, bf16[192,1536]{1,0:T(8,128)(2,1)S(1)}, bf16[192,1536]{1,0:T(8,128)(2,1)S(1)}, bf16[192,1536]{1,0:T(8,128)...) custom-call(f32[64,1024]{1,0:T(8,128)S(1)} %get-tuple-element.66.sta, ...), custom_call_target="tpu_custom_call" | custom-call | flops 1962934272 | bytes 6754304 | tf_op jit(solution)/shard_map/pallas_call | solution.py:406
  19.5 3.5 %collective-permute-start.4 = (bf16[64,1024]{1,0:T(8,128)(2,1)S(1)}, bf16[64,1024]{1,0:T(8,128)(2,1)S(1)}, u32[]{:S(2)}, u32[]{:S(2)}) collective-permute-start(bf16[64,1024]{1,0:T(8,128)(2,1)S(1)} %get-tuple-element.72), channel_id=1, source_target_pairs={{1,2},{2,1},{3,4},{4,3},{5,6},{6,5},{7,8},{8,7},{9,10},{10,9},{11,... | collective-permute-start | bytes 393224 | tf_op jit(solution)/shard_map/ppermute | solution.py:423
  23.6 2.2 %collective-permute-done.4.chip = bf16[64,1024]{1,0:T(8,128)(2,1)S(1)} collective-permute-done((bf16[64,1024]{1,0:T(8,128)(2,1)S(1)}, bf16[64,1024]{1,0:T(8,128)(2,1)S(1)}, u32[]{:S(2)}, u32[]{:S(2)}) %collective-permute-start.4) | collective-permute-done | bytes 131104 | tf_op jit(solution)/shard_map/ppermute | solution.py:423
  25.8 1.9 %shard_map.100 = (f32[64,1024]{1,0:T(8,128)S(1)}, bf16[64,512]{1,0:T(8,128)(2,1)S(1)}, bf16[64,512]{1,0:T(8,128)(2,1)S(1)}, bf16[64,1024]{1,0:T(8,128)(2,1)S(1)}...) custom-call(f32[64,1024]{1,0:T(8,128)S(1)} %get-tuple-element.71.adjoint, ...), custom_call_target="tpu_custom_call" | custom-call | flops 679477248 | bytes 3604480 | tf_op jit(solution)/shard_map/pallas_call | solution.py:406
  27.8 3.8 %collective-permute-start.6 = (bf16[64,512]{1,0:T(8,128)(2,1)S(1)}, bf16[64,512]{1,0:T(8,128)(2,1)S(1)}, u32[]{:S(2)}, u32[]{:S(2)}) collective-permute-start(bf16[64,512]{1,0:T(8,128)(2,1)S(1)} %get-tuple-element.81), channel_id=1, source_target_pairs={{1,2},{2,1},{3,4},{4,3},{5,6},{6,5},{7,8},{8,7},{9,10},{10,9},{11,... | collective-permute-start | bytes 196616 | tf_op jit(solution)/shard_map/ppermute | solution.py:423
  35.1 1.6 %collective-permute-done.7.part = bf16[4,296,128]{2,1,0:T(8,128)(2,1)S(1)} collective-permute-done((bf16[4,296,128]{2,1,0:T(8,128)(2,1)S(1)}, bf16[4,296,128]{2,1,0:T(8,128)(2,1)S(1)}, u32[]{:S(2)}, u32[]{:S(2)}) %collective-permute-start.7) | collective-permute-done | bytes 303136 | tf_op jit(solution)/shard_map/ppermute | solution.py:432
  36.7 2.7 %collective-permute-start.8 = (bf16[1,296,128]{2,1,0:T(8,128)(2,1)S(1)}, bf16[1,296,128]{2,1,0:T(8,128)(2,1)S(1)}, u32[]{:S(2)}, u32[]{:S(2)}) collective-permute-start(bf16[1,296,128]{2,1,0:T(8,128)(2,1)S(1)} %get-tuple-element.97), channel_id=1, source_target_pairs={{0,2},{1,3},{2,0},{3,1},{4,6},{5,7},{6,4},{7,5},{8,10},{9,11},{10,... | collective-permute-start | bytes 227336 | tf_op jit(solution)/shard_map/ppermute | solution.py:432
  39.5 7.6 %collective-permute-start.9 = (bf16[1,296,128]{2,1,0:T(8,128)(2,1)S(1)}, bf16[1,296,128]{2,1,0:T(8,128)(2,1)S(1)}, u32[]{:S(2)}, u32[]{:S(2)}) collective-permute-start(bf16[1,296,128]{2,1,0:T(8,128)(2,1)S(1)} %get-tuple-element.98), channel_id=1, source_target_pairs={{0,4},{1,5},{2,6},{3,7},{4,0},{5,1},{6,2},{7,3},{8,12},{9,13},{10,... | collective-permute-start | bytes 227336 | tf_op jit(solution)/shard_map/ppermute | solution.py:432
  47.6 9.4 %collective-permute-start.15 = (bf16[64,1024]{1,0:T(8,128)(2,1)S(1)}, bf16[64,1024]{1,0:T(8,128)(2,1)S(1)}, u32[]{:S(2)}, u32[]{:S(2)}) collective-permute-start(bf16[64,1024]{1,0:T(8,128)(2,1)S(1)} %get-tuple-element.101), channel_id=1, source_target_pairs={{32,64},{96,128},{160,192},{64,32},{128,96},{192,160},{33,65},{97,... | collective-permute-start | bytes 393224 | tf_op jit(solution)/shard_map/ppermute | solution.py:438
  57.1 1.7 %collective-permute-start.13 = (bf16[1,296,128]{2,1,0:T(8,128)(2,1)S(1)}, bf16[1,296,128]{2,1,0:T(8,128)(2,1)S(1)}, u32[]{:S(2)}, u32[]{:S(2)}) collective-permute-start(bf16[1,296,128]{2,1,0:T(8,128)(2,1)S(1)} %shard_map.108.own), channel_id=1, source_target_pairs={{0,24},{1,25},{2,26},{3,27},{4,28},{5,29},{6,30},{7,31},{8,16},{9,... | collective-permute-start | bytes 227336 | tf_op jit(solution)/shard_map/ppermute | solution.py:432
  59.1 1.6 %collective-permute-start.11 = (bf16[1,296,128]{2,1,0:T(8,128)(2,1)S(1)}, bf16[1,296,128]{2,1,0:T(8,128)(2,1)S(1)}, u32[]{:S(2)}, u32[]{:S(2)}) collective-permute-start(bf16[1,296,128]{2,1,0:T(8,128)(2,1)S(1)} %shard_map.108.own), channel_id=1, source_target_pairs={{0,8},{1,9},{2,10},{3,11},{4,12},{5,13},{6,14},{7,15},{8,0},{9,1},... | collective-permute-start | bytes 227336 | tf_op jit(solution)/shard_map/ppermute | solution.py:432
  60.8 2.2 %collective-permute-done.13.part3 = bf16[1,296,128]{2,1,0:T(8,128)(2,1)S(1)} collective-permute-done((bf16[1,296,128]{2,1,0:T(8,128)(2,1)S(1)}, bf16[1,296,128]{2,1,0:T(8,128)(2,1)S(1)}, u32[]{:S(2)}, u32[]{:S(2)}) %collective-permute-start.13) | collective-permute-done | bytes 75808 | tf_op jit(solution)/shard_map/ppermute | solution.py:432
  63.0 5.6 %collective-permute-done.12.part2 = bf16[1,296,128]{2,1,0:T(8,128)(2,1)S(1)} collective-permute-done((bf16[1,296,128]{2,1,0:T(8,128)(2,1)S(1)}, bf16[1,296,128]{2,1,0:T(8,128)(2,1)S(1)}, u32[]{:S(2)}, u32[]{:S(2)}) %collective-permute-start.12) | collective-permute-done | bytes 75808 | tf_op jit(solution)/shard_map/ppermute | solution.py:432
  68.7 1.6 %collective-permute-start.18 = (bf16[1,296,128]{2,1,0:T(8,128)(2,1)S(1)}, bf16[1,296,128]{2,1,0:T(8,128)(2,1)S(1)}, u32[]{:S(2)}, u32[]{:S(2)}) collective-permute-start(bf16[1,296,128]{2,1,0:T(8,128)(2,1)S(1)} %shard_map.109.own), channel_id=1, source_target_pairs={{0,6},{1,7},{2,4},{3,5},{4,2},{5,3},{6,0},{7,1},{8,14},{9,15},{10,... | collective-permute-start | bytes 227336 | tf_op jit(solution)/shard_map/ppermute | solution.py:432
  71.0 1.1 %collective-permute-start.16 = (bf16[1,296,128]{2,1,0:T(8,128)(2,1)S(1)}, bf16[1,296,128]{2,1,0:T(8,128)(2,1)S(1)}, u32[]{:S(2)}, u32[]{:S(2)}) collective-permute-start(bf16[1,296,128]{2,1,0:T(8,128)(2,1)S(1)} %shard_map.109.own), channel_id=1, source_target_pairs={{0,2},{1,3},{2,0},{3,1},{4,6},{5,7},{6,4},{7,5},{8,10},{9,11},{10,... | collective-permute-start | bytes 227336 | tf_op jit(solution)/shard_map/ppermute | solution.py:432
  72.0 1.1 %shard_map.111 = (f32[1,64,4,256]{3,2,1,0:T(4,128)}, f32[1,64,4,256]{3,2,1,0:T(4,128)}) custom-call(f32[1,64,4,256]{3,2,1,0:T(4,128)S(1)} %copy-done.3, f32[1,64,4,256]{3,2,1,0:T(4,128)S(1)} %copy-done.4, bf16[64,1024]{1,0:T(8,128)(2,1)S(1)} %collective-permute-done.14.pair, bf16[64,1024]{1,0:T(8,128)(2,1)S(1)} %collective-permute-done.15.far), custom_call_target="tpu_custom_call" | custom-call | bytes 1310720 | tf_op jit(solution)/shard_map/pallas_call | solution.py:406
  73.2 1.9 %collective-permute-done.17.part2 = bf16[1,296,128]{2,1,0:T(8,128)(2,1)S(1)} collective-permute-done((bf16[1,296,128]{2,1,0:T(8,128)(2,1)S(1)}, bf16[1,296,128]{2,1,0:T(8,128)(2,1)S(1)}, u32[]{:S(2)}, u32[]{:S(2)}) %collective-permute-start.17) | collective-permute-done | bytes 75808 | tf_op jit(solution)/shard_map/ppermute | solution.py:432
  75.1 2.3 %collective-permute-start.19 = (bf16[4,296,128]{2,1,0:T(8,128)(2,1)S(1)}, bf16[4,296,128]{2,1,0:T(8,128)(2,1)S(1)}, u32[]{:S(2)}, u32[]{:S(2)}) collective-permute-start(bf16[4,296,128]{2,1,0:T(8,128)(2,1)S(1)} %shard_map.110.own), channel_id=1, source_target_pairs={{0,1},{1,0},{2,3},{3,2},{4,5},{5,4},{6,7},{7,6},{8,9},{9,8},{10,11... | collective-permute-start | bytes 909320 | tf_op jit(solution)/shard_map/ppermute | solution.py:432
  77.4 1.0 %exit_own.1 = (f32[4,64,576]{2,1,0:T(8,128)}, f32[4,64,576]{2,1,0:T(8,128)}) custom-call(bf16[4,296,128]{2,1,0:T(8,128)(2,1)S(1)} %shard_map.110.own), custom_call_target="tpu_custom_call" | custom-call | bytes 589824 | tf_op jit(solution)/shard_map/exit_own/pallas_call | solution.py:383
  78.6 1.0 %exit_other.1 = (f32[4,64,576]{2,1,0:T(8,128)}, f32[4,64,576]{2,1,0:T(8,128)}, f32[4,64]{1,0:T(4,128)}) custom-call(bf16[4,296,128]{2,1,0:T(8,128)(2,1)S(1)} %collective-permute-done.19.part, bf16[4,296,128]{2,1,0:T(8,128)(2,1)S(1)} %shard_map.110.own, f32[4,64,576]{2,1,0:T(8,128)} %get-tuple-element.110._one, ...), custom_call_target="tpu_custom_call", output_to_operand_aliasing={{0}: (2, {}), {1}: (3, {})} | custom-call | bytes 589824 | tf_op jit(solution)/shard_map/exit_other/pallas_call | solution.py:392
  (50 shorter events, 10.3 us)
Async XLA Ops:
  1.9 1.7 %collective-permute-start = (bf16[64,1024]{1,0:T(8,128)(2,1)S(1)}, bf16[64,1024]{1,0:T(8,128)(2,1)S(1)}, u32[]{:S(2)}, u32[]{:S(2)}) collective-permute-start(bf16[64,1024]{1,0:T(8,128)(2,1)S(1)} %get-tuple-element.61.own), channel_id=1, source_target_pairs={{0,1},{1,0},{2,3},{3,2},{4,5},{5,4},{6,7},{7,6},{8,9},{9,8},{10,11... | collective-permute-start | bytes 393224 | tf_op jit(solution)/shard_map/ppermute | solution.py:418
  3.7 3.7 %copy-start = (bf16[4,64,576]{2,1,0:T(8,128)(2,1)S(1)}, bf16[4,64,576]{2,1,0:T(8,128)(2,1)}, u32[]{:S(2)}) copy-start(bf16[4,64,576]{2,1,0:T(8,128)(2,1)} %w1.3) | copy-start | bytes 884740
  3.7 3.7 %copy-start.1 = (bf16[4,64,576]{2,1,0:T(8,128)(2,1)S(1)}, bf16[4,64,576]{2,1,0:T(8,128)(2,1)}, u32[]{:S(2)}) copy-start(bf16[4,64,576]{2,1,0:T(8,128)(2,1)} %w2.3) | copy-start | bytes 884740
  3.7 4.1 %copy-start.5 = (f32[4,64]{1,0:T(4,128)S(1)}, f32[4,64]{1,0:T(4,128)}, u32[]{:S(2)}) copy-start(f32[4,64]{1,0:T(4,128)} %bias.1) | copy-start | bytes 3076
  3.7 8.5 %collective-permute-start.1 = (bf16[64,2560]{1,0:T(8,128)(2,1)S(1)}, bf16[64,2560]{1,0:T(8,128)(2,1)S(1)}, u32[]{:S(2)}, u32[]{:S(2)}) collective-permute-start(bf16[64,2560]{1,0:T(8,128)(2,1)S(1)} %shard_map.94), channel_id=1, source_target_pairs={{1,2},{2,1},{3,4},{4,3},{5,6},{6,5},{7,8},{8,7},{9,10},{10,9},{11,... | collective-permute-start | bytes 983048 | tf_op jit(solution)/shard_map/ppermute | solution.py:423
  12.3 1.5 %collective-permute-start.2 = (bf16[64,1536]{1,0:T(8,128)(2,1)S(1)}, bf16[64,1536]{1,0:T(8,128)(2,1)S(1)}, u32[]{:S(2)}, u32[]{:S(2)}) collective-permute-start(bf16[64,1536]{1,0:T(8,128)(2,1)S(1)} %shard_map.97), channel_id=1, source_target_pairs={{0,1},{1,0},{2,3},{3,2},{4,5},{5,4},{6,7},{7,6},{8,9},{9,8},{10,11... | collective-permute-start | bytes 589832 | tf_op jit(solution)/shard_map/ppermute | solution.py:418
  19.5 6.3 %collective-permute-start.4 = (bf16[64,1024]{1,0:T(8,128)(2,1)S(1)}, bf16[64,1024]{1,0:T(8,128)(2,1)S(1)}, u32[]{:S(2)}, u32[]{:S(2)}) collective-permute-start(bf16[64,1024]{1,0:T(8,128)(2,1)S(1)} %get-tuple-element.72), channel_id=1, source_target_pairs={{1,2},{2,1},{3,4},{4,3},{5,6},{6,5},{7,8},{8,7},{9,10},{10,9},{11,... | collective-permute-start | bytes 393224 | tf_op jit(solution)/shard_map/ppermute | solution.py:423
  23.0 2.8 %collective-permute-start.3 = (bf16[64,1024]{1,0:T(8,128)(2,1)S(1)}, bf16[64,1024]{1,0:T(8,128)(2,1)S(1)}, u32[]{:S(2)}, u32[]{:S(2)}) collective-permute-start(bf16[64,1024]{1,0:T(8,128)(2,1)S(1)} %get-tuple-element.72), channel_id=1, source_target_pairs={{0,1},{1,0},{2,3},{3,2},{4,5},{5,4},{6,7},{7,6},{8,9},{9,8},{10,11... | collective-permute-start | bytes 393224 | tf_op jit(solution)/shard_map/ppermute | solution.py:418
  27.7 5.0 %collective-permute-start.5 = (bf16[64,512]{1,0:T(8,128)(2,1)S(1)}, bf16[64,512]{1,0:T(8,128)(2,1)S(1)}, u32[]{:S(2)}, u32[]{:S(2)}) collective-permute-start(bf16[64,512]{1,0:T(8,128)(2,1)S(1)} %get-tuple-element.80), channel_id=1, source_target_pairs={{0,1},{1,0},{2,3},{3,2},{4,5},{5,4},{6,7},{7,6},{8,9},{9,8},{10,11... | collective-permute-start | bytes 196616 | tf_op jit(solution)/shard_map/ppermute | solution.py:418
  27.8 5.6 %collective-permute-start.6 = (bf16[64,512]{1,0:T(8,128)(2,1)S(1)}, bf16[64,512]{1,0:T(8,128)(2,1)S(1)}, u32[]{:S(2)}, u32[]{:S(2)}) collective-permute-start(bf16[64,512]{1,0:T(8,128)(2,1)S(1)} %get-tuple-element.81), channel_id=1, source_target_pairs={{1,2},{2,1},{3,4},{4,3},{5,6},{6,5},{7,8},{8,7},{9,10},{10,9},{11,... | collective-permute-start | bytes 196616 | tf_op jit(solution)/shard_map/ppermute | solution.py:423
  35.0 1.7 %collective-permute-start.7 = (bf16[4,296,128]{2,1,0:T(8,128)(2,1)S(1)}, bf16[4,296,128]{2,1,0:T(8,128)(2,1)S(1)}, u32[]{:S(2)}, u32[]{:S(2)}) collective-permute-start(bf16[4,296,128]{2,1,0:T(8,128)(2,1)S(1)} %get-tuple-element.95), channel_id=1, source_target_pairs={{0,1},{1,0},{2,3},{3,2},{4,5},{5,4},{6,7},{7,6},{8,9},{9,8},{10,11... | collective-permute-start | bytes 909320 | tf_op jit(solution)/shard_map/ppermute | solution.py:432
  36.7 20.3 %collective-permute-start.8 = (bf16[1,296,128]{2,1,0:T(8,128)(2,1)S(1)}, bf16[1,296,128]{2,1,0:T(8,128)(2,1)S(1)}, u32[]{:S(2)}, u32[]{:S(2)}) collective-permute-start(bf16[1,296,128]{2,1,0:T(8,128)(2,1)S(1)} %get-tuple-element.97), channel_id=1, source_target_pairs={{0,2},{1,3},{2,0},{3,1},{4,6},{5,7},{6,4},{7,5},{8,10},{9,11},{10,... | collective-permute-start | bytes 227336 | tf_op jit(solution)/shard_map/ppermute | solution.py:432
  39.5 17.6 %collective-permute-start.9 = (bf16[1,296,128]{2,1,0:T(8,128)(2,1)S(1)}, bf16[1,296,128]{2,1,0:T(8,128)(2,1)S(1)}, u32[]{:S(2)}, u32[]{:S(2)}) collective-permute-start(bf16[1,296,128]{2,1,0:T(8,128)(2,1)S(1)} %get-tuple-element.98), channel_id=1, source_target_pairs={{0,4},{1,5},{2,6},{3,7},{4,0},{5,1},{6,2},{7,3},{8,12},{9,13},{10,... | collective-permute-start | bytes 227336 | tf_op jit(solution)/shard_map/ppermute | solution.py:432
  47.1 10.0 %collective-permute-start.10 = (bf16[1,296,128]{2,1,0:T(8,128)(2,1)S(1)}, bf16[1,296,128]{2,1,0:T(8,128)(2,1)S(1)}, u32[]{:S(2)}, u32[]{:S(2)}) collective-permute-start(bf16[1,296,128]{2,1,0:T(8,128)(2,1)S(1)} %get-tuple-element.99), channel_id=1, source_target_pairs={{0,6},{1,7},{2,4},{3,5},{4,2},{5,3},{6,0},{7,1},{8,14},{9,15},{10,... | collective-permute-start | bytes 227336 | tf_op jit(solution)/shard_map/ppermute | solution.py:432
  47.1 21.6 %collective-permute-start.14 = (bf16[64,1024]{1,0:T(8,128)(2,1)S(1)}, bf16[64,1024]{1,0:T(8,128)(2,1)S(1)}, u32[]{:S(2)}, u32[]{:S(2)}) collective-permute-start(bf16[64,1024]{1,0:T(8,128)(2,1)S(1)} %get-tuple-element.100), channel_id=1, source_target_pairs={{0,32},{64,96},{128,160},{192,224},{32,0},{96,64},{160,128},{224,1... | collective-permute-start | bytes 393224 | tf_op jit(solution)/shard_map/ppermute | solution.py:438
  47.6 21.0 %collective-permute-start.15 = (bf16[64,1024]{1,0:T(8,128)(2,1)S(1)}, bf16[64,1024]{1,0:T(8,128)(2,1)S(1)}, u32[]{:S(2)}, u32[]{:S(2)}) collective-permute-start(bf16[64,1024]{1,0:T(8,128)(2,1)S(1)} %get-tuple-element.101), channel_id=1, source_target_pairs={{32,64},{96,128},{160,192},{64,32},{128,96},{192,160},{33,65},{97,... | collective-permute-start | bytes 393224 | tf_op jit(solution)/shard_map/ppermute | solution.py:438
  57.1 14.9 %copy-start.3 = (f32[1,64,4,256]{3,2,1,0:T(4,128)S(1)}, f32[1,64,4,256]{3,2,1,0:T(4,128)}, u32[]{:S(2)}) copy-start(f32[1,64,4,256]{3,2,1,0:T(4,128)} %c.1) | copy-start | bytes 786436
  57.1 5.9 %collective-permute-start.13 = (bf16[1,296,128]{2,1,0:T(8,128)(2,1)S(1)}, bf16[1,296,128]{2,1,0:T(8,128)(2,1)S(1)}, u32[]{:S(2)}, u32[]{:S(2)}) collective-permute-start(bf16[1,296,128]{2,1,0:T(8,128)(2,1)S(1)} %shard_map.108.own), channel_id=1, source_target_pairs={{0,24},{1,25},{2,26},{3,27},{4,28},{5,29},{6,30},{7,31},{8,16},{9,... | collective-permute-start | bytes 227336 | tf_op jit(solution)/shard_map/ppermute | solution.py:432
  58.8 9.8 %collective-permute-start.12 = (bf16[1,296,128]{2,1,0:T(8,128)(2,1)S(1)}, bf16[1,296,128]{2,1,0:T(8,128)(2,1)S(1)}, u32[]{:S(2)}, u32[]{:S(2)}) collective-permute-start(bf16[1,296,128]{2,1,0:T(8,128)(2,1)S(1)} %shard_map.108.own), channel_id=1, source_target_pairs={{0,16},{1,17},{2,18},{3,19},{4,20},{5,21},{6,22},{7,23},{8,24},{9,... | collective-permute-start | bytes 227336 | tf_op jit(solution)/shard_map/ppermute | solution.py:432
  59.1 9.5 %collective-permute-start.11 = (bf16[1,296,128]{2,1,0:T(8,128)(2,1)S(1)}, bf16[1,296,128]{2,1,0:T(8,128)(2,1)S(1)}, u32[]{:S(2)}, u32[]{:S(2)}) collective-permute-start(bf16[1,296,128]{2,1,0:T(8,128)(2,1)S(1)} %shard_map.108.own), channel_id=1, source_target_pairs={{0,8},{1,9},{2,10},{3,11},{4,12},{5,13},{6,14},{7,15},{8,0},{9,1},... | collective-permute-start | bytes 227336 | tf_op jit(solution)/shard_map/ppermute | solution.py:432
  68.7 4.5 %collective-permute-start.18 = (bf16[1,296,128]{2,1,0:T(8,128)(2,1)S(1)}, bf16[1,296,128]{2,1,0:T(8,128)(2,1)S(1)}, u32[]{:S(2)}, u32[]{:S(2)}) collective-permute-start(bf16[1,296,128]{2,1,0:T(8,128)(2,1)S(1)} %shard_map.109.own), channel_id=1, source_target_pairs={{0,6},{1,7},{2,4},{3,5},{4,2},{5,3},{6,0},{7,1},{8,14},{9,15},{10,... | collective-permute-start | bytes 227336 | tf_op jit(solution)/shard_map/ppermute | solution.py:432
  70.2 4.8 %collective-permute-start.17 = (bf16[1,296,128]{2,1,0:T(8,128)(2,1)S(1)}, bf16[1,296,128]{2,1,0:T(8,128)(2,1)S(1)}, u32[]{:S(2)}, u32[]{:S(2)}) collective-permute-start(bf16[1,296,128]{2,1,0:T(8,128)(2,1)S(1)} %shard_map.109.own), channel_id=1, source_target_pairs={{0,4},{1,5},{2,6},{3,7},{4,0},{5,1},{6,2},{7,3},{8,12},{9,13},{10,... | collective-permute-start | bytes 227336 | tf_op jit(solution)/shard_map/ppermute | solution.py:432
  71.0 4.1 %collective-permute-start.16 = (bf16[1,296,128]{2,1,0:T(8,128)(2,1)S(1)}, bf16[1,296,128]{2,1,0:T(8,128)(2,1)S(1)}, u32[]{:S(2)}, u32[]{:S(2)}) collective-permute-start(bf16[1,296,128]{2,1,0:T(8,128)(2,1)S(1)} %shard_map.109.own), channel_id=1, source_target_pairs={{0,2},{1,3},{2,0},{3,1},{4,6},{5,7},{6,4},{7,5},{8,10},{9,11},{10,... | collective-permute-start | bytes 227336 | tf_op jit(solution)/shard_map/ppermute | solution.py:432
  75.1 3.5 %collective-permute-start.19 = (bf16[4,296,128]{2,1,0:T(8,128)(2,1)S(1)}, bf16[4,296,128]{2,1,0:T(8,128)(2,1)S(1)}, u32[]{:S(2)}, u32[]{:S(2)}) collective-permute-start(bf16[4,296,128]{2,1,0:T(8,128)(2,1)S(1)} %shard_map.110.own), channel_id=1, source_target_pairs={{0,1},{1,0},{2,3},{3,2},{4,5},{5,4},{6,7},{7,6},{8,9},{9,8},{10,11... | collective-permute-start | bytes 909320 | tf_op jit(solution)/shard_map/ppermute | solution.py:432
  (2 other events, 2.1 us)

commit v5 on v4

--- a/solution.py
+++ b/solution.py
@@ -156,16 +156,23 @@
             put_stack(dst, k, gate(softplus(value + offset), k + 1 - reach))
         if pos < 2:
             hidden[pos][...] = dst[:, lanes(reach - 2, breadth, 6)]
+        if pos == 3:
+            break
         for k, value in conv(dst, 0, 2 * reach, weights[pos, 1], chans, breadth):
             row = k + 2 - reach
             at = lanes(row + 6, breadth)
-            value = (mid[:, at] if pos else start(row)) + STEP * value
-            if pos == 3:
-                out[:, lanes(row, breadth)] = value.astype(BF16)
-            else:
-                value = gate(value, row)
-                put_stack(xs, k, value)
-                mid[:, at] = value
+            value = gate((mid[:, at] if pos else start(row)) + STEP * value, row)
+            put_stack(xs, k, value)
+            mid[:, at] = value
+            if pos == 2 and 0 <= row < 4:
+                out[:, lanes(row, breadth)] = value
+
+
+def last_kernel(state, hidden, weights, out):
+    chans, breadth = state.shape[0], state.shape[1] // 4
+    for k, value in conv(hidden, 0, 4, weights[3, 1], chans, breadth):
+        at = lanes(k, breadth)
+        out[:, at] = (state[:, at] + STEP * value).astype(BF16)
 
 
 def slope(stack, j, chans, breadth):
@@ -178,8 +185,6 @@
     for row in range(-2, 6):
         if 0 <= row < 4:
             value = STEP * adjoint[:, lanes(row, breadth)]
-            if final is not None:
-                outs[2][:, lanes(row, breadth)] = value.astype(BF16)
         else:
             value = halo_rows(core, chip, even, breadth, row, 2, base)
         put_stack(bs, row + 2, value)
@@ -205,7 +210,7 @@
     return lax.axis_index("depth") % 2 == 0
 
 
-def double_kernel(pos, adjoint, core, chip, ha, hb, weights, out, near, far, ba16, ea16, bb16, eb16, bs, es, mid):
+def double_kernel(pos, adjoint, core, chip, ha, hb, weights, out, near, far, bc16, ba16, ea16, bb16, eb16, bs, es, mid):
     chans, breadth = adjoint.shape[0], adjoint.shape[1] // 4
     even = even_tile()
     for row in range(-4, 8):
@@ -244,6 +249,7 @@
         value = mid[:, lanes(k + 2, breadth)] + value
         out[:, lanes(k, breadth)] = value
         rows.append(STEP * value)
+        bc16[:, lanes(k, breadth)] = rows[k].astype(BF16)
     put_edge(near, 0, even, rows, breadth)
     put_edge(far, 0, jnp.logical_not(even), rows, breadth)
 
@@ -255,15 +261,22 @@
 CHUNK = 4 * 72 + 8
 
 
-def grad_kernel(skip, b, hidden, e, inputs, pay, bd, ed):
-    chans, breadth = b.shape[0], b.shape[1] // 4
-    for src, dst in ((b, bd), (e, ed)):
-        dst[...] = jnp.zeros_like(dst)
-        for dy in range(3):
-            dst[dy * chans : (dy + 1) * chans, lanes(dy, breadth, 4)] = src[...]
-    two = outer(bd[...], hidden[:, lanes(skip, breadth, 6)])
-    one = outer(ed[...], inputs[...])
-    both = jnp.concatenate([two, one], axis=1)
+def taps(src, dst):
+    chans, breadth = src.shape[0], src.shape[1] // 4
+    dst[...] = jnp.zeros_like(dst)
+    for dy in range(3):
+        dst[dy * chans : (dy + 1) * chans, lanes(dy, breadth, 4)] = src[...]
+
+
+def two_kernel(b, hidden, out, bd):
+    taps(b, bd)
+    out[...] = outer(bd[...], hidden[...])
+
+
+def put_grads(two, e, inputs, pay, ed):
+    chans = e.shape[0]
+    taps(e, ed)
+    both = jnp.concatenate([two, outer(ed[...], inputs[...])], axis=1)
     for c in range(8):
         for t in range(3):
             at = 72 * (c % 4) + 24 * t
@@ -272,6 +285,16 @@
         pay[c, 288:CHUNK, :] = jnp.zeros((8, 128), F32)
     ones = jnp.ones((8, e.shape[1]), BF16)
     pay[0, 288:289, 0:chans] = outer(ones, e[...])[0:1]
+
+
+def one_kernel(two, e, inputs, pay, ed):
+    put_grads(two[...], e, inputs, pay, ed)
+
+
+def grad_kernel(skip, b, hidden, e, inputs, pay, bd, ed):
+    taps(b, bd)
+    two = outer(bd[...], hidden[:, lanes(skip, b.shape[1] // 4, 6)])
+    put_grads(two, e, inputs, pay, ed)
 
 
 def put_packed(dst, at, total):
@@ -460,16 +483,17 @@
     bw = call(turn_kernel, [mats], [conv1_weight, conv2_weight])[0]
     far1, fw, bias, bw = lax.optimization_barrier((far1, fw, bias, bw))
     near2 = swap_cores(call(pass_kernel, [rows16(6)], [far1, b3])[0])
-    f16, x0, x1, x2, x3, a0, a1, a2, a3 = call(
+    s3, x0, x1, x2, x3, a0, a1, a2, a3 = call(
         forward_kernel,
-        [tile16, *[stack(6)] * 4, stack(6), stack(6), stack(10), stack(6)],
+        [tile32, *[stack(6)] * 4, stack(6), stack(6), stack(10), stack(6)],
         [s0, near1, far1, near2, fw, bias],
         [VMEM((wide, 20 * breadth), BF16), VMEM((wide, 18 * breadth), BF16), VMEM((chans, 16 * breadth), F32)],
-        flops=104 * row_flops,
+        flops=98 * row_flops,
     )
+    f16 = call(last_kernel, [tile16], [s3, a3, fw], flops=6 * row_flops)[0]
 
     def single(pos, skip, base, adjoint, core, chip, hidden, final):
-        outs = [tile32, tile16] if final is None else [tile16] * 3
+        outs = [tile32, tile16] if final is None else [tile16] * 2
         args = [adjoint, core, chip, hidden, bw]
 
         def kernel(*refs):
@@ -500,19 +524,22 @@
     q3, b2h, e3 = single(3, 0, (4, 8), q4, near2, far1, a3, None)
     near3, far3 = swaps(b2h, b2h)
     g3 = grads(0, b3, a3, e3, x3)
-    q1, near4, far4, b2, e2, b1, e1 = call(
+    q1, near4, far4, b0, b2, e2, b1, e1 = call(
         functools.partial(double_kernel, 2),
-        [tile32, rows16(2), rows16(2), tile16, tile16, tile16, tile16],
+        [tile32, rows16(2), rows16(2), *[tile16] * 5],
         [q3, near3, far3, a2, a1, bw],
         [VMEM((wide, 12 * breadth), BF16), VMEM((wide, 10 * breadth), BF16), VMEM((chans, 8 * breadth), F32)],
         flops=36 * row_flops,
     )
-    near4, far4, g3 = lax.optimization_barrier((near4, far4, g3))
+    near4, far4, g3, f16 = lax.optimization_barrier((near4, far4, g3, f16))
     near4, far4 = swaps(near4, far4)
     g2 = grads(2, b2, a2, e2, x2)
     g1 = grads(0, b1, a1, e1, x1)
-    pair, far, b0, e0 = single(0, 0, (0, 0), q1, near4, far4, a0, f16)
-    g0 = grads(0, b0, a0, e0, x0)
+    square = S((wide, wide), F32)
+    taps_scratch = [VMEM((wide, 6 * breadth), BF16)]
+    two0 = call(two_kernel, [square], [b0, a0], taps_scratch, flops=6 * row_flops)[0]
+    pair, far, e0 = single(0, 0, (0, 0), q1, near4, far4, a0, f16)
+    g0 = call(one_kernel, [S((2, CHUNK, 128), F32)], [two0, e0, x0], taps_scratch, flops=6 * row_flops)[0]
 
     def chunks(n, kind):
         return S((n, CHUNK, 128), kind)

time: 80 us -> 79.6 us (level)
    pallas_call x20 -> x22, Pallas kernels: 13.7 us -> 13.9 us  [call(): pl.pallas_call(kernel, out_shape=outs, in_specs=[pl.BlockSpec(memory_spac...]
  transfers between devices with their start and end apart: 20 -> 20, of which waited for: 11 -> 11; matrix products, arithmetic and copies ran while one was open for 0% -> 0% of each run, Pallas kernels for 6% -> 7%
where the time goes in v5:
time: 79.6 us; the launch traced here: 79.4 us
  starting transfers between devices  41.5 us (52%)
  waiting for transfers between devices  20 us (25%)
  Pallas kernels  15.9 us (20%)
  between operations  1.08 us (1%)
  local copies, waits for them, and re-layouts  0.97 us (1%)
    ppermute x11, starting transfers between devices, partner(): lax.ppermute(value, 'space', [(i, i ^ mask) for i in range(lax.axis_size(...  19.7 us
    pallas_call x22, Pallas kernels, call(): pl.pallas_call(kernel, out_shape=outs, in_specs=[pl.BlockSpec(memory_spac...  13.9 us
    ppermute x11, waiting for transfers between devices, partner(): lax.ppermute(value, 'space', [(i, i ^ mask) for i in range(lax.axis_size(...  11.6 us
    ppermute x3, starting transfers between devices, swap_chips(): lax.ppermute(value, 'space', [(i, i + 1 if i % 2 else i - 1) for i in ran...  10.8 us
    ppermute x2, starting transfers between devices, pairs_of_groups(): return lax.ppermute(block, 'depth', pairs + [(b, a) for a, b in pairs])  9.94 us
    ppermute x3, waiting for transfers between devices, swap_chips(): lax.ppermute(value, 'space', [(i, i + 1 if i % 2 else i - 1) for i in ran...  6.39 us
    ppermute x4, waiting for transfers between devices, swap_cores(): lax.ppermute(value, 'space', [(i, i ^ 1) for i in range(lax.axis_size('sp...  1.96 us
  transfers between devices with their start and end apart: 20, of which 11 were waited for; matrix products, arithmetic and copies ran while one was open for 0% of the time, Pallas kernels for 7%

profile of v5, /device:TPU:7, one launch (start us, length us, event | category | flops | bytes accessed | tf_op | source)
XLA Modules:
  0.0 79.4 jit_solution(16856900802787374513)
XLA Ops:
  0.6 0.9 %copy-done.2 = f32[1,64,4,256]{3,2,1,0:T(4,128)S(1)} copy-done((f32[1,64,4,256]{3,2,1,0:T(4,128)S(1)}, f32[1,64,4,256]{3,2,1,0:T(4,128)}, u32[]{:S(2)}) %copy-start.2) | copy-done | bytes 262168
  3.7 3.6 %collective-permute-start.1 = (bf16[64,2560]{1,0:T(8,128)(2,1)S(1)}, bf16[64,2560]{1,0:T(8,128)(2,1)S(1)}, u32[]{:S(2)}, u32[]{:S(2)}) collective-permute-start(bf16[64,2560]{1,0:T(8,128)(2,1)S(1)} %shard_map.94), channel_id=1, source_target_pairs={{1,2},{2,1},{3,4},{4,3},{5,6},{6,5},{7,8},{8,7},{9,10},{10,9},{11,... | collective-permute-start | bytes 983048 | tf_op jit(solution)/shard_map/ppermute | solution.py:446
  8.1 4.2 %collective-permute-done.1.chip.refs_2_ = bf16[64,2560]{1,0:T(8,128)(2,1)S(1)} collective-permute-done((bf16[64,2560]{1,0:T(8,128)(2,1)S(1)}, bf16[64,2560]{1,0:T(8,128)(2,1)S(1)}, u32[]{:S(2)}, u32[]{:S(2)}) %collective-permute-start.1) | collective-permute-done | bytes 327712 | tf_op jit(solution)/shard_map/ppermute | solution.py:446
  12.4 1.4 %collective-permute-done.2.edge.refs_1_ = bf16[64,1536]{1,0:T(8,128)(2,1)S(1)} collective-permute-done((bf16[64,1536]{1,0:T(8,128)(2,1)S(1)}, bf16[64,1536]{1,0:T(8,128)(2,1)S(1)}, u32[]{:S(2)}, u32[]{:S(2)}) %collective-permute-start.2) | collective-permute-done | bytes 196640 | tf_op jit(solution)/shard_map/ppermute | solution.py:441
  13.8 4.5 %shard_map.98 = (f32[64,1024]{1,0:T(8,128)S(1)}, bf16[192,1536]{1,0:T(8,128)(2,1)S(1)}, bf16[192,1536]{1,0:T(8,128)(2,1)S(1)}, bf16[192,1536]{1,0:T(8,128)(2,1)S...) custom-call(f32[64,1024]{1,0:T(8,128)S(1)} %get-tuple-element.67.sta, ...), custom_call_target="tpu_custom_call" | custom-call | flops 1849688064 | bytes 6885376 | tf_op jit(solution)/shard_map/pallas_call | solution.py:429
  19.2 3.5 %collective-permute-start.4 = (bf16[64,1024]{1,0:T(8,128)(2,1)S(1)}, bf16[64,1024]{1,0:T(8,128)(2,1)S(1)}, u32[]{:S(2)}, u32[]{:S(2)}) collective-permute-start(bf16[64,1024]{1,0:T(8,128)(2,1)S(1)} %get-tuple-element.73), channel_id=1, source_target_pairs={{1,2},{2,1},{3,4},{4,3},{5,6},{6,5},{7,8},{8,7},{9,10},{10,9},{11,... | collective-permute-start | bytes 393224 | tf_op jit(solution)/shard_map/ppermute | solution.py:446
  23.7 1.8 %collective-permute-done.4.chip = bf16[64,1024]{1,0:T(8,128)(2,1)S(1)} collective-permute-done((bf16[64,1024]{1,0:T(8,128)(2,1)S(1)}, bf16[64,1024]{1,0:T(8,128)(2,1)S(1)}, u32[]{:S(2)}, u32[]{:S(2)}) %collective-permute-start.4) | collective-permute-done | bytes 131104 | tf_op jit(solution)/shard_map/ppermute | solution.py:446
  25.5 1.9 %shard_map.100 = (f32[64,1024]{1,0:T(8,128)S(1)}, bf16[64,512]{1,0:T(8,128)(2,1)S(1)}, bf16[64,512]{1,0:T(8,128)(2,1)S(1)}, bf16[64,1024]{1,0:T(8,128)(2,1)S(1)}...) custom-call(f32[64,1024]{1,0:T(8,128)S(1)} %get-tuple-element.72.adj, ...), custom_call_target="tpu_custom_call" | custom-call | flops 679477248 | bytes 3735552 | tf_op jit(solution)/shard_map/pallas_call | solution.py:429
  27.5 3.8 %collective-permute-start.6 = (bf16[64,512]{1,0:T(8,128)(2,1)S(1)}, bf16[64,512]{1,0:T(8,128)(2,1)S(1)}, u32[]{:S(2)}, u32[]{:S(2)}) collective-permute-start(bf16[64,512]{1,0:T(8,128)(2,1)S(1)} %get-tuple-element.85), channel_id=1, source_target_pairs={{1,2},{2,1},{3,4},{4,3},{5,6},{6,5},{7,8},{8,7},{9,10},{10,9},{11,... | collective-permute-start | bytes 196616 | tf_op jit(solution)/shard_map/ppermute | solution.py:446
  34.7 1.6 %collective-permute-done.7.part = bf16[4,296,128]{2,1,0:T(8,128)(2,1)S(1)} collective-permute-done((bf16[4,296,128]{2,1,0:T(8,128)(2,1)S(1)}, bf16[4,296,128]{2,1,0:T(8,128)(2,1)S(1)}, u32[]{:S(2)}, u32[]{:S(2)}) %collective-permute-start.7) | collective-permute-done | bytes 303136 | tf_op jit(solution)/shard_map/ppermute | solution.py:455
  36.3 2.7 %collective-permute-start.8 = (bf16[1,296,128]{2,1,0:T(8,128)(2,1)S(1)}, bf16[1,296,128]{2,1,0:T(8,128)(2,1)S(1)}, u32[]{:S(2)}, u32[]{:S(2)}) collective-permute-start(bf16[1,296,128]{2,1,0:T(8,128)(2,1)S(1)} %get-tuple-element.99), channel_id=1, source_target_pairs={{0,2},{1,3},{2,0},{3,1},{4,6},{5,7},{6,4},{7,5},{8,10},{9,11},{10,... | collective-permute-start | bytes 227336 | tf_op jit(solution)/shard_map/ppermute | solution.py:455
  39.1 7.6 %collective-permute-start.9 = (bf16[1,296,128]{2,1,0:T(8,128)(2,1)S(1)}, bf16[1,296,128]{2,1,0:T(8,128)(2,1)S(1)}, u32[]{:S(2)}, u32[]{:S(2)}) collective-permute-start(bf16[1,296,128]{2,1,0:T(8,128)(2,1)S(1)} %get-tuple-element.100), channel_id=1, source_target_pairs={{0,4},{1,5},{2,6},{3,7},{4,0},{5,1},{6,2},{7,3},{8,12},{9,13},{10,... | collective-permute-start | bytes 227336 | tf_op jit(solution)/shard_map/ppermute | solution.py:455
  47.2 9.4 %collective-permute-start.15 = (bf16[64,1024]{1,0:T(8,128)(2,1)S(1)}, bf16[64,1024]{1,0:T(8,128)(2,1)S(1)}, u32[]{:S(2)}, u32[]{:S(2)}) collective-permute-start(bf16[64,1024]{1,0:T(8,128)(2,1)S(1)} %get-tuple-element.103), channel_id=1, source_target_pairs={{32,64},{96,128},{160,192},{64,32},{128,96},{192,160},{33,65},{97,... | collective-permute-start | bytes 393224 | tf_op jit(solution)/shard_map/ppermute | solution.py:461
  56.7 1.6 %collective-permute-start.13 = (bf16[1,296,128]{2,1,0:T(8,128)(2,1)S(1)}, bf16[1,296,128]{2,1,0:T(8,128)(2,1)S(1)}, u32[]{:S(2)}, u32[]{:S(2)}) collective-permute-start(bf16[1,296,128]{2,1,0:T(8,128)(2,1)S(1)} %shard_map.110.own), channel_id=1, source_target_pairs={{0,24},{1,25},{2,26},{3,27},{4,28},{5,29},{6,30},{7,31},{8,16},{9,... | collective-permute-start | bytes 227336 | tf_op jit(solution)/shard_map/ppermute | solution.py:455
  58.7 1.6 %collective-permute-start.11 = (bf16[1,296,128]{2,1,0:T(8,128)(2,1)S(1)}, bf16[1,296,128]{2,1,0:T(8,128)(2,1)S(1)}, u32[]{:S(2)}, u32[]{:S(2)}) collective-permute-start(bf16[1,296,128]{2,1,0:T(8,128)(2,1)S(1)} %shard_map.110.own), channel_id=1, source_target_pairs={{0,8},{1,9},{2,10},{3,11},{4,12},{5,13},{6,14},{7,15},{8,0},{9,1},... | collective-permute-start | bytes 227336 | tf_op jit(solution)/shard_map/ppermute | solution.py:455
  60.4 2.2 %collective-permute-done.13.part3 = bf16[1,296,128]{2,1,0:T(8,128)(2,1)S(1)} collective-permute-done((bf16[1,296,128]{2,1,0:T(8,128)(2,1)S(1)}, bf16[1,296,128]{2,1,0:T(8,128)(2,1)S(1)}, u32[]{:S(2)}, u32[]{:S(2)}) %collective-permute-start.13) | collective-permute-done | bytes 75808 | tf_op jit(solution)/shard_map/ppermute | solution.py:455
  62.6 5.6 %collective-permute-done.12.part2 = bf16[1,296,128]{2,1,0:T(8,128)(2,1)S(1)} collective-permute-done((bf16[1,296,128]{2,1,0:T(8,128)(2,1)S(1)}, bf16[1,296,128]{2,1,0:T(8,128)(2,1)S(1)}, u32[]{:S(2)}, u32[]{:S(2)}) %collective-permute-start.12) | collective-permute-done | bytes 75808 | tf_op jit(solution)/shard_map/ppermute | solution.py:455
  68.3 1.6 %collective-permute-start.18 = (bf16[1,296,128]{2,1,0:T(8,128)(2,1)S(1)}, bf16[1,296,128]{2,1,0:T(8,128)(2,1)S(1)}, u32[]{:S(2)}, u32[]{:S(2)}) collective-permute-start(bf16[1,296,128]{2,1,0:T(8,128)(2,1)S(1)} %shard_map.111.own), channel_id=1, source_target_pairs={{0,6},{1,7},{2,4},{3,5},{4,2},{5,3},{6,0},{7,1},{8,14},{9,15},{10,... | collective-permute-start | bytes 227336 | tf_op jit(solution)/shard_map/ppermute | solution.py:455
  70.6 1.1 %collective-permute-start.16 = (bf16[1,296,128]{2,1,0:T(8,128)(2,1)S(1)}, bf16[1,296,128]{2,1,0:T(8,128)(2,1)S(1)}, u32[]{:S(2)}, u32[]{:S(2)}) collective-permute-start(bf16[1,296,128]{2,1,0:T(8,128)(2,1)S(1)} %shard_map.111.own), channel_id=1, source_target_pairs={{0,2},{1,3},{2,0},{3,1},{4,6},{5,7},{6,4},{7,5},{8,10},{9,11},{10,... | collective-permute-start | bytes 227336 | tf_op jit(solution)/shard_map/ppermute | solution.py:455
  71.6 1.1 %shard_map.113 = (f32[1,64,4,256]{3,2,1,0:T(4,128)}, f32[1,64,4,256]{3,2,1,0:T(4,128)}) custom-call(f32[1,64,4,256]{3,2,1,0:T(4,128)S(1)} %copy-done.3, f32[1,64,4,256]{3,2,1,0:T(4,128)S(1)} %copy-done.4, bf16[64,1024]{1,0:T(8,128)(2,1)S(1)} %collective-permute-done.14.pair, bf16[64,1024]{1,0:T(8,128)(2,1)S(1)} %collective-permute-done.15.far), custom_call_target="tpu_custom_call" | custom-call | bytes 1310720 | tf_op jit(solution)/shard_map/pallas_call | solution.py:429
  72.8 1.9 %collective-permute-done.17.part2 = bf16[1,296,128]{2,1,0:T(8,128)(2,1)S(1)} collective-permute-done((bf16[1,296,128]{2,1,0:T(8,128)(2,1)S(1)}, bf16[1,296,128]{2,1,0:T(8,128)(2,1)S(1)}, u32[]{:S(2)}, u32[]{:S(2)}) %collective-permute-start.17) | collective-permute-done | bytes 75808 | tf_op jit(solution)/shard_map/ppermute | solution.py:455
  74.7 2.3 %collective-permute-start.19 = (bf16[4,296,128]{2,1,0:T(8,128)(2,1)S(1)}, bf16[4,296,128]{2,1,0:T(8,128)(2,1)S(1)}, u32[]{:S(2)}, u32[]{:S(2)}) collective-permute-start(bf16[4,296,128]{2,1,0:T(8,128)(2,1)S(1)} %shard_map.112.own), channel_id=1, source_target_pairs={{0,1},{1,0},{2,3},{3,2},{4,5},{5,4},{6,7},{7,6},{8,9},{9,8},{10,11... | collective-permute-start | bytes 909320 | tf_op jit(solution)/shard_map/ppermute | solution.py:455
  77.0 1.0 %exit_own.1 = (f32[4,64,576]{2,1,0:T(8,128)}, f32[4,64,576]{2,1,0:T(8,128)}) custom-call(bf16[4,296,128]{2,1,0:T(8,128)(2,1)S(1)} %shard_map.112.own), custom_call_target="tpu_custom_call" | custom-call | bytes 589824 | tf_op jit(solution)/shard_map/exit_own/pallas_call | solution.py:406
  78.2 1.0 %exit_other.1 = (f32[4,64,576]{2,1,0:T(8,128)}, f32[4,64,576]{2,1,0:T(8,128)}, f32[4,64]{1,0:T(4,128)}) custom-call(bf16[4,296,128]{2,1,0:T(8,128)(2,1)S(1)} %collective-permute-done.19.part, bf16[4,296,128]{2,1,0:T(8,128)(2,1)S(1)} %shard_map.112.own, f32[4,64,576]{2,1,0:T(8,128)} %get-tuple-element.112._one, ...), custom_call_target="tpu_custom_call", output_to_operand_aliasing={{0}: (2, {}), {1}: (3, {})} | custom-call | bytes 589824 | tf_op jit(solution)/shard_map/exit_other/pallas_call | solution.py:415
  (52 shorter events, 10.4 us)
Async XLA Ops:
  1.9 1.7 %collective-permute-start = (bf16[64,1024]{1,0:T(8,128)(2,1)S(1)}, bf16[64,1024]{1,0:T(8,128)(2,1)S(1)}, u32[]{:S(2)}, u32[]{:S(2)}) collective-permute-start(bf16[64,1024]{1,0:T(8,128)(2,1)S(1)} %get-tuple-element.62.own), channel_id=1, source_target_pairs={{0,1},{1,0},{2,3},{3,2},{4,5},{5,4},{6,7},{7,6},{8,9},{9,8},{10,11... | collective-permute-start | bytes 393224 | tf_op jit(solution)/shard_map/ppermute | solution.py:441
  3.7 3.6 %copy-start = (bf16[4,64,576]{2,1,0:T(8,128)(2,1)S(1)}, bf16[4,64,576]{2,1,0:T(8,128)(2,1)}, u32[]{:S(2)}) copy-start(bf16[4,64,576]{2,1,0:T(8,128)(2,1)} %w1.3) | copy-start | bytes 884740
  3.7 3.7 %copy-start.1 = (bf16[4,64,576]{2,1,0:T(8,128)(2,1)S(1)}, bf16[4,64,576]{2,1,0:T(8,128)(2,1)}, u32[]{:S(2)}) copy-start(bf16[4,64,576]{2,1,0:T(8,128)(2,1)} %w2.3) | copy-start | bytes 884740
  3.7 4.1 %copy-start.5 = (f32[4,64]{1,0:T(4,128)S(1)}, f32[4,64]{1,0:T(4,128)}, u32[]{:S(2)}) copy-start(f32[4,64]{1,0:T(4,128)} %bias.1) | copy-start | bytes 3076
  3.7 8.5 %collective-permute-start.1 = (bf16[64,2560]{1,0:T(8,128)(2,1)S(1)}, bf16[64,2560]{1,0:T(8,128)(2,1)S(1)}, u32[]{:S(2)}, u32[]{:S(2)}) collective-permute-start(bf16[64,2560]{1,0:T(8,128)(2,1)S(1)} %shard_map.94), channel_id=1, source_target_pairs={{1,2},{2,1},{3,4},{4,3},{5,6},{6,5},{7,8},{8,7},{9,10},{10,9},{11,... | collective-permute-start | bytes 983048 | tf_op jit(solution)/shard_map/ppermute | solution.py:446
  12.3 1.5 %collective-permute-start.2 = (bf16[64,1536]{1,0:T(8,128)(2,1)S(1)}, bf16[64,1536]{1,0:T(8,128)(2,1)S(1)}, u32[]{:S(2)}, u32[]{:S(2)}) collective-permute-start(bf16[64,1536]{1,0:T(8,128)(2,1)S(1)} %shard_map.97), channel_id=1, source_target_pairs={{0,1},{1,0},{2,3},{3,2},{4,5},{5,4},{6,7},{7,6},{8,9},{9,8},{10,11... | collective-permute-start | bytes 589832 | tf_op jit(solution)/shard_map/ppermute | solution.py:441
  19.2 6.3 %collective-permute-start.4 = (bf16[64,1024]{1,0:T(8,128)(2,1)S(1)}, bf16[64,1024]{1,0:T(8,128)(2,1)S(1)}, u32[]{:S(2)}, u32[]{:S(2)}) collective-permute-start(bf16[64,1024]{1,0:T(8,128)(2,1)S(1)} %get-tuple-element.73), channel_id=1, source_target_pairs={{1,2},{2,1},{3,4},{4,3},{5,6},{6,5},{7,8},{8,7},{9,10},{10,9},{11,... | collective-permute-start | bytes 393224 | tf_op jit(solution)/shard_map/ppermute | solution.py:446
  22.7 2.8 %collective-permute-start.3 = (bf16[64,1024]{1,0:T(8,128)(2,1)S(1)}, bf16[64,1024]{1,0:T(8,128)(2,1)S(1)}, u32[]{:S(2)}, u32[]{:S(2)}) collective-permute-start(bf16[64,1024]{1,0:T(8,128)(2,1)S(1)} %get-tuple-element.73), channel_id=1, source_target_pairs={{0,1},{1,0},{2,3},{3,2},{4,5},{5,4},{6,7},{7,6},{8,9},{9,8},{10,11... | collective-permute-start | bytes 393224 | tf_op jit(solution)/shard_map/ppermute | solution.py:441
  27.4 5.3 %collective-permute-start.5 = (bf16[64,512]{1,0:T(8,128)(2,1)S(1)}, bf16[64,512]{1,0:T(8,128)(2,1)S(1)}, u32[]{:S(2)}, u32[]{:S(2)}) collective-permute-start(bf16[64,512]{1,0:T(8,128)(2,1)S(1)} %get-tuple-element.84), channel_id=1, source_target_pairs={{0,1},{1,0},{2,3},{3,2},{4,5},{5,4},{6,7},{7,6},{8,9},{9,8},{10,11... | collective-permute-start | bytes 196616 | tf_op jit(solution)/shard_map/ppermute | solution.py:441
  27.5 5.6 %collective-permute-start.6 = (bf16[64,512]{1,0:T(8,128)(2,1)S(1)}, bf16[64,512]{1,0:T(8,128)(2,1)S(1)}, u32[]{:S(2)}, u32[]{:S(2)}) collective-permute-start(bf16[64,512]{1,0:T(8,128)(2,1)S(1)} %get-tuple-element.85), channel_id=1, source_target_pairs={{1,2},{2,1},{3,4},{4,3},{5,6},{6,5},{7,8},{8,7},{9,10},{10,9},{11,... | collective-permute-start | bytes 196616 | tf_op jit(solution)/shard_map/ppermute | solution.py:446
  34.6 1.7 %collective-permute-start.7 = (bf16[4,296,128]{2,1,0:T(8,128)(2,1)S(1)}, bf16[4,296,128]{2,1,0:T(8,128)(2,1)S(1)}, u32[]{:S(2)}, u32[]{:S(2)}) collective-permute-start(bf16[4,296,128]{2,1,0:T(8,128)(2,1)S(1)} %get-tuple-element.97), channel_id=1, source_target_pairs={{0,1},{1,0},{2,3},{3,2},{4,5},{5,4},{6,7},{7,6},{8,9},{9,8},{10,11... | collective-permute-start | bytes 909320 | tf_op jit(solution)/shard_map/ppermute | solution.py:455
  36.3 20.3 %collective-permute-start.8 = (bf16[1,296,128]{2,1,0:T(8,128)(2,1)S(1)}, bf16[1,296,128]{2,1,0:T(8,128)(2,1)S(1)}, u32[]{:S(2)}, u32[]{:S(2)}) collective-permute-start(bf16[1,296,128]{2,1,0:T(8,128)(2,1)S(1)} %get-tuple-element.99), channel_id=1, source_target_pairs={{0,2},{1,3},{2,0},{3,1},{4,6},{5,7},{6,4},{7,5},{8,10},{9,11},{10,... | collective-permute-start | bytes 227336 | tf_op jit(solution)/shard_map/ppermute | solution.py:455
  39.1 17.6 %collective-permute-start.9 = (bf16[1,296,128]{2,1,0:T(8,128)(2,1)S(1)}, bf16[1,296,128]{2,1,0:T(8,128)(2,1)S(1)}, u32[]{:S(2)}, u32[]{:S(2)}) collective-permute-start(bf16[1,296,128]{2,1,0:T(8,128)(2,1)S(1)} %get-tuple-element.100), channel_id=1, source_target_pairs={{0,4},{1,5},{2,6},{3,7},{4,0},{5,1},{6,2},{7,3},{8,12},{9,13},{10,... | collective-permute-start | bytes 227336 | tf_op jit(solution)/shard_map/ppermute | solution.py:455
  46.7 10.0 %collective-permute-start.10 = (bf16[1,296,128]{2,1,0:T(8,128)(2,1)S(1)}, bf16[1,296,128]{2,1,0:T(8,128)(2,1)S(1)}, u32[]{:S(2)}, u32[]{:S(2)}) collective-permute-start(bf16[1,296,128]{2,1,0:T(8,128)(2,1)S(1)} %get-tuple-element.101), channel_id=1, source_target_pairs={{0,6},{1,7},{2,4},{3,5},{4,2},{5,3},{6,0},{7,1},{8,14},{9,15},{10,... | collective-permute-start | bytes 227336 | tf_op jit(solution)/shard_map/ppermute | solution.py:455
  46.7 21.6 %collective-permute-start.14 = (bf16[64,1024]{1,0:T(8,128)(2,1)S(1)}, bf16[64,1024]{1,0:T(8,128)(2,1)S(1)}, u32[]{:S(2)}, u32[]{:S(2)}) collective-permute-start(bf16[64,1024]{1,0:T(8,128)(2,1)S(1)} %get-tuple-element.102), channel_id=1, source_target_pairs={{0,32},{64,96},{128,160},{192,224},{32,0},{96,64},{160,128},{224,1... | collective-permute-start | bytes 393224 | tf_op jit(solution)/shard_map/ppermute | solution.py:461
  47.2 21.0 %collective-permute-start.15 = (bf16[64,1024]{1,0:T(8,128)(2,1)S(1)}, bf16[64,1024]{1,0:T(8,128)(2,1)S(1)}, u32[]{:S(2)}, u32[]{:S(2)}) collective-permute-start(bf16[64,1024]{1,0:T(8,128)(2,1)S(1)} %get-tuple-element.103), channel_id=1, source_target_pairs={{32,64},{96,128},{160,192},{64,32},{128,96},{192,160},{33,65},{97,... | collective-permute-start | bytes 393224 | tf_op jit(solution)/shard_map/ppermute | solution.py:461
  56.7 14.9 %copy-start.3 = (f32[1,64,4,256]{3,2,1,0:T(4,128)S(1)}, f32[1,64,4,256]{3,2,1,0:T(4,128)}, u32[]{:S(2)}) copy-start(f32[1,64,4,256]{3,2,1,0:T(4,128)} %c.1) | copy-start | bytes 786436
  56.7 5.9 %collective-permute-start.13 = (bf16[1,296,128]{2,1,0:T(8,128)(2,1)S(1)}, bf16[1,296,128]{2,1,0:T(8,128)(2,1)S(1)}, u32[]{:S(2)}, u32[]{:S(2)}) collective-permute-start(bf16[1,296,128]{2,1,0:T(8,128)(2,1)S(1)} %shard_map.110.own), channel_id=1, source_target_pairs={{0,24},{1,25},{2,26},{3,27},{4,28},{5,29},{6,30},{7,31},{8,16},{9,... | collective-permute-start | bytes 227336 | tf_op jit(solution)/shard_map/ppermute | solution.py:455
  58.4 9.8 %collective-permute-start.12 = (bf16[1,296,128]{2,1,0:T(8,128)(2,1)S(1)}, bf16[1,296,128]{2,1,0:T(8,128)(2,1)S(1)}, u32[]{:S(2)}, u32[]{:S(2)}) collective-permute-start(bf16[1,296,128]{2,1,0:T(8,128)(2,1)S(1)} %shard_map.110.own), channel_id=1, source_target_pairs={{0,16},{1,17},{2,18},{3,19},{4,20},{5,21},{6,22},{7,23},{8,24},{9,... | collective-permute-start | bytes 227336 | tf_op jit(solution)/shard_map/ppermute | solution.py:455
  58.7 9.5 %collective-permute-start.11 = (bf16[1,296,128]{2,1,0:T(8,128)(2,1)S(1)}, bf16[1,296,128]{2,1,0:T(8,128)(2,1)S(1)}, u32[]{:S(2)}, u32[]{:S(2)}) collective-permute-start(bf16[1,296,128]{2,1,0:T(8,128)(2,1)S(1)} %shard_map.110.own), channel_id=1, source_target_pairs={{0,8},{1,9},{2,10},{3,11},{4,12},{5,13},{6,14},{7,15},{8,0},{9,1},... | collective-permute-start | bytes 227336 | tf_op jit(solution)/shard_map/ppermute | solution.py:455
  68.3 4.5 %collective-permute-start.18 = (bf16[1,296,128]{2,1,0:T(8,128)(2,1)S(1)}, bf16[1,296,128]{2,1,0:T(8,128)(2,1)S(1)}, u32[]{:S(2)}, u32[]{:S(2)}) collective-permute-start(bf16[1,296,128]{2,1,0:T(8,128)(2,1)S(1)} %shard_map.111.own), channel_id=1, source_target_pairs={{0,6},{1,7},{2,4},{3,5},{4,2},{5,3},{6,0},{7,1},{8,14},{9,15},{10,... | collective-permute-start | bytes 227336 | tf_op jit(solution)/shard_map/ppermute | solution.py:455
  69.8 4.8 %collective-permute-start.17 = (bf16[1,296,128]{2,1,0:T(8,128)(2,1)S(1)}, bf16[1,296,128]{2,1,0:T(8,128)(2,1)S(1)}, u32[]{:S(2)}, u32[]{:S(2)}) collective-permute-start(bf16[1,296,128]{2,1,0:T(8,128)(2,1)S(1)} %shard_map.111.own), channel_id=1, source_target_pairs={{0,4},{1,5},{2,6},{3,7},{4,0},{5,1},{6,2},{7,3},{8,12},{9,13},{10,... | collective-permute-start | bytes 227336 | tf_op jit(solution)/shard_map/ppermute | solution.py:455
  70.6 4.1 %collective-permute-start.16 = (bf16[1,296,128]{2,1,0:T(8,128)(2,1)S(1)}, bf16[1,296,128]{2,1,0:T(8,128)(2,1)S(1)}, u32[]{:S(2)}, u32[]{:S(2)}) collective-permute-start(bf16[1,296,128]{2,1,0:T(8,128)(2,1)S(1)} %shard_map.111.own), channel_id=1, source_target_pairs={{0,2},{1,3},{2,0},{3,1},{4,6},{5,7},{6,4},{7,5},{8,10},{9,11},{10,... | collective-permute-start | bytes 227336 | tf_op jit(solution)/shard_map/ppermute | solution.py:455
  74.7 3.5 %collective-permute-start.19 = (bf16[4,296,128]{2,1,0:T(8,128)(2,1)S(1)}, bf16[4,296,128]{2,1,0:T(8,128)(2,1)S(1)}, u32[]{:S(2)}, u32[]{:S(2)}) collective-permute-start(bf16[4,296,128]{2,1,0:T(8,128)(2,1)S(1)} %shard_map.112.own), channel_id=1, source_target_pairs={{0,1},{1,0},{2,3},{3,2},{4,5},{5,4},{6,7},{7,6},{8,9},{9,8},{10,11... | collective-permute-start | bytes 909320 | tf_op jit(solution)/shard_map/ppermute | solution.py:455
  (2 other events, 2.1 us)

commit v6 on v5

--- a/solution.py
+++ b/solution.py
@@ -263,9 +263,12 @@
 
 def taps(src, dst):
     chans, breadth = src.shape[0], src.shape[1] // 4
-    dst[...] = jnp.zeros_like(dst)
+    none = jnp.zeros((chans, breadth), dst.dtype)
     for dy in range(3):
-        dst[dy * chans : (dy + 1) * chans, lanes(dy, breadth, 4)] = src[...]
+        rows = slice(dy * chans, (dy + 1) * chans)
+        dst[rows, lanes(dy, breadth, 4)] = src[...]
+        for j in (*range(dy), *range(dy + 4, 6)):
+            dst[rows, lanes(j, breadth)] = none
 
 
 def two_kernel(b, hidden, out, bd):

time: 79.6 us -> 79.6 us (level)
  no operation moved by 1% of the time
where the time goes in v6:
time: 79.6 us; the launch traced here: 79.4 us
  starting transfers between devices  41.5 us (52%)
  waiting for transfers between devices  20 us (25%)
  Pallas kernels  15.9 us (20%)
  between operations  1.08 us (1%)
  local copies, waits for them, and re-layouts  0.97 us (1%)
    ppermute x11, starting transfers between devices, partner(): lax.ppermute(value, 'space', [(i, i ^ mask) for i in range(lax.axis_size(...  19.7 us
    pallas_call x22, Pallas kernels, call(): pl.pallas_call(kernel, out_shape=outs, in_specs=[pl.BlockSpec(memory_spac...  13.9 us
    ppermute x11, waiting for transfers between devices, partner(): lax.ppermute(value, 'space', [(i, i ^ mask) for i in range(lax.axis_size(...  11.6 us
    ppermute x3, starting transfers between devices, swap_chips(): lax.ppermute(value, 'space', [(i, i + 1 if i % 2 else i - 1) for i in ran...  10.8 us
    ppermute x2, starting transfers between devices, pairs_of_groups(): return lax.ppermute(block, 'depth', pairs + [(b, a) for a, b in pairs])  9.94 us
    ppermute x3, waiting for transfers between devices, swap_chips(): lax.ppermute(value, 'space', [(i, i + 1 if i % 2 else i - 1) for i in ran...  6.39 us
    ppermute x4, waiting for transfers between devices, swap_cores(): lax.ppermute(value, 'space', [(i, i ^ 1) for i in range(lax.axis_size('sp...  1.96 us
  transfers between devices with their start and end apart: 20, of which 11 were waited for; matrix products, arithmetic and copies ran while one was open for 0% of the time, Pallas kernels for 7%

profile of v6, /device:TPU:7, one launch (start us, length us, event | category | flops | bytes accessed | tf_op | source)
XLA Modules:
  0.0 79.4 jit_solution(16856900802787374513)
XLA Ops:
  0.6 0.9 %copy-done.2 = f32[1,64,4,256]{3,2,1,0:T(4,128)S(1)} copy-done((f32[1,64,4,256]{3,2,1,0:T(4,128)S(1)}, f32[1,64,4,256]{3,2,1,0:T(4,128)}, u32[]{:S(2)}) %copy-start.2) | copy-done | bytes 262168
  3.7 3.6 %collective-permute-start.1 = (bf16[64,2560]{1,0:T(8,128)(2,1)S(1)}, bf16[64,2560]{1,0:T(8,128)(2,1)S(1)}, u32[]{:S(2)}, u32[]{:S(2)}) collective-permute-start(bf16[64,2560]{1,0:T(8,128)(2,1)S(1)} %shard_map.94), channel_id=1, source_target_pairs={{1,2},{2,1},{3,4},{4,3},{5,6},{6,5},{7,8},{8,7},{9,10},{10,9},{11,... | collective-permute-start | bytes 983048 | tf_op jit(solution)/shard_map/ppermute | solution.py:449
  8.1 4.2 %collective-permute-done.1.chip.refs_2_ = bf16[64,2560]{1,0:T(8,128)(2,1)S(1)} collective-permute-done((bf16[64,2560]{1,0:T(8,128)(2,1)S(1)}, bf16[64,2560]{1,0:T(8,128)(2,1)S(1)}, u32[]{:S(2)}, u32[]{:S(2)}) %collective-permute-start.1) | collective-permute-done | bytes 327712 | tf_op jit(solution)/shard_map/ppermute | solution.py:449
  12.4 1.4 %collective-permute-done.2.edge.refs_1_ = bf16[64,1536]{1,0:T(8,128)(2,1)S(1)} collective-permute-done((bf16[64,1536]{1,0:T(8,128)(2,1)S(1)}, bf16[64,1536]{1,0:T(8,128)(2,1)S(1)}, u32[]{:S(2)}, u32[]{:S(2)}) %collective-permute-start.2) | collective-permute-done | bytes 196640 | tf_op jit(solution)/shard_map/ppermute | solution.py:444
  13.8 4.5 %shard_map.98 = (f32[64,1024]{1,0:T(8,128)S(1)}, bf16[192,1536]{1,0:T(8,128)(2,1)S(1)}, bf16[192,1536]{1,0:T(8,128)(2,1)S(1)}, bf16[192,1536]{1,0:T(8,128)(2,1)S...) custom-call(f32[64,1024]{1,0:T(8,128)S(1)} %get-tuple-element.67.sta, ...), custom_call_target="tpu_custom_call" | custom-call | flops 1849688064 | bytes 6885376 | tf_op jit(solution)/shard_map/pallas_call | solution.py:432
  19.2 3.5 %collective-permute-start.4 = (bf16[64,1024]{1,0:T(8,128)(2,1)S(1)}, bf16[64,1024]{1,0:T(8,128)(2,1)S(1)}, u32[]{:S(2)}, u32[]{:S(2)}) collective-permute-start(bf16[64,1024]{1,0:T(8,128)(2,1)S(1)} %get-tuple-element.73), channel_id=1, source_target_pairs={{1,2},{2,1},{3,4},{4,3},{5,6},{6,5},{7,8},{8,7},{9,10},{10,9},{11,... | collective-permute-start | bytes 393224 | tf_op jit(solution)/shard_map/ppermute | solution.py:449
  23.7 1.8 %collective-permute-done.4.chip = bf16[64,1024]{1,0:T(8,128)(2,1)S(1)} collective-permute-done((bf16[64,1024]{1,0:T(8,128)(2,1)S(1)}, bf16[64,1024]{1,0:T(8,128)(2,1)S(1)}, u32[]{:S(2)}, u32[]{:S(2)}) %collective-permute-start.4) | collective-permute-done | bytes 131104 | tf_op jit(solution)/shard_map/ppermute | solution.py:449
  25.5 1.9 %shard_map.100 = (f32[64,1024]{1,0:T(8,128)S(1)}, bf16[64,512]{1,0:T(8,128)(2,1)S(1)}, bf16[64,512]{1,0:T(8,128)(2,1)S(1)}, bf16[64,1024]{1,0:T(8,128)(2,1)S(1)}...) custom-call(f32[64,1024]{1,0:T(8,128)S(1)} %get-tuple-element.72.adj, ...), custom_call_target="tpu_custom_call" | custom-call | flops 679477248 | bytes 3735552 | tf_op jit(solution)/shard_map/pallas_call | solution.py:432
  27.5 3.8 %collective-permute-start.6 = (bf16[64,512]{1,0:T(8,128)(2,1)S(1)}, bf16[64,512]{1,0:T(8,128)(2,1)S(1)}, u32[]{:S(2)}, u32[]{:S(2)}) collective-permute-start(bf16[64,512]{1,0:T(8,128)(2,1)S(1)} %get-tuple-element.85), channel_id=1, source_target_pairs={{1,2},{2,1},{3,4},{4,3},{5,6},{6,5},{7,8},{8,7},{9,10},{10,9},{11,... | collective-permute-start | bytes 196616 | tf_op jit(solution)/shard_map/ppermute | solution.py:449
  34.7 1.6 %collective-permute-done.7.part = bf16[4,296,128]{2,1,0:T(8,128)(2,1)S(1)} collective-permute-done((bf16[4,296,128]{2,1,0:T(8,128)(2,1)S(1)}, bf16[4,296,128]{2,1,0:T(8,128)(2,1)S(1)}, u32[]{:S(2)}, u32[]{:S(2)}) %collective-permute-start.7) | collective-permute-done | bytes 303136 | tf_op jit(solution)/shard_map/ppermute | solution.py:458
  36.3 2.7 %collective-permute-start.8 = (bf16[1,296,128]{2,1,0:T(8,128)(2,1)S(1)}, bf16[1,296,128]{2,1,0:T(8,128)(2,1)S(1)}, u32[]{:S(2)}, u32[]{:S(2)}) collective-permute-start(bf16[1,296,128]{2,1,0:T(8,128)(2,1)S(1)} %get-tuple-element.99), channel_id=1, source_target_pairs={{0,2},{1,3},{2,0},{3,1},{4,6},{5,7},{6,4},{7,5},{8,10},{9,11},{10,... | collective-permute-start | bytes 227336 | tf_op jit(solution)/shard_map/ppermute | solution.py:458
  39.1 7.6 %collective-permute-start.9 = (bf16[1,296,128]{2,1,0:T(8,128)(2,1)S(1)}, bf16[1,296,128]{2,1,0:T(8,128)(2,1)S(1)}, u32[]{:S(2)}, u32[]{:S(2)}) collective-permute-start(bf16[1,296,128]{2,1,0:T(8,128)(2,1)S(1)} %get-tuple-element.100), channel_id=1, source_target_pairs={{0,4},{1,5},{2,6},{3,7},{4,0},{5,1},{6,2},{7,3},{8,12},{9,13},{10,... | collective-permute-start | bytes 227336 | tf_op jit(solution)/shard_map/ppermute | solution.py:458
  47.2 9.4 %collective-permute-start.15 = (bf16[64,1024]{1,0:T(8,128)(2,1)S(1)}, bf16[64,1024]{1,0:T(8,128)(2,1)S(1)}, u32[]{:S(2)}, u32[]{:S(2)}) collective-permute-start(bf16[64,1024]{1,0:T(8,128)(2,1)S(1)} %get-tuple-element.103), channel_id=1, source_target_pairs={{32,64},{96,128},{160,192},{64,32},{128,96},{192,160},{33,65},{97,... | collective-permute-start | bytes 393224 | tf_op jit(solution)/shard_map/ppermute | solution.py:464
  56.7 1.6 %collective-permute-start.13 = (bf16[1,296,128]{2,1,0:T(8,128)(2,1)S(1)}, bf16[1,296,128]{2,1,0:T(8,128)(2,1)S(1)}, u32[]{:S(2)}, u32[]{:S(2)}) collective-permute-start(bf16[1,296,128]{2,1,0:T(8,128)(2,1)S(1)} %shard_map.110.own), channel_id=1, source_target_pairs={{0,24},{1,25},{2,26},{3,27},{4,28},{5,29},{6,30},{7,31},{8,16},{9,... | collective-permute-start | bytes 227336 | tf_op jit(solution)/shard_map/ppermute | solution.py:458
  58.7 1.6 %collective-permute-start.11 = (bf16[1,296,128]{2,1,0:T(8,128)(2,1)S(1)}, bf16[1,296,128]{2,1,0:T(8,128)(2,1)S(1)}, u32[]{:S(2)}, u32[]{:S(2)}) collective-permute-start(bf16[1,296,128]{2,1,0:T(8,128)(2,1)S(1)} %shard_map.110.own), channel_id=1, source_target_pairs={{0,8},{1,9},{2,10},{3,11},{4,12},{5,13},{6,14},{7,15},{8,0},{9,1},... | collective-permute-start | bytes 227336 | tf_op jit(solution)/shard_map/ppermute | solution.py:458
  60.4 2.2 %collective-permute-done.13.part3 = bf16[1,296,128]{2,1,0:T(8,128)(2,1)S(1)} collective-permute-done((bf16[1,296,128]{2,1,0:T(8,128)(2,1)S(1)}, bf16[1,296,128]{2,1,0:T(8,128)(2,1)S(1)}, u32[]{:S(2)}, u32[]{:S(2)}) %collective-permute-start.13) | collective-permute-done | bytes 75808 | tf_op jit(solution)/shard_map/ppermute | solution.py:458
  62.6 5.6 %collective-permute-done.12.part2 = bf16[1,296,128]{2,1,0:T(8,128)(2,1)S(1)} collective-permute-done((bf16[1,296,128]{2,1,0:T(8,128)(2,1)S(1)}, bf16[1,296,128]{2,1,0:T(8,128)(2,1)S(1)}, u32[]{:S(2)}, u32[]{:S(2)}) %collective-permute-start.12) | collective-permute-done | bytes 75808 | tf_op jit(solution)/shard_map/ppermute | solution.py:458
  68.3 1.6 %collective-permute-start.18 = (bf16[1,296,128]{2,1,0:T(8,128)(2,1)S(1)}, bf16[1,296,128]{2,1,0:T(8,128)(2,1)S(1)}, u32[]{:S(2)}, u32[]{:S(2)}) collective-permute-start(bf16[1,296,128]{2,1,0:T(8,128)(2,1)S(1)} %shard_map.111.own), channel_id=1, source_target_pairs={{0,6},{1,7},{2,4},{3,5},{4,2},{5,3},{6,0},{7,1},{8,14},{9,15},{10,... | collective-permute-start | bytes 227336 | tf_op jit(solution)/shard_map/ppermute | solution.py:458
  70.6 1.1 %collective-permute-start.16 = (bf16[1,296,128]{2,1,0:T(8,128)(2,1)S(1)}, bf16[1,296,128]{2,1,0:T(8,128)(2,1)S(1)}, u32[]{:S(2)}, u32[]{:S(2)}) collective-permute-start(bf16[1,296,128]{2,1,0:T(8,128)(2,1)S(1)} %shard_map.111.own), channel_id=1, source_target_pairs={{0,2},{1,3},{2,0},{3,1},{4,6},{5,7},{6,4},{7,5},{8,10},{9,11},{10,... | collective-permute-start | bytes 227336 | tf_op jit(solution)/shard_map/ppermute | solution.py:458
  71.6 1.1 %shard_map.113 = (f32[1,64,4,256]{3,2,1,0:T(4,128)}, f32[1,64,4,256]{3,2,1,0:T(4,128)}) custom-call(f32[1,64,4,256]{3,2,1,0:T(4,128)S(1)} %copy-done.3, f32[1,64,4,256]{3,2,1,0:T(4,128)S(1)} %copy-done.4, bf16[64,1024]{1,0:T(8,128)(2,1)S(1)} %collective-permute-done.14.pair, bf16[64,1024]{1,0:T(8,128)(2,1)S(1)} %collective-permute-done.15.far), custom_call_target="tpu_custom_call" | custom-call | bytes 1310720 | tf_op jit(solution)/shard_map/pallas_call | solution.py:432
  72.8 1.9 %collective-permute-done.17.part2 = bf16[1,296,128]{2,1,0:T(8,128)(2,1)S(1)} collective-permute-done((bf16[1,296,128]{2,1,0:T(8,128)(2,1)S(1)}, bf16[1,296,128]{2,1,0:T(8,128)(2,1)S(1)}, u32[]{:S(2)}, u32[]{:S(2)}) %collective-permute-start.17) | collective-permute-done | bytes 75808 | tf_op jit(solution)/shard_map/ppermute | solution.py:458
  74.7 2.3 %collective-permute-start.19 = (bf16[4,296,128]{2,1,0:T(8,128)(2,1)S(1)}, bf16[4,296,128]{2,1,0:T(8,128)(2,1)S(1)}, u32[]{:S(2)}, u32[]{:S(2)}) collective-permute-start(bf16[4,296,128]{2,1,0:T(8,128)(2,1)S(1)} %shard_map.112.own), channel_id=1, source_target_pairs={{0,1},{1,0},{2,3},{3,2},{4,5},{5,4},{6,7},{7,6},{8,9},{9,8},{10,11... | collective-permute-start | bytes 909320 | tf_op jit(solution)/shard_map/ppermute | solution.py:458
  77.0 1.0 %exit_own.1 = (f32[4,64,576]{2,1,0:T(8,128)}, f32[4,64,576]{2,1,0:T(8,128)}) custom-call(bf16[4,296,128]{2,1,0:T(8,128)(2,1)S(1)} %shard_map.112.own), custom_call_target="tpu_custom_call" | custom-call | bytes 589824 | tf_op jit(solution)/shard_map/exit_own/pallas_call | solution.py:409
  78.2 1.0 %exit_other.1 = (f32[4,64,576]{2,1,0:T(8,128)}, f32[4,64,576]{2,1,0:T(8,128)}, f32[4,64]{1,0:T(4,128)}) custom-call(bf16[4,296,128]{2,1,0:T(8,128)(2,1)S(1)} %collective-permute-done.19.part, bf16[4,296,128]{2,1,0:T(8,128)(2,1)S(1)} %shard_map.112.own, f32[4,64,576]{2,1,0:T(8,128)} %get-tuple-element.112._one, ...), custom_call_target="tpu_custom_call", output_to_operand_aliasing={{0}: (2, {}), {1}: (3, {})} | custom-call | bytes 589824 | tf_op jit(solution)/shard_map/exit_other/pallas_call | solution.py:418
  (52 shorter events, 10.4 us)
Async XLA Ops:
  1.9 1.7 %collective-permute-start = (bf16[64,1024]{1,0:T(8,128)(2,1)S(1)}, bf16[64,1024]{1,0:T(8,128)(2,1)S(1)}, u32[]{:S(2)}, u32[]{:S(2)}) collective-permute-start(bf16[64,1024]{1,0:T(8,128)(2,1)S(1)} %get-tuple-element.62.own), channel_id=1, source_target_pairs={{0,1},{1,0},{2,3},{3,2},{4,5},{5,4},{6,7},{7,6},{8,9},{9,8},{10,11... | collective-permute-start | bytes 393224 | tf_op jit(solution)/shard_map/ppermute | solution.py:444
  3.7 3.6 %copy-start = (bf16[4,64,576]{2,1,0:T(8,128)(2,1)S(1)}, bf16[4,64,576]{2,1,0:T(8,128)(2,1)}, u32[]{:S(2)}) copy-start(bf16[4,64,576]{2,1,0:T(8,128)(2,1)} %w1.3) | copy-start | bytes 884740
  3.7 3.7 %copy-start.1 = (bf16[4,64,576]{2,1,0:T(8,128)(2,1)S(1)}, bf16[4,64,576]{2,1,0:T(8,128)(2,1)}, u32[]{:S(2)}) copy-start(bf16[4,64,576]{2,1,0:T(8,128)(2,1)} %w2.3) | copy-start | bytes 884740
  3.7 4.1 %copy-start.5 = (f32[4,64]{1,0:T(4,128)S(1)}, f32[4,64]{1,0:T(4,128)}, u32[]{:S(2)}) copy-start(f32[4,64]{1,0:T(4,128)} %bias.1) | copy-start | bytes 3076
  3.7 8.5 %collective-permute-start.1 = (bf16[64,2560]{1,0:T(8,128)(2,1)S(1)}, bf16[64,2560]{1,0:T(8,128)(2,1)S(1)}, u32[]{:S(2)}, u32[]{:S(2)}) collective-permute-start(bf16[64,2560]{1,0:T(8,128)(2,1)S(1)} %shard_map.94), channel_id=1, source_target_pairs={{1,2},{2,1},{3,4},{4,3},{5,6},{6,5},{7,8},{8,7},{9,10},{10,9},{11,... | collective-permute-start | bytes 983048 | tf_op jit(solution)/shard_map/ppermute | solution.py:449
  12.3 1.5 %collective-permute-start.2 = (bf16[64,1536]{1,0:T(8,128)(2,1)S(1)}, bf16[64,1536]{1,0:T(8,128)(2,1)S(1)}, u32[]{:S(2)}, u32[]{:S(2)}) collective-permute-start(bf16[64,1536]{1,0:T(8,128)(2,1)S(1)} %shard_map.97), channel_id=1, source_target_pairs={{0,1},{1,0},{2,3},{3,2},{4,5},{5,4},{6,7},{7,6},{8,9},{9,8},{10,11... | collective-permute-start | bytes 589832 | tf_op jit(solution)/shard_map/ppermute | solution.py:444
  19.2 6.3 %collective-permute-start.4 = (bf16[64,1024]{1,0:T(8,128)(2,1)S(1)}, bf16[64,1024]{1,0:T(8,128)(2,1)S(1)}, u32[]{:S(2)}, u32[]{:S(2)}) collective-permute-start(bf16[64,1024]{1,0:T(8,128)(2,1)S(1)} %get-tuple-element.73), channel_id=1, source_target_pairs={{1,2},{2,1},{3,4},{4,3},{5,6},{6,5},{7,8},{8,7},{9,10},{10,9},{11,... | collective-permute-start | bytes 393224 | tf_op jit(solution)/shard_map/ppermute | solution.py:449
  22.7 2.8 %collective-permute-start.3 = (bf16[64,1024]{1,0:T(8,128)(2,1)S(1)}, bf16[64,1024]{1,0:T(8,128)(2,1)S(1)}, u32[]{:S(2)}, u32[]{:S(2)}) collective-permute-start(bf16[64,1024]{1,0:T(8,128)(2,1)S(1)} %get-tuple-element.73), channel_id=1, source_target_pairs={{0,1},{1,0},{2,3},{3,2},{4,5},{5,4},{6,7},{7,6},{8,9},{9,8},{10,11... | collective-permute-start | bytes 393224 | tf_op jit(solution)/shard_map/ppermute | solution.py:444
  27.4 5.3 %collective-permute-start.5 = (bf16[64,512]{1,0:T(8,128)(2,1)S(1)}, bf16[64,512]{1,0:T(8,128)(2,1)S(1)}, u32[]{:S(2)}, u32[]{:S(2)}) collective-permute-start(bf16[64,512]{1,0:T(8,128)(2,1)S(1)} %get-tuple-element.84), channel_id=1, source_target_pairs={{0,1},{1,0},{2,3},{3,2},{4,5},{5,4},{6,7},{7,6},{8,9},{9,8},{10,11... | collective-permute-start | bytes 196616 | tf_op jit(solution)/shard_map/ppermute | solution.py:444
  27.5 5.6 %collective-permute-start.6 = (bf16[64,512]{1,0:T(8,128)(2,1)S(1)}, bf16[64,512]{1,0:T(8,128)(2,1)S(1)}, u32[]{:S(2)}, u32[]{:S(2)}) collective-permute-start(bf16[64,512]{1,0:T(8,128)(2,1)S(1)} %get-tuple-element.85), channel_id=1, source_target_pairs={{1,2},{2,1},{3,4},{4,3},{5,6},{6,5},{7,8},{8,7},{9,10},{10,9},{11,... | collective-permute-start | bytes 196616 | tf_op jit(solution)/shard_map/ppermute | solution.py:449
  34.6 1.7 %collective-permute-start.7 = (bf16[4,296,128]{2,1,0:T(8,128)(2,1)S(1)}, bf16[4,296,128]{2,1,0:T(8,128)(2,1)S(1)}, u32[]{:S(2)}, u32[]{:S(2)}) collective-permute-start(bf16[4,296,128]{2,1,0:T(8,128)(2,1)S(1)} %get-tuple-element.97), channel_id=1, source_target_pairs={{0,1},{1,0},{2,3},{3,2},{4,5},{5,4},{6,7},{7,6},{8,9},{9,8},{10,11... | collective-permute-start | bytes 909320 | tf_op jit(solution)/shard_map/ppermute | solution.py:458
  36.3 20.3 %collective-permute-start.8 = (bf16[1,296,128]{2,1,0:T(8,128)(2,1)S(1)}, bf16[1,296,128]{2,1,0:T(8,128)(2,1)S(1)}, u32[]{:S(2)}, u32[]{:S(2)}) collective-permute-start(bf16[1,296,128]{2,1,0:T(8,128)(2,1)S(1)} %get-tuple-element.99), channel_id=1, source_target_pairs={{0,2},{1,3},{2,0},{3,1},{4,6},{5,7},{6,4},{7,5},{8,10},{9,11},{10,... | collective-permute-start | bytes 227336 | tf_op jit(solution)/shard_map/ppermute | solution.py:458
  39.1 17.6 %collective-permute-start.9 = (bf16[1,296,128]{2,1,0:T(8,128)(2,1)S(1)}, bf16[1,296,128]{2,1,0:T(8,128)(2,1)S(1)}, u32[]{:S(2)}, u32[]{:S(2)}) collective-permute-start(bf16[1,296,128]{2,1,0:T(8,128)(2,1)S(1)} %get-tuple-element.100), channel_id=1, source_target_pairs={{0,4},{1,5},{2,6},{3,7},{4,0},{5,1},{6,2},{7,3},{8,12},{9,13},{10,... | collective-permute-start | bytes 227336 | tf_op jit(solution)/shard_map/ppermute | solution.py:458
  46.7 10.0 %collective-permute-start.10 = (bf16[1,296,128]{2,1,0:T(8,128)(2,1)S(1)}, bf16[1,296,128]{2,1,0:T(8,128)(2,1)S(1)}, u32[]{:S(2)}, u32[]{:S(2)}) collective-permute-start(bf16[1,296,128]{2,1,0:T(8,128)(2,1)S(1)} %get-tuple-element.101), channel_id=1, source_target_pairs={{0,6},{1,7},{2,4},{3,5},{4,2},{5,3},{6,0},{7,1},{8,14},{9,15},{10,... | collective-permute-start | bytes 227336 | tf_op jit(solution)/shard_map/ppermute | solution.py:458
  46.7 21.6 %collective-permute-start.14 = (bf16[64,1024]{1,0:T(8,128)(2,1)S(1)}, bf16[64,1024]{1,0:T(8,128)(2,1)S(1)}, u32[]{:S(2)}, u32[]{:S(2)}) collective-permute-start(bf16[64,1024]{1,0:T(8,128)(2,1)S(1)} %get-tuple-element.102), channel_id=1, source_target_pairs={{0,32},{64,96},{128,160},{192,224},{32,0},{96,64},{160,128},{224,1... | collective-permute-start | bytes 393224 | tf_op jit(solution)/shard_map/ppermute | solution.py:464
  47.2 21.0 %collective-permute-start.15 = (bf16[64,1024]{1,0:T(8,128)(2,1)S(1)}, bf16[64,1024]{1,0:T(8,128)(2,1)S(1)}, u32[]{:S(2)}, u32[]{:S(2)}) collective-permute-start(bf16[64,1024]{1,0:T(8,128)(2,1)S(1)} %get-tuple-element.103), channel_id=1, source_target_pairs={{32,64},{96,128},{160,192},{64,32},{128,96},{192,160},{33,65},{97,... | collective-permute-start | bytes 393224 | tf_op jit(solution)/shard_map/ppermute | solution.py:464
  56.7 14.9 %copy-start.3 = (f32[1,64,4,256]{3,2,1,0:T(4,128)S(1)}, f32[1,64,4,256]{3,2,1,0:T(4,128)}, u32[]{:S(2)}) copy-start(f32[1,64,4,256]{3,2,1,0:T(4,128)} %c.1) | copy-start | bytes 786436
  56.7 5.9 %collective-permute-start.13 = (bf16[1,296,128]{2,1,0:T(8,128)(2,1)S(1)}, bf16[1,296,128]{2,1,0:T(8,128)(2,1)S(1)}, u32[]{:S(2)}, u32[]{:S(2)}) collective-permute-start(bf16[1,296,128]{2,1,0:T(8,128)(2,1)S(1)} %shard_map.110.own), channel_id=1, source_target_pairs={{0,24},{1,25},{2,26},{3,27},{4,28},{5,29},{6,30},{7,31},{8,16},{9,... | collective-permute-start | bytes 227336 | tf_op jit(solution)/shard_map/ppermute | solution.py:458
  58.4 9.8 %collective-permute-start.12 = (bf16[1,296,128]{2,1,0:T(8,128)(2,1)S(1)}, bf16[1,296,128]{2,1,0:T(8,128)(2,1)S(1)}, u32[]{:S(2)}, u32[]{:S(2)}) collective-permute-start(bf16[1,296,128]{2,1,0:T(8,128)(2,1)S(1)} %shard_map.110.own), channel_id=1, source_target_pairs={{0,16},{1,17},{2,18},{3,19},{4,20},{5,21},{6,22},{7,23},{8,24},{9,... | collective-permute-start | bytes 227336 | tf_op jit(solution)/shard_map/ppermute | solution.py:458
  58.7 9.5 %collective-permute-start.11 = (bf16[1,296,128]{2,1,0:T(8,128)(2,1)S(1)}, bf16[1,296,128]{2,1,0:T(8,128)(2,1)S(1)}, u32[]{:S(2)}, u32[]{:S(2)}) collective-permute-start(bf16[1,296,128]{2,1,0:T(8,128)(2,1)S(1)} %shard_map.110.own), channel_id=1, source_target_pairs={{0,8},{1,9},{2,10},{3,11},{4,12},{5,13},{6,14},{7,15},{8,0},{9,1},... | collective-permute-start | bytes 227336 | tf_op jit(solution)/shard_map/ppermute | solution.py:458
  68.3 4.5 %collective-permute-start.18 = (bf16[1,296,128]{2,1,0:T(8,128)(2,1)S(1)}, bf16[1,296,128]{2,1,0:T(8,128)(2,1)S(1)}, u32[]{:S(2)}, u32[]{:S(2)}) collective-permute-start(bf16[1,296,128]{2,1,0:T(8,128)(2,1)S(1)} %shard_map.111.own), channel_id=1, source_target_pairs={{0,6},{1,7},{2,4},{3,5},{4,2},{5,3},{6,0},{7,1},{8,14},{9,15},{10,... | collective-permute-start | bytes 227336 | tf_op jit(solution)/shard_map/ppermute | solution.py:458
  69.8 4.8 %collective-permute-start.17 = (bf16[1,296,128]{2,1,0:T(8,128)(2,1)S(1)}, bf16[1,296,128]{2,1,0:T(8,128)(2,1)S(1)}, u32[]{:S(2)}, u32[]{:S(2)}) collective-permute-start(bf16[1,296,128]{2,1,0:T(8,128)(2,1)S(1)} %shard_map.111.own), channel_id=1, source_target_pairs={{0,4},{1,5},{2,6},{3,7},{4,0},{5,1},{6,2},{7,3},{8,12},{9,13},{10,... | collective-permute-start | bytes 227336 | tf_op jit(solution)/shard_map/ppermute | solution.py:458
  70.6 4.1 %collective-permute-start.16 = (bf16[1,296,128]{2,1,0:T(8,128)(2,1)S(1)}, bf16[1,296,128]{2,1,0:T(8,128)(2,1)S(1)}, u32[]{:S(2)}, u32[]{:S(2)}) collective-permute-start(bf16[1,296,128]{2,1,0:T(8,128)(2,1)S(1)} %shard_map.111.own), channel_id=1, source_target_pairs={{0,2},{1,3},{2,0},{3,1},{4,6},{5,7},{6,4},{7,5},{8,10},{9,11},{10,... | collective-permute-start | bytes 227336 | tf_op jit(solution)/shard_map/ppermute | solution.py:458
  74.7 3.5 %collective-permute-start.19 = (bf16[4,296,128]{2,1,0:T(8,128)(2,1)S(1)}, bf16[4,296,128]{2,1,0:T(8,128)(2,1)S(1)}, u32[]{:S(2)}, u32[]{:S(2)}) collective-permute-start(bf16[4,296,128]{2,1,0:T(8,128)(2,1)S(1)} %shard_map.112.own), channel_id=1, source_target_pairs={{0,1},{1,0},{2,3},{3,2},{4,5},{5,4},{6,7},{7,6},{8,9},{9,8},{10,11... | collective-permute-start | bytes 909320 | tf_op jit(solution)/shard_map/ppermute | solution.py:458
  (2 other events, 2.1 us)
